TPU v7x, 32 devices: a whole 2x2x4 slice. The times are simulated.
32 devices in a mesh: tmpl: 2 (over core), row: 16 (over z, y, x).
Axes of the slice: x: 2, y: 2, z: 4, core: 2. Of those that a mesh axis runs over, the one named last changes fastest.
Arguments:
- pair_maps: bfloat16 [2, 2048, 2048, 64], P('tmpl', 'row'), may hold values from -6 to 6
- crop_tiles: int32 [2, 8], P('tmpl'), may hold values from 0 to 15, as said below
- full_length: int32 [1], replicated, may hold values from 1536 to 2048
- proj_weight: bfloat16 [2, 64, 320], replicated, may hold values from -0.75 to 0.75
- out_weight: bfloat16 [2, 64, 64], replicated, may hold values from -0.75 to 0.75
- final_weight: bfloat16 [64, 128], replicated, may hold values from -0.75 to 0.75
Outputs:
- embedding: bfloat16 [128, 1024, 1024], P(None, 'row')
Inputs may be any that keep to these rules, and one draw needn't show every extreme that they name: Each row of crop_tiles names 8 different tiles of the 16, in increasing order; its last 4 entries are the tiles 16 - 8 // 2 to 15.
All inputs are finite; a program needn't handle non-finite values.
Results may differ from a plain program's by a relative error of at most 0.014.
Values may be sent and summed in bfloat16 or wider, within the bound.
A program may use at most 256 MiB of HBM per device.

v0:
```python
import jax
import jax.numpy as jnp
from jax import lax
from jax.experimental import pallas as pl
from jax.experimental.pallas import tpu as pltpu
from jax.sharding import PartitionSpec as P

CH = 64
CROP = 1024
TILE = 128
NLAYER = 2
FULL = 2048


EPSILON = 1e-05


def from_partner(value, axis, bit):
    mask = 2**bit
    pairs = [(source, source ^ mask) for source in range(lax.axis_size(axis))]
    return lax.ppermute(value, axis, pairs)


def channel_norm(values):
    center = values - jnp.mean(values, axis=0, keepdims=True)
    spread = jnp.mean(center * center, axis=0, keepdims=True)
    return center * lax.rsqrt(spread + EPSILON)


SPLIT = 2


def product_kernel(left_ref, *refs):
    rights, out_ref = refs[:-1], refs[-1]
    sources, _, width, chunk = left_ref.shape
    left = left_ref[...].reshape(sources * width, chunk)
    per = out_ref.shape[0] // len(rights)
    for number, right_ref in enumerate(rights):
        right = right_ref[...].reshape(sources * width, right_ref.shape[-1])
        product = lax.dot_general(
            right, left, (((0,), (0,)), ((), ())), preferred_element_type=jnp.float32
        )
        out_ref[number * per : (number + 1) * per] = product.astype(out_ref.dtype).reshape(
            per, 1, width, chunk
        )


def channel_products(left, rights):
    sources, channels, width, chunk = left.shape
    spec = pl.BlockSpec((sources, 1, width, chunk), lambda c: (0, c, 0, 0))
    depth = sources * width
    return pl.pallas_call(
        product_kernel,
        grid=(channels,),
        in_specs=[spec] * (1 + len(rights)),
        out_specs=spec,
        out_shape=jax.ShapeDtypeStruct(left.shape, left.dtype),
        compiler_params=pltpu.CompilerParams(vmem_limit_bytes=32 << 20),
        cost_estimate=pl.CostEstimate(
            flops=2 * channels * depth * depth * chunk,
            bytes_accessed=2 * left.size * (2 + len(rights)),
            transcendentals=0,
        ),
    )(left, *rights)


def exchange(value):
    return lax.all_to_all(value, "row", split_axis=0, concat_axis=0, tiled=True)


def in_chunks(pair_maps, crop_tiles, full_length, proj_weight, out_weight, final_weight):
    row_count = lax.axis_size("row")
    my_index = lax.axis_index("row")
    crop_ids = crop_tiles[0]
    col_width = CROP // row_count
    per_group = CH // row_count
    tiles = CROP // TILE
    chunk = CROP // SPLIT
    steps_crop = jnp.arange(CROP, dtype=jnp.int32)
    position = crop_ids[steps_crop // TILE] * TILE + steps_crop % TILE
    usable = (position < full_length[0]).astype(jnp.float32)
    col_usable = lax.dynamic_slice_in_dim(usable, my_index * col_width, col_width)
    pair_mask = col_usable[:, None] * usable[None, :]
    masks = jnp.split(pair_mask, SPLIT, axis=1)
    by_channel = jnp.transpose(pair_maps[0], (0, 2, 1))
    columns = jnp.concatenate(
        [
            lax.dynamic_slice_in_dim(by_channel, crop_ids[tile] * TILE, TILE, axis=2)
            for tile in range(tiles)
        ],
        axis=2,
    )
    send = jnp.transpose(columns, (2, 1, 0)).reshape(row_count, col_width, CH, TILE)
    got = exchange(send)
    per = tiles // SPLIT
    current = []
    for number in range(SPLIT):
        pieces = [
            lax.dynamic_index_in_dim(got, crop_ids[number * per + tile], 0, keepdims=False)
            for tile in range(per)
        ]
        current.append(jnp.transpose(jnp.concatenate(pieces, axis=2), (1, 0, 2)))
    for layer_idx in range(NLAYER):
        lefts, rights, gates = [], [], []
        for values, mask in zip(current, masks):
            normed_in = channel_norm(values.astype(jnp.float32)).astype(jnp.bfloat16)
            projected = jnp.einsum(
                "cd,cwi->dwi", proj_weight[layer_idx], normed_in, preferred_element_type=jnp.float32
            )
            left = jax.nn.sigmoid(projected[:CH]) * projected[CH : 2 * CH] * mask
            right = jax.nn.sigmoid(projected[2 * CH : 3 * CH]) * projected[3 * CH : 4 * CH] * mask
            shape = (row_count, per_group, col_width, chunk)
            rights.append(exchange(right.astype(jnp.bfloat16).reshape(shape)))
            lefts.append(exchange(left.astype(jnp.bfloat16).reshape(shape)))
            gates.append(jax.nn.sigmoid(projected[4 * CH :]))
        following = []
        for values, left, gate in zip(current, lefts, gates):
            merged = exchange(channel_products(left, rights)).reshape(CH, col_width, chunk)
            normed_out = channel_norm(merged.astype(jnp.float32)).astype(jnp.bfloat16)
            update = jnp.einsum(
                "cd,cwi->dwi", out_weight[layer_idx], normed_out, preferred_element_type=jnp.float32
            )
            following.append((values.astype(jnp.float32) + gate * update).astype(jnp.bfloat16))
        current = following
    template_count = lax.axis_size("tmpl")
    results = []
    for values in current:
        normed_final = channel_norm(values.astype(jnp.float32))
        summed = lax.psum(normed_final.astype(jnp.bfloat16), "tmpl").astype(jnp.float32)
        hidden = jnp.maximum(summed / template_count, 0.0).astype(jnp.bfloat16)
        results.append(
            jnp.einsum("cz,cwi->zwi", final_weight, hidden, preferred_element_type=jnp.float32)
            .astype(jnp.bfloat16)
        )
    return jnp.concatenate(results, axis=2)


def on_device(pair_maps, crop_tiles, full_length, proj_weight, out_weight, final_weight):
    row_count = lax.axis_size("row")
    my_index = lax.axis_index("row")
    pair_local = pair_maps[0]
    crop_ids = crop_tiles[0]
    local_rows = pair_local.shape[0]
    col_width = CROP // row_count
    parts_count = max(1, row_count // CH)
    per_group = CH * parts_count // row_count
    groups = CH // per_group
    part_rows = CROP // parts_count
    steps_crop = jnp.arange(CROP, dtype=jnp.int32)
    position = crop_ids[steps_crop // TILE] * TILE + steps_crop % TILE
    usable = (position < full_length[0]).astype(jnp.float32)
    col_usable = lax.dynamic_slice_in_dim(usable, my_index * col_width, col_width)
    pair_mask = col_usable[:, None] * usable[None, :]
    columns = pair_local.reshape(local_rows, FULL // TILE, TILE, CH)[:, crop_ids]
    columns = columns.reshape(local_rows, CROP * CH)
    received = lax.all_to_all(columns, "row", split_axis=1, concat_axis=0, tiled=True)
    cropped = received.reshape(FULL // TILE, TILE, col_width * CH)[crop_ids]
    current = jnp.transpose(cropped.reshape(CROP, col_width, CH), (2, 1, 0))
    for layer_idx in range(NLAYER):
        normed_in = channel_norm(current.astype(jnp.float32)).astype(jnp.bfloat16)
        projected = jnp.einsum(
            "cd,cwi->dwi", proj_weight[layer_idx], normed_in, preferred_element_type=jnp.float32
        )
        left_proj = (jax.nn.sigmoid(projected[:CH]) * projected[CH : 2 * CH] * pair_mask).astype(
            jnp.bfloat16
        )
        right_proj = (
            jax.nn.sigmoid(projected[2 * CH : 3 * CH]) * projected[3 * CH : 4 * CH] * pair_mask
        ).astype(jnp.bfloat16)
        gate_vals = jax.nn.sigmoid(projected[4 * CH :])
        left_send = left_proj.reshape(groups, per_group, col_width, parts_count, part_rows)
        left_send = jnp.transpose(left_send, (0, 3, 1, 2, 4)).reshape(
            row_count, per_group, col_width, part_rows
        )
        right_send = right_proj.reshape(groups, per_group, col_width, parts_count, part_rows)
        right_send = jnp.transpose(right_send, (0, 3, 1, 2, 4)).reshape(
            row_count, per_group, col_width, part_rows
        )
        left_got, right_got = (
            lax.all_to_all(left_send, "row", split_axis=0, concat_axis=2, tiled=True),
            lax.all_to_all(right_send, "row", split_axis=0, concat_axis=2, tiled=True),
        )
        right_whole = right_got[0]
        for bit_pos in range(parts_count.bit_length() - 1):
            partner = from_partner(right_whole, "row", bit_pos)
            lower_side = my_index // (1 << bit_pos) % 2 == 0
            right_whole = jnp.where(
                lower_side,
                jnp.concatenate([right_whole, partner], axis=2),
                jnp.concatenate([partner, right_whole], axis=2),
            )
        products = jnp.einsum(
            "cki,ckj->cij", left_got[0], right_whole, preferred_element_type=jnp.float32
        ).astype(jnp.bfloat16)
        back_send = jnp.transpose(
            products.reshape(per_group, part_rows, row_count, col_width), (2, 0, 3, 1)
        )
        back_got = lax.all_to_all(back_send, "row", split_axis=0, concat_axis=0, tiled=True)
        merged = back_got.reshape(groups, parts_count, per_group, col_width, part_rows)
        merged = jnp.transpose(merged, (0, 2, 3, 1, 4)).reshape(CH, col_width, CROP)
        normed_out = channel_norm(merged.astype(jnp.float32)).astype(jnp.bfloat16)
        update = jnp.einsum(
            "cd,cwi->dwi", out_weight[layer_idx], normed_out, preferred_element_type=jnp.float32
        )
        current = (current.astype(jnp.float32) + gate_vals * update).astype(jnp.bfloat16)
    normed_final = channel_norm(current.astype(jnp.float32))
    template_count = lax.axis_size("tmpl")
    summed = lax.psum(normed_final.astype(jnp.bfloat16), "tmpl").astype(jnp.float32)
    hidden = jnp.maximum(summed / template_count, 0.0).astype(jnp.bfloat16)
    result = jnp.einsum(
        "cz,cwi->zwi", final_weight, hidden, preferred_element_type=jnp.float32
    ).astype(jnp.bfloat16)
    return result


def solution(mesh):
    placed = (P("tmpl", "row", None, None), P("tmpl", None), P(), P(), P(), P())
    rows = mesh.shape["row"]
    whole_tiles = FULL // rows == TILE and CH % rows == 0
    return jax.shard_map(
        in_chunks if whole_tiles else on_device,
        mesh=mesh,
        in_specs=placed,
        out_specs=P(None, "row", None),
        check_vma=False,
    )
```

profile of v0, /device:TPU:0, one launch (start us, length us, event | category | flops | bytes accessed | tf_op | source)
XLA Modules:
  0.0 1788.0 jit_solution(6446459816706652474)
XLA Ops:
  37.5 26.0 %copy.45 = bf16[1024,64,128]{2,1,0:T(8,128)(2,1)} copy(bf16[1024,64,128]{0,1,2:T(8,128)(2,1)} %bitcast.24) | data formatting | bytes 33554432 | tf_op jit(solution)/shard_map/transpose | solution.py:93
  63.5 8.6 all-to-all-start
  92.4 294.9 %all-to-all-done = bf16[16,64,64,128]{3,2,1,0:T(8,128)(2,1)} async-done(((bf16[16,64,64,128]{3,2,1,0:T(8,128)(2,1)}), bf16[16,64,64,128]{3,2,1,0:T(8,128)(2,1)}, u32[]{:S(2)}, u32[]{:S(2)}) %all-to-all-start) | async-done | bytes 16777248 | tf_op jit(solution)/shard_map/all_to_all | solution.py:68
  399.4 17.4 convolution_bitcast_fusion.2
  416.8 15.8 fusion.73
  436.9 73.4 %all-to-all-start.3 = ((bf16[16,4,64,512]{3,2,1,0:T(8,128)(2,1)}), bf16[16,4,64,512]{3,2,1,0:T(8,128)(2,1)}, u32[]{:S(2)}, u32[]{:S(2)}) async-start(bf16[16,4,64,512]{3,2,1,0:T(8,128)(2,1)} %bitcast.171), calls=%async_computation.3 | async-start | bytes 8388608 | tf_op jit(solution)/shard_map/all_to_all | solution.py:68
  513.4 17.6 convolution_bitcast_fusion.3
  531.0 15.5 fusion.83
  551.0 37.7 %all-to-all-done.3.refs_1_ = bf16[16,4,64,512]{3,2,1,0:T(8,128)(2,1)} async-done(((bf16[16,4,64,512]{3,2,1,0:T(8,128)(2,1)}), bf16[16,4,64,512]{3,2,1,0:T(8,128)(2,1)}, u32[]{:S(2)}, u32[]{:S(2)}) %all-to-all-start.3) | async-done | bytes 4194336 | tf_op jit(solution)/shard_map/all_to_all | solution.py:68
  588.7 19.3 %all-to-all-start.1 = ((bf16[16,4,64,512]{3,2,1,0:T(8,128)(2,1)}), bf16[16,4,64,512]{3,2,1,0:T(8,128)(2,1)}, u32[]{:S(2)}, u32[]{:S(2)}) async-start(bf16[16,4,64,512]{3,2,1,0:T(8,128)(2,1)} %bitcast.172), calls=%async_computation.1 | async-start | bytes 8388608 | tf_op jit(solution)/shard_map/all_to_all | solution.py:68
  614.5 71.9 %all-to-all-done.1.left_ref = bf16[16,4,64,512]{3,2,1,0:T(8,128)(2,1)} async-done(((bf16[16,4,64,512]{3,2,1,0:T(8,128)(2,1)}), bf16[16,4,64,512]{3,2,1,0:T(8,128)(2,1)}, u32[]{:S(2)}, u32[]{:S(2)}) %all-to-all-start.1) | async-done | bytes 4194336 | tf_op jit(solution)/shard_map/all_to_all | solution.py:68
  686.5 19.4 %all-to-all-start.2 = ((bf16[16,4,64,512]{3,2,1,0:T(8,128)(2,1)}), bf16[16,4,64,512]{3,2,1,0:T(8,128)(2,1)}, u32[]{:S(2)}, u32[]{:S(2)}) async-start(bf16[16,4,64,512]{3,2,1,0:T(8,128)(2,1)} %bitcast.173), calls=%async_computation.2 | async-start | bytes 8388608 | tf_op jit(solution)/shard_map/all_to_all | solution.py:68
  705.9 6.6 copy.53
  712.5 71.9 %all-to-all-done.2.refs_0_ = bf16[16,4,64,512]{3,2,1,0:T(8,128)(2,1)} async-done(((bf16[16,4,64,512]{3,2,1,0:T(8,128)(2,1)}), bf16[16,4,64,512]{3,2,1,0:T(8,128)(2,1)}, u32[]{:S(2)}, u32[]{:S(2)}) %all-to-all-start.2) | async-done | bytes 4194336 | tf_op jit(solution)/shard_map/all_to_all | solution.py:68
  784.4 19.5 %all-to-all-start.7 = ((bf16[16,4,64,512]{3,2,1,0:T(8,128)(2,1)}), bf16[16,4,64,512]{3,2,1,0:T(8,128)(2,1)}, u32[]{:S(2)}, u32[]{:S(2)}) async-start(bf16[16,4,64,512]{3,2,1,0:T(8,128)(2,1)} %bitcast.175), calls=%async_computation.7 | async-start | bytes 8388608 | tf_op jit(solution)/shard_map/all_to_all | solution.py:68
  803.9 7.9 shard_map.64
  813.8 68.6 %all-to-all-done.7.left_ref = bf16[16,4,64,512]{3,2,1,0:T(8,128)(2,1)} async-done(((bf16[16,4,64,512]{3,2,1,0:T(8,128)(2,1)}), bf16[16,4,64,512]{3,2,1,0:T(8,128)(2,1)}, u32[]{:S(2)}, u32[]{:S(2)}) %all-to-all-start.7) | async-done | bytes 4194336 | tf_op jit(solution)/shard_map/all_to_all | solution.py:68
  882.3 19.5 %all-to-all-start.4 = ((bf16[16,4,64,512]{3,2,1,0:T(8,128)(2,1)}), bf16[16,4,64,512]{3,2,1,0:T(8,128)(2,1)}, u32[]{:S(2)}, u32[]{:S(2)}) async-start(bf16[16,4,64,512]{3,2,1,0:T(8,128)(2,1)} %copy-done.3), calls=%async_computation.4 | async-start | bytes 8388608 | tf_op jit(solution)/shard_map/all_to_all | solution.py:68
  901.8 7.9 shard_map.65
  911.8 68.5 %all-to-all-done.4 = bf16[16,4,64,512]{3,2,1,0:T(8,128)(2,1)} async-done(((bf16[16,4,64,512]{3,2,1,0:T(8,128)(2,1)}), bf16[16,4,64,512]{3,2,1,0:T(8,128)(2,1)}, u32[]{:S(2)}, u32[]{:S(2)}) %all-to-all-start.4) | async-done | bytes 4194336 | tf_op jit(solution)/shard_map/all_to_all | solution.py:68
  980.3 19.7 %all-to-all-start.8 = ((bf16[16,4,64,512]{3,2,1,0:T(8,128)(2,1)}), bf16[16,4,64,512]{3,2,1,0:T(8,128)(2,1)}, u32[]{:S(2)}, u32[]{:S(2)}) async-start(bf16[16,4,64,512]{3,2,1,0:T(8,128)(2,1)} %copy-done.1), calls=%async_computation.8 | async-start | bytes 8388608 | tf_op jit(solution)/shard_map/all_to_all | solution.py:68
  1009.7 9.8 convert_reduce_fusion.1
  1021.2 16.3 convolution_bitcast_fusion.1
  1037.6 17.4 fusion.64
  1061.4 16.9 all-to-all-done.8
  1078.4 19.4 %all-to-all-start.5 = ((bf16[16,4,64,512]{3,2,1,0:T(8,128)(2,1)}), bf16[16,4,64,512]{3,2,1,0:T(8,128)(2,1)}, u32[]{:S(2)}, u32[]{:S(2)}) async-start(bf16[16,4,64,512]{3,2,1,0:T(8,128)(2,1)} %bitcast.170), calls=%async_computation.5 | async-start | bytes 8388608 | tf_op jit(solution)/shard_map/all_to_all | solution.py:68
  1116.1 60.1 %all-to-all-done.5.left_ref = bf16[16,4,64,512]{3,2,1,0:T(8,128)(2,1)} async-done(((bf16[16,4,64,512]{3,2,1,0:T(8,128)(2,1)}), bf16[16,4,64,512]{3,2,1,0:T(8,128)(2,1)}, u32[]{:S(2)}, u32[]{:S(2)}) %all-to-all-start.5) | async-done | bytes 4194336 | tf_op jit(solution)/shard_map/all_to_all | solution.py:68
  1176.3 19.9 %all-to-all-start.6 = ((bf16[16,4,64,512]{3,2,1,0:T(8,128)(2,1)}), bf16[16,4,64,512]{3,2,1,0:T(8,128)(2,1)}, u32[]{:S(2)}, u32[]{:S(2)}) async-start(bf16[16,4,64,512]{3,2,1,0:T(8,128)(2,1)} %bitcast.169), calls=%async_computation.6 | async-start | bytes 8388608 | tf_op jit(solution)/shard_map/all_to_all | solution.py:68
  1196.2 10.8 convert_reduce_fusion
  1208.9 16.4 convolution_bitcast_fusion
  1225.2 17.3 fusion.44
  1249.0 25.6 %all-to-all-done.6.refs_0_ = bf16[16,4,64,512]{3,2,1,0:T(8,128)(2,1)} async-done(((bf16[16,4,64,512]{3,2,1,0:T(8,128)(2,1)}), bf16[16,4,64,512]{3,2,1,0:T(8,128)(2,1)}, u32[]{:S(2)}, u32[]{:S(2)}) %all-to-all-start.6) | async-done | bytes 4194336 | tf_op jit(solution)/shard_map/all_to_all | solution.py:68
  1274.6 19.4 %all-to-all-start.9 = ((bf16[16,4,64,512]{3,2,1,0:T(8,128)(2,1)}), bf16[16,4,64,512]{3,2,1,0:T(8,128)(2,1)}, u32[]{:S(2)}, u32[]{:S(2)}) async-start(bf16[16,4,64,512]{3,2,1,0:T(8,128)(2,1)} %bitcast.174), calls=%async_computation.9 | async-start | bytes 8388608 | tf_op jit(solution)/shard_map/all_to_all | solution.py:68
  1294.1 6.5 copy.58
  1300.6 71.9 %all-to-all-done.9.refs_1_ = bf16[16,4,64,512]{3,2,1,0:T(8,128)(2,1)} async-done(((bf16[16,4,64,512]{3,2,1,0:T(8,128)(2,1)}), bf16[16,4,64,512]{3,2,1,0:T(8,128)(2,1)}, u32[]{:S(2)}, u32[]{:S(2)}) %all-to-all-start.9) | async-done | bytes 4194336 | tf_op jit(solution)/shard_map/all_to_all | solution.py:68
  1372.5 19.5 %all-to-all-start.11 = ((bf16[16,4,64,512]{3,2,1,0:T(8,128)(2,1)}), bf16[16,4,64,512]{3,2,1,0:T(8,128)(2,1)}, u32[]{:S(2)}, u32[]{:S(2)}) async-start(bf16[16,4,64,512]{3,2,1,0:T(8,128)(2,1)} %bitcast.176), calls=%async_computation.11 | async-start | bytes 8388608 | tf_op jit(solution)/shard_map/all_to_all | solution.py:68
  1392.0 7.9 shard_map.66
  1401.9 68.6 %all-to-all-done.11.left_ref = bf16[16,4,64,512]{3,2,1,0:T(8,128)(2,1)} async-done(((bf16[16,4,64,512]{3,2,1,0:T(8,128)(2,1)}), bf16[16,4,64,512]{3,2,1,0:T(8,128)(2,1)}, u32[]{:S(2)}, u32[]{:S(2)}) %all-to-all-start.11) | async-done | bytes 4194336 | tf_op jit(solution)/shard_map/all_to_all | solution.py:68
  1470.5 19.5 %all-to-all-start.10 = ((bf16[16,4,64,512]{3,2,1,0:T(8,128)(2,1)}), bf16[16,4,64,512]{3,2,1,0:T(8,128)(2,1)}, u32[]{:S(2)}, u32[]{:S(2)}) async-start(bf16[16,4,64,512]{3,2,1,0:T(8,128)(2,1)} %copy-done.4), calls=%async_computation.10 | async-start | bytes 8388608 | tf_op jit(solution)/shard_map/all_to_all | solution.py:68
  1490.0 7.9 shard_map.67
  1499.9 68.5 %all-to-all-done.10 = bf16[16,4,64,512]{3,2,1,0:T(8,128)(2,1)} async-done(((bf16[16,4,64,512]{3,2,1,0:T(8,128)(2,1)}), bf16[16,4,64,512]{3,2,1,0:T(8,128)(2,1)}, u32[]{:S(2)}, u32[]{:S(2)}) %all-to-all-start.10) | async-done | bytes 4194336 | tf_op jit(solution)/shard_map/all_to_all | solution.py:68
  1568.4 19.5 %all-to-all-start.12 = ((bf16[16,4,64,512]{3,2,1,0:T(8,128)(2,1)}), bf16[16,4,64,512]{3,2,1,0:T(8,128)(2,1)}, u32[]{:S(2)}, u32[]{:S(2)}) async-start(bf16[16,4,64,512]{3,2,1,0:T(8,128)(2,1)} %copy-done.2), calls=%async_computation.12 | async-start | bytes 8388608 | tf_op jit(solution)/shard_map/all_to_all | solution.py:68
  1597.7 9.7 convert_reduce_fusion.4
  1613.3 53.1 %all-to-all-done.12 = bf16[16,4,64,512]{3,2,1,0:T(8,128)(2,1)} async-done(((bf16[16,4,64,512]{3,2,1,0:T(8,128)(2,1)}), bf16[16,4,64,512]{3,2,1,0:T(8,128)(2,1)}, u32[]{:S(2)}, u32[]{:S(2)}) %all-to-all-start.12) | async-done | bytes 4194336 | tf_op jit(solution)/shard_map/all_to_all | solution.py:68
  1676.0 9.8 convert_reduce_fusion.2
  1691.8 51.8 %all-reduce.3.cloned.1.call-done = (bf16[64,64,512]{2,0,1:T(8,128)(2,1)}, bf16[64,64,512]{2,0,1:T(8,128)(2,1)}) async-done(((bf16[64,64,512]{2,0,1:T(8,128)(2,1)}, bf16[64,64,512]{2,0,1:T(8,128)(2,1)}), (bf16[64,64,512]{2,0,1:T(8,128)(2,1)}, bf16[64,64,512]{2,0,1:T(8,128)(2,1)})) %all-reduce.3.cloned.1.call-update) | async-done | bytes 8388624 | tf_op jit(solution)/shard_map/psum | solution.py:129
  1751.1 6.5 pad_maximum_fusion
  1757.6 23.3 %copy.60 = bf16[128,64,1024]{2,1,0:T(8,128)(2,1)} copy(bf16[128,64,1024]{0,2,1:T(8,128)(2,1)} %pad_maximum_fusion) | data formatting | bytes 33554432 | tf_op jit(solution)/shard_map/concatenate | solution.py:135
  (119 shorter events, 153.0 us)
Async XLA Ops:
  6.5 1737.1 %copy-start = (bf16[64,128]{1,0:T(8,128)(2,1)S(1)}, bf16[64,128]{1,0:T(8,128)(2,1)}, u32[]{:S(2)}) copy-start(bf16[64,128]{1,0:T(8,128)(2,1)} %param.11) | copy-start | bytes 49156
  63.5 323.8 %all-to-all-start = ((bf16[16,64,64,128]{3,2,1,0:T(8,128)(2,1)}), bf16[16,64,64,128]{3,2,1,0:T(8,128)(2,1)}, u32[]{:S(2)}, u32[]{:S(2)}) async-start(bf16[16,64,64,128]{3,2,1,0:T(8,128)(2,1)} %bitcast.168), calls=%async_computation | async-start | bytes 33554432 | tf_op jit(solution)/shard_map/all_to_all | solution.py:68
  92.4 324.4 %copy-start.20 = (f32[64,512]{1,0:T(8,128)}, f32[64,512]{1,0:T(8,128)S(1)}, u32[]{:S(2)}) copy-start(f32[64,512]{1,0:T(8,128)S(1)} %get-tuple-element.24) | copy-start | bytes 393220
  392.7 1.0 copy-start.15
  392.7 4.8 copy-start.17
  392.7 24.0 %copy-start.9 = (bf16[64,64,128]{2,1,0:T(8,128)(2,1)}, bf16[64,64,128]{2,1,0:T(8,128)(2,1)S(1)}, u32[]{:S(2)}) copy-start(bf16[64,64,128]{2,1,0:T(8,128)(2,1)S(1)} %get-tuple-element.16) | copy-start | bytes 3145732
  392.7 24.0 %copy-start.11 = (bf16[64,64,128]{2,1,0:T(8,128)(2,1)}, bf16[64,64,128]{2,1,0:T(8,128)(2,1)S(1)}, u32[]{:S(2)}) copy-start(bf16[64,64,128]{2,1,0:T(8,128)(2,1)S(1)} %get-tuple-element.17) | copy-start | bytes 3145732
  392.8 24.0 %copy-start.13 = (bf16[64,64,128]{2,1,0:T(8,128)(2,1)}, bf16[64,64,128]{2,1,0:T(8,128)(2,1)S(1)}, u32[]{:S(2)}) copy-start(bf16[64,64,128]{2,1,0:T(8,128)(2,1)S(1)} %get-tuple-element.18) | copy-start | bytes 3145732
  392.8 24.0 %copy-start.14 = (bf16[64,64,128]{2,1,0:T(8,128)(2,1)}, bf16[64,64,128]{2,1,0:T(8,128)(2,1)S(1)}, u32[]{:S(2)}) copy-start(bf16[64,64,128]{2,1,0:T(8,128)(2,1)S(1)} %get-tuple-element.19) | copy-start | bytes 3145732
  432.5 77.7 %copy-start.23 = (f32[64,512]{1,0:T(8,128)S(1)}, f32[64,512]{1,0:T(8,128)}, u32[]{:S(2)}) copy-start(f32[64,512]{1,0:T(8,128)} %get-tuple-element.42) | copy-start | bytes 393220
  436.9 76.5 %copy-start.24 = (bf16[2,64,320]{2,1,0:T(8,128)(2,1)S(1)}, bf16[2,64,320]{2,1,0:T(8,128)(2,1)}, u32[]{:S(2)}) copy-start(bf16[2,64,320]{2,1,0:T(8,128)(2,1)} %param.9) | copy-start | bytes 245764
  436.9 151.8 %all-to-all-start.3 = ((bf16[16,4,64,512]{3,2,1,0:T(8,128)(2,1)}), bf16[16,4,64,512]{3,2,1,0:T(8,128)(2,1)}, u32[]{:S(2)}, u32[]{:S(2)}) async-start(bf16[16,4,64,512]{3,2,1,0:T(8,128)(2,1)} %bitcast.171), calls=%async_computation.3 | async-start | bytes 8388608 | tf_op jit(solution)/shard_map/all_to_all | solution.py:68
  513.4 17.6 copy-start.22
  588.7 97.8 %all-to-all-start.1 = ((bf16[16,4,64,512]{3,2,1,0:T(8,128)(2,1)}), bf16[16,4,64,512]{3,2,1,0:T(8,128)(2,1)}, u32[]{:S(2)}, u32[]{:S(2)}) async-start(bf16[16,4,64,512]{3,2,1,0:T(8,128)(2,1)} %bitcast.172), calls=%async_computation.1 | async-start | bytes 8388608 | tf_op jit(solution)/shard_map/all_to_all | solution.py:68
  686.5 97.9 %all-to-all-start.2 = ((bf16[16,4,64,512]{3,2,1,0:T(8,128)(2,1)}), bf16[16,4,64,512]{3,2,1,0:T(8,128)(2,1)}, u32[]{:S(2)}, u32[]{:S(2)}) async-start(bf16[16,4,64,512]{3,2,1,0:T(8,128)(2,1)} %bitcast.173), calls=%async_computation.2 | async-start | bytes 8388608 | tf_op jit(solution)/shard_map/all_to_all | solution.py:68
  784.4 98.0 %all-to-all-start.7 = ((bf16[16,4,64,512]{3,2,1,0:T(8,128)(2,1)}), bf16[16,4,64,512]{3,2,1,0:T(8,128)(2,1)}, u32[]{:S(2)}, u32[]{:S(2)}) async-start(bf16[16,4,64,512]{3,2,1,0:T(8,128)(2,1)} %bitcast.175), calls=%async_computation.7 | async-start | bytes 8388608 | tf_op jit(solution)/shard_map/all_to_all | solution.py:68
  811.8 1.9 copy-start.3
  882.3 97.9 %all-to-all-start.4 = ((bf16[16,4,64,512]{3,2,1,0:T(8,128)(2,1)}), bf16[16,4,64,512]{3,2,1,0:T(8,128)(2,1)}, u32[]{:S(2)}, u32[]{:S(2)}) async-start(bf16[16,4,64,512]{3,2,1,0:T(8,128)(2,1)} %copy-done.3), calls=%async_computation.4 | async-start | bytes 8388608 | tf_op jit(solution)/shard_map/all_to_all | solution.py:68
  909.8 2.0 copy-start.1
  980.3 98.1 %all-to-all-start.8 = ((bf16[16,4,64,512]{3,2,1,0:T(8,128)(2,1)}), bf16[16,4,64,512]{3,2,1,0:T(8,128)(2,1)}, u32[]{:S(2)}, u32[]{:S(2)}) async-start(bf16[16,4,64,512]{3,2,1,0:T(8,128)(2,1)} %copy-done.1), calls=%async_computation.8 | async-start | bytes 8388608 | tf_op jit(solution)/shard_map/all_to_all | solution.py:68
  1000.0 9.7 copy-start.16
  1000.0 9.7 copy-start.18
  1000.0 9.7 copy-start.25
  1019.5 18.1 %copy-start.5 = (bf16[64,64,512]{2,0,1:T(8,128)(2,1)}, bf16[64,64,512]{2,0,1:T(8,128)(2,1)S(1)}, u32[]{:S(2)}) copy-start(bf16[64,64,512]{2,0,1:T(8,128)(2,1)S(1)} %get-tuple-element.36) | copy-start | bytes 12582916
  1078.4 97.9 %all-to-all-start.5 = ((bf16[16,4,64,512]{3,2,1,0:T(8,128)(2,1)}), bf16[16,4,64,512]{3,2,1,0:T(8,128)(2,1)}, u32[]{:S(2)}, u32[]{:S(2)}) async-start(bf16[16,4,64,512]{3,2,1,0:T(8,128)(2,1)} %bitcast.170), calls=%async_computation.5 | async-start | bytes 8388608 | tf_op jit(solution)/shard_map/all_to_all | solution.py:68
  1110.5 85.7 %copy-start.10 = (bf16[64,64,128]{2,1,0:T(8,128)(2,1)S(1)}, bf16[64,64,128]{2,1,0:T(8,128)(2,1)}, u32[]{:S(2)}) copy-start(bf16[64,64,128]{2,1,0:T(8,128)(2,1)} %copy-done.9) | copy-start | bytes 3145732
  1110.5 85.7 %copy-start.12 = (bf16[64,64,128]{2,1,0:T(8,128)(2,1)S(1)}, bf16[64,64,128]{2,1,0:T(8,128)(2,1)}, u32[]{:S(2)}) copy-start(bf16[64,64,128]{2,1,0:T(8,128)(2,1)} %copy-done.11) | copy-start | bytes 3145732
  1176.3 98.3 %all-to-all-start.6 = ((bf16[16,4,64,512]{3,2,1,0:T(8,128)(2,1)}), bf16[16,4,64,512]{3,2,1,0:T(8,128)(2,1)}, u32[]{:S(2)}, u32[]{:S(2)}) async-start(bf16[16,4,64,512]{3,2,1,0:T(8,128)(2,1)} %bitcast.169), calls=%async_computation.6 | async-start | bytes 8388608 | tf_op jit(solution)/shard_map/all_to_all | solution.py:68
  1207.1 18.2 %copy-start.7 = (bf16[64,64,512]{2,0,1:T(8,128)(2,1)}, bf16[64,64,512]{2,0,1:T(8,128)(2,1)S(1)}, u32[]{:S(2)}) copy-start(bf16[64,64,512]{2,0,1:T(8,128)(2,1)S(1)} %get-tuple-element.34) | copy-start | bytes 12582916
  1208.8 16.4 copy-start.21
  1274.6 97.9 %all-to-all-start.9 = ((bf16[16,4,64,512]{3,2,1,0:T(8,128)(2,1)}), bf16[16,4,64,512]{3,2,1,0:T(8,128)(2,1)}, u32[]{:S(2)}, u32[]{:S(2)}) async-start(bf16[16,4,64,512]{3,2,1,0:T(8,128)(2,1)} %bitcast.174), calls=%async_computation.9 | async-start | bytes 8388608 | tf_op jit(solution)/shard_map/all_to_all | solution.py:68
  1372.5 98.0 %all-to-all-start.11 = ((bf16[16,4,64,512]{3,2,1,0:T(8,128)(2,1)}), bf16[16,4,64,512]{3,2,1,0:T(8,128)(2,1)}, u32[]{:S(2)}, u32[]{:S(2)}) async-start(bf16[16,4,64,512]{3,2,1,0:T(8,128)(2,1)} %bitcast.176), calls=%async_computation.11 | async-start | bytes 8388608 | tf_op jit(solution)/shard_map/all_to_all | solution.py:68
  1400.0 1.9 copy-start.4
  1470.5 97.9 %all-to-all-start.10 = ((bf16[16,4,64,512]{3,2,1,0:T(8,128)(2,1)}), bf16[16,4,64,512]{3,2,1,0:T(8,128)(2,1)}, u32[]{:S(2)}, u32[]{:S(2)}) async-start(bf16[16,4,64,512]{3,2,1,0:T(8,128)(2,1)} %copy-done.4), calls=%async_computation.10 | async-start | bytes 8388608 | tf_op jit(solution)/shard_map/all_to_all | solution.py:68
  1497.9 2.0 copy-start.2
  1568.4 97.9 %all-to-all-start.12 = ((bf16[16,4,64,512]{3,2,1,0:T(8,128)(2,1)}), bf16[16,4,64,512]{3,2,1,0:T(8,128)(2,1)}, u32[]{:S(2)}, u32[]{:S(2)}) async-start(bf16[16,4,64,512]{3,2,1,0:T(8,128)(2,1)} %copy-done.2), calls=%async_computation.12 | async-start | bytes 8388608 | tf_op jit(solution)/shard_map/all_to_all | solution.py:68
  1587.9 155.7 %all-reduce.3.cloned.1.call-start = ((), (), s32[]{:S(2)}) async-start(), calls=%async_computation.13 | async-start | bytes 16777216 | tf_op jit(solution)/shard_map/psum | solution.py:129
  1588.0 9.7 copy-start.6
  1666.4 9.7 copy-start.8
  1743.6 4.8 copy-start.19
Sparse Core Ops, SparseCore 0:
  1692.0 51.5 all-reduce.2
where the time goes:
time: 1790 us
  waiting for transfers between devices  1030 us (58%)
  starting transfers between devices  297 us (17%)
  other arithmetic  142 us (8%)
  local copies, waits for them, and re-layouts  138 us (8%)
  matrix products  115 us (6%)
  between operations  33.9 us (2%)
  Pallas kernels  31.7 us (2%)
    all_to_all x13, waiting for transfers between devices, exchange(): return lax.all_to_all(value, 'row', split_axis=0, concat_axis=0, tiled=True)  978 us
    all_to_all x13, starting transfers between devices, exchange(): return lax.all_to_all(value, 'row', split_axis=0, concat_axis=0, tiled=True)  297 us
    dot_general x4, matrix products, in_chunks(): jnp.einsum('cd,cwi->dwi', proj_weight[layer_idx], normed_in, preferred_el...  67.7 us
    psum x1, waiting for transfers between devices, in_chunks(): lax.psum(normed_final.astype(jnp.bfloat16), 'tmpl').astype(jnp.float32)  51.8 us
    dot_general x4, matrix products, in_chunks(): jnp.einsum('cd,cwi->dwi', out_weight[layer_idx], normed_out, preferred_el...  40.2 us
  transfers between devices with their start and end apart: 14, of which 14 were waited for; matrix products, arithmetic and copies ran while one was open for 12% of the time, Pallas kernels for 2%

commit v1 on v0

--- a/solution.py
+++ b/solution.py
@@ -3,7 +3,7 @@
 from jax import lax
 from jax.experimental import pallas as pl
 from jax.experimental.pallas import tpu as pltpu
-from jax.sharding import PartitionSpec as P
+from jax.sharding import Mesh, PartitionSpec as P
 
 CH = 64
 CROP = 1024
@@ -64,18 +64,126 @@
     )(left, *rights)
 
 
+def spread_kernel(send_ref, got_ref, hold, send_sem, recv_sem, hold_sem):
+    core, half, inner = (lax.axis_index(name) for name in ("core", "half", "inner"))
+    cores, halves, width = (lax.axis_size(name) for name in ("core", "half", "inner"))
+    blocks = cores * width
+    row = half * width + inner
+    mine = core * width + inner
+    barrier = pltpu.get_barrier_semaphore()
+    total = cores * halves * width
+    flat = (core * halves + half) * width + inner
+    for step in range(1, total):
+        other = lax.rem(flat + step, total)
+        pl.semaphore_signal(
+            barrier,
+            inc=1,
+            device_id={
+                "core": other // (halves * width),
+                "half": lax.rem(other // width, halves),
+                "inner": lax.rem(other, width),
+            },
+            device_id_type=pl.DeviceIdType.MESH,
+        )
+    pl.semaphore_wait(barrier, total - 1)
+
+    def outgoing(step):
+        block = lax.rem(mine + step, blocks)
+        return pltpu.make_async_remote_copy(
+            src_ref=send_ref.at[block],
+            dst_ref=got_ref.at[row],
+            send_sem=send_sem.at[step],
+            recv_sem=recv_sem.at[row],
+            device_id={"core": block // width, "half": core, "inner": lax.rem(block, width)},
+            device_id_type=pl.DeviceIdType.MESH,
+        )
+
+    home = half == core
+    for step in range(1, blocks):
+        outgoing(step).start()
+
+    @pl.when(home)
+    def _():
+        bring = pltpu.make_async_copy(send_ref.at[mine], hold, hold_sem.at[0])
+        bring.start()
+        bring.wait()
+        put = pltpu.make_async_copy(hold, got_ref.at[row], hold_sem.at[1])
+        put.start()
+        put.wait()
+
+    @pl.when(jnp.logical_not(home))
+    def _():
+        outgoing(0).start()
+
+    def incoming(slot):
+        return pltpu.make_async_remote_copy(
+            src_ref=send_ref.at[0],
+            dst_ref=got_ref.at[slot],
+            send_sem=send_sem.at[0],
+            recv_sem=recv_sem.at[slot],
+            device_id={"core": core, "half": half, "inner": inner},
+            device_id_type=pl.DeviceIdType.MESH,
+        )
+
+    for step in range(1, blocks):
+        outgoing(step).wait_send()
+
+    @pl.when(jnp.logical_not(home))
+    def _():
+        outgoing(0).wait_send()
+
+    for step in range(1, blocks):
+        incoming(lax.rem(row + step, blocks)).wait_recv()
+
+    @pl.when(jnp.logical_not(home))
+    def _():
+        incoming(row).wait_recv()
+
+
+def spread(send):
+    blocks = send.shape[0]
+    return pl.pallas_call(
+        spread_kernel,
+        in_specs=[pl.BlockSpec(memory_space=pl.ANY)],
+        out_specs=pl.BlockSpec(memory_space=pl.ANY),
+        out_shape=jax.ShapeDtypeStruct(send.shape, send.dtype),
+        scratch_shapes=[
+            pltpu.VMEM(send.shape[1:], send.dtype),
+            pltpu.SemaphoreType.DMA((blocks,)),
+            pltpu.SemaphoreType.DMA((blocks,)),
+            pltpu.SemaphoreType.DMA((2,)),
+        ],
+        compiler_params=pltpu.CompilerParams(
+            collective_id=0, has_side_effects=True, vmem_limit_bytes=32 << 20
+        ),
+    )(send)
+
+
+GROUP = ("core", "inner")
+
+
 def exchange(value):
-    return lax.all_to_all(value, "row", split_axis=0, concat_axis=0, tiled=True)
-
-
-def in_chunks(pair_maps, crop_tiles, full_length, proj_weight, out_weight, final_weight):
-    row_count = lax.axis_size("row")
-    my_index = lax.axis_index("row")
-    crop_ids = crop_tiles[0]
+    return lax.all_to_all(value, GROUP, split_axis=0, concat_axis=0, tiled=True)
+
+
+def moved(value, pairs):
+    halves = lax.axis_size("half")
+    steps = [(a * halves + b, c * halves + d) for (a, b), (c, d) in pairs]
+    return lax.ppermute(value, ("core", "half"), steps)
+
+
+def in_halves(pair_maps, crop_tiles, full_length, proj_weight, out_weight, final_weight):
+    cores, halves, inner_count = (lax.axis_size(name) for name in ("core", "half", "inner"))
+    core, half, inner = (lax.axis_index(name) for name in ("core", "half", "inner"))
+    row_count = cores * inner_count
+    my_index = core * inner_count + inner
     col_width = CROP // row_count
     per_group = CH // row_count
     tiles = CROP // TILE
     chunk = CROP // SPLIT
+    held_ids = crop_tiles[0]
+    other_ids = lax.ppermute(held_ids, "core", [(0, 1), (1, 0)])
+    crop_ids = jnp.where(core == half, held_ids, other_ids)
     steps_crop = jnp.arange(CROP, dtype=jnp.int32)
     position = crop_ids[steps_crop // TILE] * TILE + steps_crop % TILE
     usable = (position < full_length[0]).astype(jnp.float32)
@@ -85,13 +193,13 @@
     by_channel = jnp.transpose(pair_maps[0], (0, 2, 1))
     columns = jnp.concatenate(
         [
-            lax.dynamic_slice_in_dim(by_channel, crop_ids[tile] * TILE, TILE, axis=2)
+            lax.dynamic_slice_in_dim(by_channel, held_ids[tile] * TILE, TILE, axis=2)
             for tile in range(tiles)
         ],
         axis=2,
     )
     send = jnp.transpose(columns, (2, 1, 0)).reshape(row_count, col_width, CH, TILE)
-    got = exchange(send)
+    got = spread(send)
     per = tiles // SPLIT
     current = []
     for number in range(SPLIT):
@@ -122,12 +230,14 @@
             )
             following.append((values.astype(jnp.float32) + gate * update).astype(jnp.bfloat16))
         current = following
-    template_count = lax.axis_size("tmpl")
     results = []
     for values in current:
-        normed_final = channel_norm(values.astype(jnp.float32))
-        summed = lax.psum(normed_final.astype(jnp.bfloat16), "tmpl").astype(jnp.float32)
-        hidden = jnp.maximum(summed / template_count, 0.0).astype(jnp.bfloat16)
+        normed_final = channel_norm(values.astype(jnp.float32)).astype(jnp.bfloat16)
+        across = moved(normed_final, [((0, 1), (0, 0)), ((1, 0), (1, 1))])
+        summed = normed_final.astype(jnp.float32) + across.astype(jnp.float32)
+        hidden = jnp.maximum(summed / halves, 0.0).astype(jnp.bfloat16)
+        shared = moved(hidden, [((0, 0), (1, 0)), ((1, 1), (0, 1))])
+        hidden = jnp.where(core == half, hidden, shared)
         results.append(
             jnp.einsum("cz,cwi->zwi", final_weight, hidden, preferred_element_type=jnp.float32)
             .astype(jnp.bfloat16)
@@ -214,13 +324,19 @@
 
 
 def solution(mesh):
+    rows, templates = mesh.shape["row"], mesh.shape["tmpl"]
+    whole_tiles = FULL // rows == TILE and CH % rows == 0
+    if whole_tiles and templates == 2:
+        grid = Mesh(
+            mesh.devices.reshape(templates, templates, rows // templates),
+            ("core", "half", "inner"),
+        )
+        lines = ("half", "inner")
+        placed = (P("core", lines, None, None), P("core", None), P(), P(), P(), P())
+        return jax.shard_map(
+            in_halves, mesh=grid, in_specs=placed, out_specs=P(None, lines, None), check_vma=False
+        )
     placed = (P("tmpl", "row", None, None), P("tmpl", None), P(), P(), P(), P())
-    rows = mesh.shape["row"]
-    whole_tiles = FULL // rows == TILE and CH % rows == 0
     return jax.shard_map(
-        in_chunks if whole_tiles else on_device,
-        mesh=mesh,
-        in_specs=placed,
-        out_specs=P(None, "row", None),
-        check_vma=False,
+        on_device, mesh=mesh, in_specs=placed, out_specs=P(None, "row", None), check_vma=False
     )

time: 1790 us -> 1550 us (0.87)
  waiting for transfers between devices: 1030 us -> 538 us
  Pallas kernels: 31.7 us -> 412 us
  starting transfers between devices: 297 us -> 157 us
    all_to_all x13 -> x12, waiting for transfers between devices: 978 us -> 362 us  [exchange(): return lax.all_to_all(value, GROUP, split_axis=0, concat_axis=0, tiled=True)]
    pallas_call x0 -> x1, Pallas kernels: none -> 380 us  [spread(): pl.pallas_call(spread_kernel, in_specs=[pl.BlockSpec(memory_space=pl.ANY)...]
    ppermute x0 -> x5, waiting for transfers between devices: none -> 176 us  [the longest x4 176 us: moved(): return lax.ppermute(value, ('core', 'half'), steps)]
    all_to_all x13 -> x12, starting transfers between devices: 297 us -> 147 us  [exchange(): return lax.all_to_all(value, GROUP, split_axis=0, concat_axis=0, tiled=True)]
    psum x1 -> x0, waiting for transfers between devices: 51.8 us -> none  [in_chunks(): lax.psum(normed_final.astype(jnp.bfloat16), 'tmpl').astype(jnp.float32)]
    unnamed x59 -> x65, local copies, waits for them, and re-layouts: 30.4 us -> 36.6 us
    convert_element_type x11 -> x13, other arithmetic: 90.2 us -> 91.8 us  [the longest x2 33.1 us: in_halves(): lefts.append(exchange(left.astype(jnp.bfloat16).reshape(shape)))]
  transfers between devices with their start and end apart: 14 -> 17, of which waited for: 14 -> 13; matrix products, arithmetic and copies ran while one was open for 12% -> 18% of each run, Pallas kernels for 2% -> 27%
where the time goes in v1:
time: 1550 us; the launch traced here: 1530 us
  waiting for transfers between devices  538 us (35%)
  Pallas kernels  412 us (27%)
  starting transfers between devices  157 us (10%)
  local copies, waits for them, and re-layouts  145 us (9%)
  other arithmetic  144 us (9%)
  matrix products  116 us (7%)
  between operations  21.7 us (1%)
    pallas_call x1, Pallas kernels, spread(): pl.pallas_call(spread_kernel, in_specs=[pl.BlockSpec(memory_space=pl.ANY)...  380 us
    all_to_all x12, waiting for transfers between devices, exchange(): return lax.all_to_all(value, GROUP, split_axis=0, concat_axis=0, tiled=True)  362 us
    ppermute x4, waiting for transfers between devices, moved(): return lax.ppermute(value, ('core', 'half'), steps)  176 us
    all_to_all x12, starting transfers between devices, exchange(): return lax.all_to_all(value, GROUP, split_axis=0, concat_axis=0, tiled=True)  147 us
    dot_general x4, matrix products, in_halves(): jnp.einsum('cd,cwi->dwi', proj_weight[layer_idx], normed_in, preferred_el...  67.7 us
    dot_general x4, matrix products, in_halves(): jnp.einsum('cd,cwi->dwi', out_weight[layer_idx], normed_out, preferred_el...  41.2 us
    unnamed x65, local copies, waits for them, and re-layouts  36.6 us
    convert_element_type x2, other arithmetic, in_halves(): lefts.append(exchange(left.astype(jnp.bfloat16).reshape(shape)))  33.1 us
  transfers between devices with their start and end apart: 17, of which 13 were waited for; matrix products, arithmetic and copies ran while one was open for 18% of the time, Pallas kernels for 27%

profile of v1, /device:TPU:0, one launch (start us, length us, event | category | flops | bytes accessed | tf_op | source)
XLA Modules:
  0.0 1533.3 jit_solution(16879412620610253779)
XLA Ops:
  32.5 26.0 %copy.22 = bf16[1024,64,128]{2,1,0:T(8,128)(2,1)} copy(bf16[1024,64,128]{0,1,2:T(8,128)(2,1)} %bitcast.24) | data formatting | bytes 33554432 | tf_op jit(solution)/shard_map/transpose | solution.py:201
  58.4 379.9 %shard_map.64 = bf16[16,64,64,128]{3,2,1,0:T(8,128)(2,1)S(1)} custom-call(bf16[16,64,64,128]{3,2,1,0:T(8,128)(2,1)} %bitcast.178), custom_call_target="tpu_custom_call" | custom-call | tf_op jit(solution)/shard_map/pallas_call | solution.py:145
  478.4 17.4 %convolution_bitcast_fusion.2 = f32[320,64,512]{2,0,1:T(8,128)} fusion(f32[64,512]{1,0:T(8,128)S(1)} %add_rsqrt_fusion.8, f32[64,512]{1,0:T(8,128)S(1)} %broadcast_multiply_fusion.9, bf16[2,64,320]{2,1,0:T(8,128)(2,1)} %param.9, bf16[64,64,128]{2,1,0:T(8,128)(2,1)S(1)} %get-tuple-element.14, bf16[64,64,128]{2,1,0:T(8,128)(2,1)S(1)} %get-tuple-element.15, ...), kind=kOutput, calls=%fused_computation.2 | convolution fusion | flops 1365245952 | bytes 46448640 | tf_op jit(solution)/shard_map/cd,cwi->dwi/dot_general | solution.py:215
  495.8 15.6 %fusion.73 = (bf16[64,64,512]{2,0,1:T(8,128)(2,1)S(1)}, bf16[64,64,512]{2,0,1:T(8,128)(2,1)}) fusion(f32[320,64,512]{2,0,1:T(8,128)} %convolution_bitcast_fusion.2, f32[64,512]{1,0:T(8,128)S(1)} %get-tuple-element.22), kind=kLoop, calls=%fused_computation.110 | loop fusion | flops 25165824 | bytes 42074112 | tf_op jit(solution)/shard_map/convert_element_type | solution.py:221
  515.7 39.1 %all-to-all-start.2 = ((bf16[16,4,64,512]{3,2,1,0:T(8,128)(2,1)}), bf16[16,4,64,512]{3,2,1,0:T(8,128)(2,1)}, u32[]{:S(2)}, u32[]{:S(2)}) async-start(bf16[16,4,64,512]{3,2,1,0:T(8,128)(2,1)} %bitcast.181), calls=%async_computation.2 | async-start | bytes 8388608 | tf_op jit(solution)/shard_map/all_to_all | solution.py:166
  558.0 17.6 %convolution_bitcast_fusion.3 = f32[320,64,512]{2,0,1:T(8,128)} fusion(f32[64,512]{1,0:T(8,128)S(1)} %add_rsqrt_fusion.9, f32[64,512]{1,0:T(8,128)S(1)} %broadcast_multiply_fusion.10, bf16[2,64,320]{2,1,0:T(8,128)(2,1)S(1)} %copy-done.26, bf16[64,64,128]{2,1,0:T(8,128)(2,1)S(1)} %get-tuple-element.18, bf16[64,64,128]{2,1,0:T(8,128)(2,1)} %copy-done.17, ...), kind=kOutput, calls=%fused_computation.3 | convolution fusion | flops 1365245952 | bytes 46448640 | tf_op jit(solution)/shard_map/cd,cwi->dwi/dot_general | solution.py:215
  575.6 15.6 %fusion.83 = (bf16[64,64,512]{2,0,1:T(8,128)(2,1)S(1)}, bf16[64,64,512]{2,0,1:T(8,128)(2,1)}) fusion(f32[320,64,512]{2,0,1:T(8,128)} %convolution_bitcast_fusion.3, f32[64,512]{1,0:T(8,128)S(1)} %copy-done.24), kind=kLoop, calls=%fused_computation.124 | loop fusion | flops 25165824 | bytes 42074112 | tf_op jit(solution)/shard_map/convert_element_type | solution.py:222
  595.6 9.4 all-to-all-done.2.refs_1_
  604.9 10.3 all-to-all-start
  615.3 6.5 copy.24
  621.8 43.6 %all-to-all-done.left_ref = bf16[16,4,64,512]{3,2,1,0:T(8,128)(2,1)} async-done(((bf16[16,4,64,512]{3,2,1,0:T(8,128)(2,1)}), bf16[16,4,64,512]{3,2,1,0:T(8,128)(2,1)}, u32[]{:S(2)}, u32[]{:S(2)}) %all-to-all-start) | async-done | bytes 4194336 | tf_op jit(solution)/shard_map/all_to_all | solution.py:166
  665.4 10.6 all-to-all-start.1
  676.0 6.6 copy.30
  682.6 43.6 %all-to-all-done.1.refs_0_ = bf16[16,4,64,512]{3,2,1,0:T(8,128)(2,1)} async-done(((bf16[16,4,64,512]{3,2,1,0:T(8,128)(2,1)}), bf16[16,4,64,512]{3,2,1,0:T(8,128)(2,1)}, u32[]{:S(2)}, u32[]{:S(2)}) %all-to-all-start.1) | async-done | bytes 4194336 | tf_op jit(solution)/shard_map/all_to_all | solution.py:166
  726.2 10.4 all-to-all-start.6
  736.6 7.9 shard_map.65
  746.5 40.2 %all-to-all-done.6.left_ref = bf16[16,4,64,512]{3,2,1,0:T(8,128)(2,1)} async-done(((bf16[16,4,64,512]{3,2,1,0:T(8,128)(2,1)}), bf16[16,4,64,512]{3,2,1,0:T(8,128)(2,1)}, u32[]{:S(2)}, u32[]{:S(2)}) %all-to-all-start.6) | async-done | bytes 4194336 | tf_op jit(solution)/shard_map/all_to_all | solution.py:166
  786.7 10.5 all-to-all-start.3
  797.2 7.9 shard_map.66
  807.1 40.1 %all-to-all-done.3 = bf16[16,4,64,512]{3,2,1,0:T(8,128)(2,1)} async-done(((bf16[16,4,64,512]{3,2,1,0:T(8,128)(2,1)}), bf16[16,4,64,512]{3,2,1,0:T(8,128)(2,1)}, u32[]{:S(2)}, u32[]{:S(2)}) %all-to-all-start.3) | async-done | bytes 4194336 | tf_op jit(solution)/shard_map/all_to_all | solution.py:166
  847.2 10.5 all-to-all-start.7
  867.4 9.8 convert_reduce_fusion.1
  879.0 16.3 %convolution_bitcast_fusion.1 = f32[320,64,512]{2,0,1:T(8,128)} fusion(bf16[64,64,512]{2,0,1:T(8,128)(2,1)S(1)} %get-tuple-element.42, f32[64,512]{1,0:T(8,128)S(1)} %add_rsqrt_fusion.6, f32[64,512]{1,0:T(8,128)S(1)} %broadcast_multiply_fusion.7, bf16[2,64,320]{2,1,0:T(8,128)(2,1)S(1)} %copy-done.26), kind=kOutput, calls=%fused_computation.1 | convolution fusion | flops 1350565888 | bytes 46448640 | tf_op jit(solution)/shard_map/cd,cwi->dwi/dot_general | solution.py:215
  895.3 17.6 %fusion.64 = (bf16[64,64,512]{2,0,1:T(8,128)(2,1)}, bf16[64,64,512]{2,0,1:T(8,128)(2,1)}) fusion(f32[320,64,512]{2,0,1:T(8,128)} %convolution_bitcast_fusion.1, f32[64,512]{1,0:T(8,128)S(1)} %copy-done.24), kind=kLoop, calls=%fused_computation.98 | loop fusion | flops 25165824 | bytes 42074112 | tf_op jit(solution)/shard_map/convert_element_type | solution.py:222
  912.9 6.5 copy.28
  924.5 6.5 copy.29
  942.9 31.5 %all-to-all-done.4.left_ref = bf16[16,4,64,512]{3,2,1,0:T(8,128)(2,1)} async-done(((bf16[16,4,64,512]{3,2,1,0:T(8,128)(2,1)}), bf16[16,4,64,512]{3,2,1,0:T(8,128)(2,1)}, u32[]{:S(2)}, u32[]{:S(2)}) %all-to-all-start.4) | async-done | bytes 4194336 | tf_op jit(solution)/shard_map/all_to_all | solution.py:166
  974.4 10.8 all-to-all-start.5
  985.3 10.8 convert_reduce_fusion
  997.9 16.4 %convolution_bitcast_fusion = f32[320,64,512]{2,0,1:T(8,128)} fusion(bf16[64,64,512]{2,0,1:T(8,128)(2,1)S(1)} %get-tuple-element.40, f32[64,512]{1,0:T(8,128)S(1)} %add_rsqrt_fusion.4, f32[64,512]{1,0:T(8,128)S(1)} %broadcast_multiply_fusion.5, bf16[2,64,320]{2,1,0:T(8,128)(2,1)S(1)} %copy-done.26), kind=kOutput, calls=%fused_computation | convolution fusion | flops 1350565888 | bytes 46448640 | tf_op jit(solution)/shard_map/cd,cwi->dwi/dot_general | solution.py:215
  1014.3 17.3 %fusion.44 = (bf16[64,64,512]{2,0,1:T(8,128)(2,1)}, bf16[64,64,512]{2,0,1:T(8,128)(2,1)}) fusion(f32[320,64,512]{2,0,1:T(8,128)} %convolution_bitcast_fusion, f32[64,512]{1,0:T(8,128)S(1)} %copy-done.23), kind=kLoop, calls=%fused_computation.71 | loop fusion | flops 25165824 | bytes 42074112 | tf_op jit(solution)/shard_map/convert_element_type | solution.py:221
  1038.1 7.8 all-to-all-start.8
  1045.9 6.5 copy.35
  1052.4 43.5 %all-to-all-done.8.refs_1_ = bf16[16,4,64,512]{3,2,1,0:T(8,128)(2,1)} async-done(((bf16[16,4,64,512]{3,2,1,0:T(8,128)(2,1)}), bf16[16,4,64,512]{3,2,1,0:T(8,128)(2,1)}, u32[]{:S(2)}, u32[]{:S(2)}) %all-to-all-start.8) | async-done | bytes 4194336 | tf_op jit(solution)/shard_map/all_to_all | solution.py:166
  1095.9 10.5 all-to-all-start.10
  1106.4 7.9 shard_map.67
  1116.3 40.2 %all-to-all-done.10.left_ref = bf16[16,4,64,512]{3,2,1,0:T(8,128)(2,1)} async-done(((bf16[16,4,64,512]{3,2,1,0:T(8,128)(2,1)}), bf16[16,4,64,512]{3,2,1,0:T(8,128)(2,1)}, u32[]{:S(2)}, u32[]{:S(2)}) %all-to-all-start.10) | async-done | bytes 4194336 | tf_op jit(solution)/shard_map/all_to_all | solution.py:166
  1156.5 10.5 all-to-all-start.9
  1167.0 7.9 shard_map.68
  1177.0 40.1 %all-to-all-done.9 = bf16[16,4,64,512]{3,2,1,0:T(8,128)(2,1)} async-done(((bf16[16,4,64,512]{3,2,1,0:T(8,128)(2,1)}), bf16[16,4,64,512]{3,2,1,0:T(8,128)(2,1)}, u32[]{:S(2)}, u32[]{:S(2)}) %all-to-all-start.9) | async-done | bytes 4194336 | tf_op jit(solution)/shard_map/all_to_all | solution.py:166
  1217.1 10.9 all-to-all-start.11
  1237.7 10.9 convert_reduce_fusion.4
  1248.6 29.7 %all-to-all-done.11 = bf16[16,4,64,512]{3,2,1,0:T(8,128)(2,1)} async-done(((bf16[16,4,64,512]{3,2,1,0:T(8,128)(2,1)}), bf16[16,4,64,512]{3,2,1,0:T(8,128)(2,1)}, u32[]{:S(2)}, u32[]{:S(2)}) %all-to-all-start.11) | async-done | bytes 4194336 | tf_op jit(solution)/shard_map/all_to_all | solution.py:166
  1287.9 9.7 convert_reduce_fusion.2
  1308.3 134.5 %collective-permute-done.3 = bf16[64,64,512]{2,0,1:T(8,128)(2,1)S(1)} collective-permute-done((bf16[64,64,512]{2,0,1:T(8,128)(2,1)S(1)}, bf16[64,64,512]{2,0,1:T(8,128)(2,1)S(1)}, u32[]{:S(2)}, u32[]{:S(2)}) %collective-permute-start.3) | collective-permute-done | bytes 4194336 | tf_op jit(solution)/shard_map/ppermute | solution.py:172
  1449.0 38.9 %collective-permute-done.1 = bf16[64,64,512]{2,0,1:T(8,128)(2,1)S(1)} collective-permute-done((bf16[64,64,512]{2,0,1:T(8,128)(2,1)S(1)}, bf16[64,64,512]{2,0,1:T(8,128)(2,1)S(1)}, u32[]{:S(2)}, u32[]{:S(2)}) %collective-permute-start.1) | collective-permute-done | bytes 4194336 | tf_op jit(solution)/shard_map/ppermute | solution.py:172
  1503.2 6.5 pad_maximum_fusion
  1509.7 23.3 %copy.37 = bf16[128,64,1024]{2,1,0:T(8,128)(2,1)} copy(bf16[128,64,1024]{0,2,1:T(8,128)(2,1)} %pad_maximum_fusion) | data formatting | bytes 33554432 | tf_op jit(solution)/shard_map/concatenate | solution.py:245
  (135 shorter events, 159.4 us)
Async XLA Ops:
  0.0 1493.6 %copy-start = (bf16[64,128]{1,0:T(8,128)(2,1)S(1)}, bf16[64,128]{1,0:T(8,128)(2,1)}, u32[]{:S(2)}) copy-start(bf16[64,128]{1,0:T(8,128)(2,1)} %param.11) | copy-start | bytes 49156
  0.0 444.5 %collective-permute-start = (s32[8]{0:T(128)}, s32[8]{0:T(128)S(1)}, u32[]{:S(2)}, u32[]{:S(2)}) collective-permute-start(s32[8]{0:T(128)} %bitcast.191), channel_id=1, source_target_pairs={{0,16},{16,0},{1,17},{17,1},{2,18},{18,2},{3,19},{19,3},{4,20},{20... | collective-permute-start | bytes 104 | tf_op jit(solution)/shard_map/ppermute | solution.py:185
  58.4 386.1 %copy-start.27 = (s32[1,8]{1,0:T(1,128)S(1)}, s32[1,8]{1,0:T(1,128)}, u32[]{:S(2)}) copy-start(s32[1,8]{1,0:T(1,128)} %param.7) | copy-start | bytes 100
  438.3 6.2 copy-start.1
  461.1 34.7 %copy-start.22 = (f32[64,512]{1,0:T(8,128)}, f32[64,512]{1,0:T(8,128)S(1)}, u32[]{:S(2)}) copy-start(f32[64,512]{1,0:T(8,128)S(1)} %get-tuple-element.22) | copy-start | bytes 393220
  471.5 1.0 copy-start.17
  471.5 5.0 copy-start.19
  471.5 24.2 %copy-start.11 = (bf16[64,64,128]{2,1,0:T(8,128)(2,1)}, bf16[64,64,128]{2,1,0:T(8,128)(2,1)S(1)}, u32[]{:S(2)}) copy-start(bf16[64,64,128]{2,1,0:T(8,128)(2,1)S(1)} %get-tuple-element.14) | copy-start | bytes 3145732
  471.6 24.2 %copy-start.13 = (bf16[64,64,128]{2,1,0:T(8,128)(2,1)}, bf16[64,64,128]{2,1,0:T(8,128)(2,1)S(1)}, u32[]{:S(2)}) copy-start(bf16[64,64,128]{2,1,0:T(8,128)(2,1)S(1)} %get-tuple-element.15) | copy-start | bytes 3145732
  471.6 24.2 %copy-start.15 = (bf16[64,64,128]{2,1,0:T(8,128)(2,1)}, bf16[64,64,128]{2,1,0:T(8,128)(2,1)S(1)}, u32[]{:S(2)}) copy-start(bf16[64,64,128]{2,1,0:T(8,128)(2,1)S(1)} %get-tuple-element.16) | copy-start | bytes 3145732
  471.6 24.2 %copy-start.16 = (bf16[64,64,128]{2,1,0:T(8,128)(2,1)}, bf16[64,64,128]{2,1,0:T(8,128)(2,1)S(1)}, u32[]{:S(2)}) copy-start(bf16[64,64,128]{2,1,0:T(8,128)(2,1)S(1)} %get-tuple-element.17) | copy-start | bytes 3145732
  511.3 43.5 %copy-start.25 = (f32[64,512]{1,0:T(8,128)S(1)}, f32[64,512]{1,0:T(8,128)}, u32[]{:S(2)}) copy-start(f32[64,512]{1,0:T(8,128)} %get-tuple-element.48) | copy-start | bytes 393220
  515.7 42.3 %copy-start.26 = (bf16[2,64,320]{2,1,0:T(8,128)(2,1)S(1)}, bf16[2,64,320]{2,1,0:T(8,128)(2,1)}, u32[]{:S(2)}) copy-start(bf16[2,64,320]{2,1,0:T(8,128)(2,1)} %param.9) | copy-start | bytes 245764
  515.7 89.2 %all-to-all-start.2 = ((bf16[16,4,64,512]{3,2,1,0:T(8,128)(2,1)}), bf16[16,4,64,512]{3,2,1,0:T(8,128)(2,1)}, u32[]{:S(2)}, u32[]{:S(2)}) async-start(bf16[16,4,64,512]{3,2,1,0:T(8,128)(2,1)} %bitcast.181), calls=%async_computation.2 | async-start | bytes 8388608 | tf_op jit(solution)/shard_map/all_to_all | solution.py:166
  557.9 17.6 %copy-start.24 = (f32[64,512]{1,0:T(8,128)S(1)}, f32[64,512]{1,0:T(8,128)}, u32[]{:S(2)}) copy-start(f32[64,512]{1,0:T(8,128)} %get-tuple-element.21) | copy-start | bytes 393220
  604.9 60.5 %all-to-all-start = ((bf16[16,4,64,512]{3,2,1,0:T(8,128)(2,1)}), bf16[16,4,64,512]{3,2,1,0:T(8,128)(2,1)}, u32[]{:S(2)}, u32[]{:S(2)}) async-start(bf16[16,4,64,512]{3,2,1,0:T(8,128)(2,1)} %bitcast.182), calls=%async_computation | async-start | bytes 8388608 | tf_op jit(solution)/shard_map/all_to_all | solution.py:166
  665.4 60.9 %all-to-all-start.1 = ((bf16[16,4,64,512]{3,2,1,0:T(8,128)(2,1)}), bf16[16,4,64,512]{3,2,1,0:T(8,128)(2,1)}, u32[]{:S(2)}, u32[]{:S(2)}) async-start(bf16[16,4,64,512]{3,2,1,0:T(8,128)(2,1)} %bitcast.183), calls=%async_computation.1 | async-start | bytes 8388608 | tf_op jit(solution)/shard_map/all_to_all | solution.py:166
  726.2 60.4 %all-to-all-start.6 = ((bf16[16,4,64,512]{3,2,1,0:T(8,128)(2,1)}), bf16[16,4,64,512]{3,2,1,0:T(8,128)(2,1)}, u32[]{:S(2)}, u32[]{:S(2)}) async-start(bf16[16,4,64,512]{3,2,1,0:T(8,128)(2,1)} %bitcast.185), calls=%async_computation.6 | async-start | bytes 8388608 | tf_op jit(solution)/shard_map/all_to_all | solution.py:166
  744.5 2.0 copy-start.4
  786.7 60.6 %all-to-all-start.3 = ((bf16[16,4,64,512]{3,2,1,0:T(8,128)(2,1)}), bf16[16,4,64,512]{3,2,1,0:T(8,128)(2,1)}, u32[]{:S(2)}, u32[]{:S(2)}) async-start(bf16[16,4,64,512]{3,2,1,0:T(8,128)(2,1)} %copy-done.4), calls=%async_computation.3 | async-start | bytes 8388608 | tf_op jit(solution)/shard_map/all_to_all | solution.py:166
  805.1 2.0 copy-start.2
  847.2 72.2 %all-to-all-start.7 = ((bf16[16,4,64,512]{3,2,1,0:T(8,128)(2,1)}), bf16[16,4,64,512]{3,2,1,0:T(8,128)(2,1)}, u32[]{:S(2)}, u32[]{:S(2)}) async-start(bf16[16,4,64,512]{3,2,1,0:T(8,128)(2,1)} %copy-done.2), calls=%async_computation.7 | async-start | bytes 8388608 | tf_op jit(solution)/shard_map/all_to_all | solution.py:166
  857.7 9.7 copy-start.18
  857.7 9.7 copy-start.20
  857.7 9.7 copy-start.28
  877.2 18.1 %copy-start.7 = (bf16[64,64,512]{2,0,1:T(8,128)(2,1)}, bf16[64,64,512]{2,0,1:T(8,128)(2,1)S(1)}, u32[]{:S(2)}) copy-start(bf16[64,64,512]{2,0,1:T(8,128)(2,1)S(1)} %get-tuple-element.42) | copy-start | bytes 12582916
  919.4 55.0 %all-to-all-start.4 = ((bf16[16,4,64,512]{3,2,1,0:T(8,128)(2,1)}), bf16[16,4,64,512]{3,2,1,0:T(8,128)(2,1)}, u32[]{:S(2)}, u32[]{:S(2)}) async-start(bf16[16,4,64,512]{3,2,1,0:T(8,128)(2,1)} %bitcast.180), calls=%async_computation.4 | async-start | bytes 8388608 | tf_op jit(solution)/shard_map/all_to_all | solution.py:166
  937.2 48.1 %copy-start.12 = (bf16[64,64,128]{2,1,0:T(8,128)(2,1)S(1)}, bf16[64,64,128]{2,1,0:T(8,128)(2,1)}, u32[]{:S(2)}) copy-start(bf16[64,64,128]{2,1,0:T(8,128)(2,1)} %copy-done.11) | copy-start | bytes 3145732
  937.2 48.1 %copy-start.14 = (bf16[64,64,128]{2,1,0:T(8,128)(2,1)S(1)}, bf16[64,64,128]{2,1,0:T(8,128)(2,1)}, u32[]{:S(2)}) copy-start(bf16[64,64,128]{2,1,0:T(8,128)(2,1)} %copy-done.13) | copy-start | bytes 3145732
  974.4 63.7 %all-to-all-start.5 = ((bf16[16,4,64,512]{3,2,1,0:T(8,128)(2,1)}), bf16[16,4,64,512]{3,2,1,0:T(8,128)(2,1)}, u32[]{:S(2)}, u32[]{:S(2)}) async-start(bf16[16,4,64,512]{3,2,1,0:T(8,128)(2,1)} %bitcast.179), calls=%async_computation.5 | async-start | bytes 8388608 | tf_op jit(solution)/shard_map/all_to_all | solution.py:166
  996.2 18.1 %copy-start.9 = (bf16[64,64,512]{2,0,1:T(8,128)(2,1)}, bf16[64,64,512]{2,0,1:T(8,128)(2,1)S(1)}, u32[]{:S(2)}) copy-start(bf16[64,64,512]{2,0,1:T(8,128)(2,1)S(1)} %get-tuple-element.40) | copy-start | bytes 12582916
  997.9 16.4 %copy-start.23 = (f32[64,512]{1,0:T(8,128)S(1)}, f32[64,512]{1,0:T(8,128)}, u32[]{:S(2)}) copy-start(f32[64,512]{1,0:T(8,128)} %copy-done.22) | copy-start | bytes 393220
  1038.1 57.8 %all-to-all-start.8 = ((bf16[16,4,64,512]{3,2,1,0:T(8,128)(2,1)}), bf16[16,4,64,512]{3,2,1,0:T(8,128)(2,1)}, u32[]{:S(2)}, u32[]{:S(2)}) async-start(bf16[16,4,64,512]{3,2,1,0:T(8,128)(2,1)} %bitcast.184), calls=%async_computation.8 | async-start | bytes 8388608 | tf_op jit(solution)/shard_map/all_to_all | solution.py:166
  1095.9 60.6 %all-to-all-start.10 = ((bf16[16,4,64,512]{3,2,1,0:T(8,128)(2,1)}), bf16[16,4,64,512]{3,2,1,0:T(8,128)(2,1)}, u32[]{:S(2)}, u32[]{:S(2)}) async-start(bf16[16,4,64,512]{3,2,1,0:T(8,128)(2,1)} %bitcast.186), calls=%async_computation.10 | async-start | bytes 8388608 | tf_op jit(solution)/shard_map/all_to_all | solution.py:166
  1114.4 1.9 copy-start.5
  1156.5 60.6 %all-to-all-start.9 = ((bf16[16,4,64,512]{3,2,1,0:T(8,128)(2,1)}), bf16[16,4,64,512]{3,2,1,0:T(8,128)(2,1)}, u32[]{:S(2)}, u32[]{:S(2)}) async-start(bf16[16,4,64,512]{3,2,1,0:T(8,128)(2,1)} %copy-done.5), calls=%async_computation.9 | async-start | bytes 8388608 | tf_op jit(solution)/shard_map/all_to_all | solution.py:166
  1174.9 2.0 copy-start.3
  1217.1 61.2 %all-to-all-start.11 = ((bf16[16,4,64,512]{3,2,1,0:T(8,128)(2,1)}), bf16[16,4,64,512]{3,2,1,0:T(8,128)(2,1)}, u32[]{:S(2)}, u32[]{:S(2)}) async-start(bf16[16,4,64,512]{3,2,1,0:T(8,128)(2,1)} %copy-done.3), calls=%async_computation.11 | async-start | bytes 8388608 | tf_op jit(solution)/shard_map/all_to_all | solution.py:166
  1228.0 9.7 copy-start.8
  1278.2 9.7 copy-start.10
  1297.6 5.4 copy-start.6
  1301.7 141.2 %collective-permute-start.3 = (bf16[64,64,512]{2,0,1:T(8,128)(2,1)S(1)}, bf16[64,64,512]{2,0,1:T(8,128)(2,1)S(1)}, u32[]{:S(2)}, u32[]{:S(2)}) collective-permute-start(bf16[64,64,512]{2,0,1:T(8,128)(2,1)S(1)} %fusion.21), channel_id=1, source_target_pairs={{8,0},{16,24},{9,1},{17,25},{10,2},{18,26},{11,3},{19,27},{12,4},{... | collective-permute-start | bytes 12582920 | tf_op jit(solution)/shard_map/ppermute | solution.py:172
  1307.0 180.8 %collective-permute-start.1 = (bf16[64,64,512]{2,0,1:T(8,128)(2,1)S(1)}, bf16[64,64,512]{2,0,1:T(8,128)(2,1)S(1)}, u32[]{:S(2)}, u32[]{:S(2)}) collective-permute-start(bf16[64,64,512]{2,0,1:T(8,128)(2,1)S(1)} %fusion.25), channel_id=1, source_target_pairs={{8,0},{16,24},{9,1},{17,25},{10,2},{18,26},{11,3},{19,27},{12,4},{... | collective-permute-start | bytes 12582920 | tf_op jit(solution)/shard_map/ppermute | solution.py:172
  1445.7 47.8 %collective-permute-start.4 = (bf16[64,64,512]{2,0,1:T(8,128)(2,1)S(1)}, bf16[64,64,512]{2,0,1:T(8,128)(2,1)}, u32[]{:S(2)}, u32[]{:S(2)}) collective-permute-start(bf16[64,64,512]{2,0,1:T(8,128)(2,1)S(1)} %maximum_convert_fusion), channel_id=1, source_target_pairs={{0,16},{24,8},{1,17},{25,9},{2,18},{26,10},{3,19},{27,11},{4,20},{... | collective-permute-start | bytes 12582920 | tf_op jit(solution)/shard_map/ppermute | solution.py:172
  1490.3 5.9 copy-start.21
  1490.3 8.2 collective-permute-start.2

commit v2 on v1

--- a/solution.py
+++ b/solution.py
@@ -1,3 +1,5 @@
+import functools
+
 import jax
 import jax.numpy as jnp
 from jax import lax
@@ -28,6 +30,214 @@
 
 
 SPLIT = 2
+SUB = 8
+PARTS = 2
+
+
+def widened(weight, source):
+    depth, columns = weight.shape
+    size = source.shape[0]
+    pick = (source == lax.broadcasted_iota(jnp.int32, (size, columns), 1)).astype(weight.dtype)
+    taken = lax.dot_general(
+        pick, weight, (((1,), (1,)), ((), ())), preferred_element_type=jnp.float32
+    ).astype(weight.dtype)
+    grow = lax.broadcasted_iota(jnp.int32, (depth, depth * SUB), 1) // SUB
+    grow = (grow == lax.broadcasted_iota(jnp.int32, grow.shape, 0)).astype(weight.dtype)
+    wide = jnp.dot(taken, grow, preferred_element_type=jnp.float32)
+    row = lax.broadcasted_iota(jnp.int32, wide.shape, 0) % SUB
+    lane = lax.broadcasted_iota(jnp.int32, wide.shape, 1) % SUB
+    return jnp.where(row == lane, wide, 0.0).astype(weight.dtype)
+
+
+def widen_kernel(proj_ref, out_ref, final_ref, wide_ref, out_wide_ref, final_wide_ref):
+    size = CH // PARTS
+    for layer in range(NLAYER):
+        for part in range(PARTS):
+            rows = lax.broadcasted_iota(jnp.int32, (5 * size * SUB, 5 * CH), 0) // SUB
+            source = rows // size * CH + part * size + rows % size
+            wide_ref[layer, part] = widened(proj_ref[layer], source)
+        rows = lax.broadcasted_iota(jnp.int32, (CH * SUB, CH), 0) // SUB
+        out_wide_ref[layer] = widened(out_ref[layer], rows)
+    columns = final_ref.shape[1]
+    rows = lax.broadcasted_iota(jnp.int32, (columns * SUB, columns), 0) // SUB
+    final_wide_ref[...] = widened(final_ref[...], rows)
+
+
+def widen(proj_weight, out_weight, final_weight):
+    kind = proj_weight.dtype
+    return pl.pallas_call(
+        widen_kernel,
+        out_shape=[
+            jax.ShapeDtypeStruct((NLAYER, PARTS, 5 * CH // PARTS * SUB, CH * SUB), kind),
+            jax.ShapeDtypeStruct((NLAYER, CH * SUB, CH * SUB), kind),
+            jax.ShapeDtypeStruct((final_weight.shape[1] * SUB, CH * SUB), kind),
+        ],
+        compiler_params=PARAMS,
+    )(proj_weight, out_weight, final_weight)
+
+
+def sigmoid(values):
+    return 0.5 * jnp.tanh(0.5 * values) + 0.5
+
+
+def flat_dot(weight, values):
+    channels, sub, lanes = values.shape
+    return jnp.dot(
+        weight,
+        values.reshape(channels * sub, lanes).astype(jnp.bfloat16),
+        preferred_element_type=jnp.float32,
+    ).reshape(weight.shape[0] // sub, sub, lanes)
+
+
+def project(values, wide_ref, mask_ref, left_ref, right_ref, gate_ref):
+    normed = channel_norm(values)
+    mask = mask_ref[...][None]
+    size = CH // PARTS
+    for part in range(PARTS):
+        projected = flat_dot(wide_ref[part], normed)
+        piece = slice(part * size, (part + 1) * size)
+        left = sigmoid(projected[:size]) * projected[size : 2 * size] * mask
+        left_ref[piece] = left.astype(left_ref.dtype)
+        right = sigmoid(projected[2 * size : 3 * size]) * projected[3 * size : 4 * size] * mask
+        right_ref[piece] = right.astype(right_ref.dtype)
+        gate_ref[piece] = sigmoid(projected[4 * size :]).astype(gate_ref.dtype)
+
+
+def updated(values, back_ref, gate_ref, out_ref):
+    normed = channel_norm(back_ref[...].astype(jnp.float32))
+    update = flat_dot(out_ref[...], normed)
+    pair = values + gate_ref[...].astype(jnp.float32) * update
+    return pair.astype(jnp.bfloat16)
+
+
+def tiles_of(refs):
+    return jnp.concatenate([ref[...].astype(jnp.float32) for ref in refs], axis=-1)
+
+
+def first_kernel(tiles, ids_ref, *refs):
+    project(tiles_of(refs[:tiles]), *refs[tiles:])
+
+
+def middle_kernel(tiles, ids_ref, *refs):
+    back_ref, gate_ref, out_ref, wide_ref, mask_ref = refs[tiles : tiles + 5]
+    pair_ref, left_ref, right_ref, next_ref = refs[tiles + 5 :]
+    pair = updated(tiles_of(refs[:tiles]), back_ref, gate_ref, out_ref)
+    pair_ref[...] = pair
+    project(pair.astype(jnp.float32), wide_ref, mask_ref, left_ref, right_ref, next_ref)
+
+
+def last_kernel(pair_ref, back_ref, gate_ref, out_ref, final_ref):
+    pair = updated(pair_ref[...].astype(jnp.float32), back_ref, gate_ref, out_ref)
+    final_ref[...] = channel_norm(pair.astype(jnp.float32)).astype(final_ref.dtype)
+
+
+def end_kernel(home_ref, *refs):
+    hiddens, shareds = refs[: len(refs) // 2 - 1], refs[len(refs) // 2 - 1 : -2]
+    wide_ref, out_ref = refs[-2:]
+    home = home_ref[0] == 1
+    lanes = hiddens[0].shape[-1]
+    for number, (hidden_ref, shared_ref) in enumerate(zip(hiddens, shareds)):
+        hidden = jnp.where(
+            home, hidden_ref[...].astype(jnp.float32), shared_ref[...].astype(jnp.float32)
+        )
+        out_ref[:, :, number * lanes : (number + 1) * lanes] = flat_dot(
+            wide_ref[...], hidden
+        ).astype(out_ref.dtype)
+
+
+PARAMS = pltpu.CompilerParams(vmem_limit_bytes=48 << 20)
+
+
+def cost(flops, moved_bytes):
+    return pl.CostEstimate(flops=int(flops), bytes_accessed=int(moved_bytes), transcendentals=0)
+
+
+def by_columns(shape):
+    return pl.BlockSpec((shape[0], SUB, shape[2]), lambda w, *_: (0, w, 0))
+
+
+def whole(shape):
+    return pl.BlockSpec(shape, lambda w, *_: (0,) * len(shape))
+
+
+def layer_of(shape, layer):
+    return pl.BlockSpec((None, *shape[1:]), lambda w, *_: (layer,) + (0,) * (len(shape) - 1))
+
+
+def tile_specs(got, number, per):
+    def at(tile):
+        return pl.BlockSpec(
+            (None, got.shape[1], SUB, got.shape[3]),
+            lambda w, ids: (ids[number * per + tile], 0, w, 0),
+        )
+
+    return [at(tile) for tile in range(per)]
+
+
+def stage(kernel, specs, out_shapes, ids, operands, flops):
+    moved_bytes = sum(2 * shape.size for shape in out_shapes) * 2
+    width = out_shapes[0].shape[1]
+    return pl.pallas_call(
+        kernel,
+        grid_spec=pltpu.PrefetchScalarGridSpec(
+            num_scalar_prefetch=1,
+            grid=(width // SUB,),
+            in_specs=specs,
+            out_specs=[by_columns(shape.shape) for shape in out_shapes],
+        ),
+        out_shape=out_shapes,
+        compiler_params=PARAMS,
+        cost_estimate=cost(flops, moved_bytes),
+    )(ids, *operands)
+
+
+def first_stage(number, per, ids, got, wide, mask):
+    _, channels, width, tile = got.shape
+    shape = jax.ShapeDtypeStruct((channels, width, per * tile), got.dtype)
+    specs = tile_specs(got, number, per) + [
+        layer_of(wide.shape, 0),
+        pl.BlockSpec((SUB, per * tile), lambda w, *_: (w, 0)),
+    ]
+    kernel = functools.partial(first_kernel, per)
+    flops = 2 * wide.size // NLAYER * width // SUB * per * tile
+    return stage(kernel, specs, [shape] * 3, ids, [got] * per + [wide, mask], flops)
+
+
+def middle_stage(layer, number, per, ids, got, back, gate, out_wide, wide, mask):
+    _, channels, width, tile = got.shape
+    shape = jax.ShapeDtypeStruct((channels, width, per * tile), got.dtype)
+    specs = tile_specs(got, number, per) + [
+        by_columns(back.shape),
+        by_columns(gate.shape),
+        layer_of(out_wide.shape, layer),
+        layer_of(wide.shape, layer + 1),
+        pl.BlockSpec((SUB, per * tile), lambda w, *_: (w, 0)),
+    ]
+    kernel = functools.partial(middle_kernel, per)
+    flops = 2 * (wide.size + out_wide.size) // NLAYER * width // SUB * per * tile
+    operands = [got] * per + [back, gate, out_wide, wide, mask]
+    return stage(kernel, specs, [shape] * 4, ids, operands, flops)
+
+
+def last_stage(layer, pair, back, gate, out_wide):
+    return pl.pallas_call(
+        last_kernel,
+        grid=(pair.shape[1] // SUB,),
+        in_specs=[by_columns(pair.shape)] * 3 + [layer_of(out_wide.shape, layer)],
+        out_specs=by_columns(pair.shape),
+        out_shape=jax.ShapeDtypeStruct(pair.shape, pair.dtype),
+        compiler_params=PARAMS,
+        cost_estimate=cost(out_wide.size * pair.size // CH // SUB, 8 * pair.size),
+    )(pair, back, gate, out_wide)
+
+
+def end_stage(home, hiddens, shareds, wide):
+    channels, width, lanes = hiddens[0].shape
+    shape = (wide.shape[0] // SUB, width, lanes * len(hiddens))
+    out = jax.ShapeDtypeStruct(shape, hiddens[0].dtype)
+    specs = [by_columns(hiddens[0].shape)] * (2 * len(hiddens)) + [whole(wide.shape)]
+    flops = 2 * wide.size * width // SUB * shape[2]
+    return stage(end_kernel, specs, [out], home, [*hiddens, *shareds, wide], flops)[0]
 
 
 def product_kernel(left_ref, *refs):
@@ -90,7 +300,7 @@
     def outgoing(step):
         block = lax.rem(mine + step, blocks)
         return pltpu.make_async_remote_copy(
-            src_ref=send_ref.at[block],
+            src_ref=send_ref.at[:, block],
             dst_ref=got_ref.at[row],
             send_sem=send_sem.at[step],
             recv_sem=recv_sem.at[row],
@@ -104,7 +314,7 @@
 
     @pl.when(home)
     def _():
-        bring = pltpu.make_async_copy(send_ref.at[mine], hold, hold_sem.at[0])
+        bring = pltpu.make_async_copy(send_ref.at[:, mine], hold, hold_sem.at[0])
         bring.start()
         bring.wait()
         put = pltpu.make_async_copy(hold, got_ref.at[row], hold_sem.at[1])
@@ -117,7 +327,7 @@
 
     def incoming(slot):
         return pltpu.make_async_remote_copy(
-            src_ref=send_ref.at[0],
+            src_ref=send_ref.at[:, 0],
             dst_ref=got_ref.at[slot],
             send_sem=send_sem.at[0],
             recv_sem=recv_sem.at[slot],
@@ -141,14 +351,14 @@
 
 
 def spread(send):
-    blocks = send.shape[0]
+    channels, blocks, width, tile = send.shape
     return pl.pallas_call(
         spread_kernel,
         in_specs=[pl.BlockSpec(memory_space=pl.ANY)],
         out_specs=pl.BlockSpec(memory_space=pl.ANY),
-        out_shape=jax.ShapeDtypeStruct(send.shape, send.dtype),
+        out_shape=jax.ShapeDtypeStruct((blocks, channels, width, tile), send.dtype),
         scratch_shapes=[
-            pltpu.VMEM(send.shape[1:], send.dtype),
+            pltpu.VMEM((channels, width, tile), send.dtype),
             pltpu.SemaphoreType.DMA((blocks,)),
             pltpu.SemaphoreType.DMA((blocks,)),
             pltpu.SemaphoreType.DMA((2,)),
@@ -170,6 +380,10 @@
     halves = lax.axis_size("half")
     steps = [(a * halves + b, c * halves + d) for (a, b), (c, d) in pairs]
     return lax.ppermute(value, ("core", "half"), steps)
+
+
+def after(value, *others):
+    return lax.optimization_barrier((value, *others))[0]
 
 
 def in_halves(pair_maps, crop_tiles, full_length, proj_weight, out_weight, final_weight):
@@ -181,6 +395,7 @@
     per_group = CH // row_count
     tiles = CROP // TILE
     chunk = CROP // SPLIT
+    per = tiles // SPLIT
     held_ids = crop_tiles[0]
     other_ids = lax.ppermute(held_ids, "core", [(0, 1), (1, 0)])
     crop_ids = jnp.where(core == half, held_ids, other_ids)
@@ -198,51 +413,42 @@
         ],
         axis=2,
     )
-    send = jnp.transpose(columns, (2, 1, 0)).reshape(row_count, col_width, CH, TILE)
+    send = jnp.transpose(columns, (1, 2, 0)).reshape(CH, row_count, col_width, TILE)
     got = spread(send)
-    per = tiles // SPLIT
-    current = []
-    for number in range(SPLIT):
-        pieces = [
-            lax.dynamic_index_in_dim(got, crop_ids[number * per + tile], 0, keepdims=False)
-            for tile in range(per)
-        ]
-        current.append(jnp.transpose(jnp.concatenate(pieces, axis=2), (1, 0, 2)))
-    for layer_idx in range(NLAYER):
-        lefts, rights, gates = [], [], []
-        for values, mask in zip(current, masks):
-            normed_in = channel_norm(values.astype(jnp.float32)).astype(jnp.bfloat16)
-            projected = jnp.einsum(
-                "cd,cwi->dwi", proj_weight[layer_idx], normed_in, preferred_element_type=jnp.float32
-            )
-            left = jax.nn.sigmoid(projected[:CH]) * projected[CH : 2 * CH] * mask
-            right = jax.nn.sigmoid(projected[2 * CH : 3 * CH]) * projected[3 * CH : 4 * CH] * mask
-            shape = (row_count, per_group, col_width, chunk)
-            rights.append(exchange(right.astype(jnp.bfloat16).reshape(shape)))
-            lefts.append(exchange(left.astype(jnp.bfloat16).reshape(shape)))
-            gates.append(jax.nn.sigmoid(projected[4 * CH :]))
+    wides, outs, final_wide = widen(proj_weight, out_weight, final_weight)
+    shape = (row_count, per_group, col_width, chunk)
+    ready = [
+        first_stage(number, per, crop_ids, got, wides, masks[number]) for number in range(SPLIT)
+    ]
+    pairs = [None] * SPLIT
+    for layer in range(NLAYER):
+        lefts = [item[0].reshape(shape) for item in ready]
+        rights = [exchange(item[1].reshape(shape)) for item in ready]
+        gates = [item[2] for item in ready]
         following = []
-        for values, left, gate in zip(current, lefts, gates):
-            merged = exchange(channel_products(left, rights)).reshape(CH, col_width, chunk)
-            normed_out = channel_norm(merged.astype(jnp.float32)).astype(jnp.bfloat16)
-            update = jnp.einsum(
-                "cd,cwi->dwi", out_weight[layer_idx], normed_out, preferred_element_type=jnp.float32
-            )
-            following.append((values.astype(jnp.float32) + gate * update).astype(jnp.bfloat16))
-        current = following
-    results = []
-    for values in current:
-        normed_final = channel_norm(values.astype(jnp.float32)).astype(jnp.bfloat16)
+        back = None
+        for number in range(SPLIT):
+            left = lefts[number] if back is None else after(lefts[number], back)
+            back = exchange(channel_products(exchange(left), rights))
+            merged = back.reshape(CH, col_width, chunk)
+            if layer + 1 < NLAYER:
+                pair, left, right, gate = middle_stage(
+                    layer, number, per, crop_ids, got, merged, gates[number], outs, wides,
+                    masks[number],
+                )
+                pairs[number] = pair
+                following.append((left, right, gate))
+            else:
+                following.append(last_stage(layer, pairs[number], merged, gates[number], outs))
+        ready = following
+    hiddens, shareds = [], []
+    for normed_final in ready:
         across = moved(normed_final, [((0, 1), (0, 0)), ((1, 0), (1, 1))])
         summed = normed_final.astype(jnp.float32) + across.astype(jnp.float32)
-        hidden = jnp.maximum(summed / halves, 0.0).astype(jnp.bfloat16)
-        shared = moved(hidden, [((0, 0), (1, 0)), ((1, 1), (0, 1))])
-        hidden = jnp.where(core == half, hidden, shared)
-        results.append(
-            jnp.einsum("cz,cwi->zwi", final_weight, hidden, preferred_element_type=jnp.float32)
-            .astype(jnp.bfloat16)
-        )
-    return jnp.concatenate(results, axis=2)
+        hiddens.append(jnp.maximum(summed / halves, 0.0).astype(jnp.bfloat16))
+        shareds.append(moved(hiddens[-1], [((0, 0), (1, 0)), ((1, 1), (0, 1))]))
+    home = (core == half).astype(jnp.int32)[None]
+    return end_stage(home, hiddens, shareds, final_wide)
 
 
 def on_device(pair_maps, crop_tiles, full_length, proj_weight, out_weight, final_weight):

time: 1550 us -> 1380 us (0.89)
  blocking collectives: 0 us -> 391 us
  waiting for transfers between devices: 538 us -> 280 us
  Pallas kernels: 412 us -> 543 us
  other arithmetic: 144 us -> 16.2 us
  matrix products: 116 us -> 0 us
  starting transfers between devices: 157 us -> 72 us
  local copies, waits for them, and re-layouts: 145 us -> 70.3 us
  between operations: 21.7 us -> 5.93 us
    all_to_all x0 -> x7, blocking collectives: none -> 391 us  [exchange(): return lax.all_to_all(value, GROUP, split_axis=0, concat_axis=0, tiled=True)]
    all_to_all x12 -> x5, waiting for transfers between devices: 362 us -> 182 us  [exchange(): return lax.all_to_all(value, GROUP, split_axis=0, concat_axis=0, tiled=True)]
    pallas_call x0 -> x8, Pallas kernels: none -> 135 us  [the longest x5 105 us: stage(): pl.pallas_call(kernel, grid_spec=pltpu.PrefetchScalarGridSpec(num_scalar_...]
    dot_general x10 -> x0, matrix products: 116 us -> none  [the longest x4 67.7 us: in_halves(): jnp.einsum('cd,cwi->dwi', proj_weight[layer_idx], normed_in, preferred_el...]
    all_to_all x12 -> x5, starting transfers between devices: 147 us -> 62.2 us  [exchange(): return lax.all_to_all(value, GROUP, split_axis=0, concat_axis=0, tiled=True)]
    convert_element_type x12 -> x2, other arithmetic: 91.2 us -> 11.1 us  [in_halves(): hiddens.append(jnp.maximum(summed / halves, 0.0).astype(jnp.bfloat16))]
    ppermute x4, waiting for transfers between devices: 176 us -> 97 us  [moved(): return lax.ppermute(value, ('core', 'half'), steps)]
    convert_element_type x8 -> x0, local copies, waits for them, and re-layouts: 47.9 us -> none  [the longest x4 24.1 us: in_halves(): lefts.append(exchange(left.astype(jnp.bfloat16).reshape(shape)))]
  transfers between devices with their start and end apart: 17 -> 10, of which waited for: 13 -> 8; matrix products, arithmetic and copies ran while one was open for 18% -> 4% of each run, Pallas kernels for 27% -> 35%
where the time goes in v2:
time: 1380 us
  Pallas kernels  543 us (39%)
  blocking collectives  391 us (28%)
  waiting for transfers between devices  280 us (20%)
  starting transfers between devices  72 us (5%)
  local copies, waits for them, and re-layouts  70.3 us (5%)
  other arithmetic  16.2 us (1%)
    all_to_all x7, blocking collectives, exchange(): return lax.all_to_all(value, GROUP, split_axis=0, concat_axis=0, tiled=True)  391 us
    pallas_call x1, Pallas kernels, spread(): pl.pallas_call(spread_kernel, in_specs=[pl.BlockSpec(memory_space=pl.ANY)...  380 us
    all_to_all x5, waiting for transfers between devices, exchange(): return lax.all_to_all(value, GROUP, split_axis=0, concat_axis=0, tiled=True)  182 us
    pallas_call x5, Pallas kernels, stage(): pl.pallas_call(kernel, grid_spec=pltpu.PrefetchScalarGridSpec(num_scalar_...  105 us
    ppermute x4, waiting for transfers between devices, moved(): return lax.ppermute(value, ('core', 'half'), steps)  97 us
    all_to_all x5, starting transfers between devices, exchange(): return lax.all_to_all(value, GROUP, split_axis=0, concat_axis=0, tiled=True)  62.2 us
    unnamed x37, local copies, waits for them, and re-layouts  41.8 us
    pallas_call x4, Pallas kernels, channel_products(): pl.pallas_call(product_kernel, grid=(channels,), in_specs=[spec] * (1 + l...  28.5 us
  transfers between devices with their start and end apart: 10, of which 8 were waited for; matrix products, arithmetic and copies ran while one was open for 4% of the time, Pallas kernels for 35%

profile of v2, /device:TPU:0, one launch (start us, length us, event | category | flops | bytes accessed | tf_op | source)
XLA Modules:
  0.0 1377.4 jit_solution(14274641052997925435)
XLA Ops:
  7.9 3.1 bitcast_dynamic-update-slice_fusion.7
  10.9 3.1 bitcast_dynamic-update-slice_fusion.6
  14.0 3.1 bitcast_dynamic-update-slice_fusion.5
  17.1 3.1 bitcast_dynamic-update-slice_fusion.4
  20.2 3.1 bitcast_dynamic-update-slice_fusion.3
  23.3 3.1 bitcast_dynamic-update-slice_fusion.2
  26.3 3.1 bitcast_dynamic-update-slice_fusion.1
  29.4 3.1 bitcast_dynamic-update-slice_fusion
  32.5 23.0 %copy.7 = bf16[64,1024,128]{2,1,0:T(8,128)(2,1)} copy(bf16[64,1024,128]{1,0,2:T(8,128)(2,1)} %bitcast.26) | data formatting | bytes 33554432 | tf_op jit(solution)/shard_map/transpose | solution.py:416
  55.5 379.7 %shard_map.64.refs_0_.refs_1_.refs_2_.refs_3_ = bf16[16,64,64,128]{3,2,1,0:T(8,128)(2,1)S(1)} custom-call(bf16[64,16,64,128]{3,2,1,0:T(8,128)(2,1)} %bitcast.70), custom_call_target="tpu_custom_call" | custom-call | tf_op jit(solution)/shard_map/pallas_call | solution.py:355
  435.2 6.2 copy-done
  441.4 5.7 shard_map.65
  447.8 4.4 compare_select_fusion.1
  453.0 18.9 %shard_map.67 = (bf16[64,64,512]{2,1,0:T(8,128)(2,1)S(1)}, bf16[64,64,512]{2,1,0:T(8,128)(2,1)}, bf16[64,64,512]{2,1,0:T(8,128)(2,1)}) custom-call(s32[8]{0:T(128)S(1)} %broadcast_select_fusion.ids_ref, bf16[16,64,64,128]{3,2,1,0:T(8,128)(2,1)} %copy-done, bf16[16,64,64,128]{3,2,1,0:T(8,128)(2,1)} %copy-done, bf16[16,64,64,128]{3,2,1,0:T(8,128)(2,1)} %copy-done, ...), custom_call_target="tpu_custom_call" | custom-call | flops 10737418240 | bytes 25165824 | tf_op jit(solution)/shard_map/pallas_call | solution.py:180
  474.0 37.6 %all-to-all-start.2 = ((bf16[16,4,64,512]{3,2,1,0:T(8,128)(2,1)}), bf16[16,4,64,512]{3,2,1,0:T(8,128)(2,1)}, u32[]{:S(2)}, u32[]{:S(2)}) async-start(bf16[16,4,64,512]{3,2,1,0:T(8,128)(2,1)} %bitcast.78), calls=%async_computation.2 | async-start | bytes 8388608 | tf_op jit(solution)/shard_map/all_to_all | solution.py:376
  511.6 18.9 %shard_map.66 = (bf16[64,64,512]{2,1,0:T(8,128)(2,1)S(1)}, bf16[64,64,512]{2,1,0:T(8,128)(2,1)}, bf16[64,64,512]{2,1,0:T(8,128)(2,1)}) custom-call(s32[8]{0:T(128)S(1)} %broadcast_select_fusion.ids_ref, bf16[16,64,64,128]{3,2,1,0:T(8,128)(2,1)} %copy-done, bf16[16,64,64,128]{3,2,1,0:T(8,128)(2,1)} %copy-done, bf16[16,64,64,128]{3,2,1,0:T(8,128)(2,1)} %copy-done, ...), custom_call_target="tpu_custom_call" | custom-call | flops 10737418240 | bytes 25165824 | tf_op jit(solution)/shard_map/pallas_call | solution.py:180
  532.5 29.0 %all-to-all-done.2.refs_1_ = bf16[16,4,64,512]{3,2,1,0:T(8,128)(2,1)} async-done(((bf16[16,4,64,512]{3,2,1,0:T(8,128)(2,1)}), bf16[16,4,64,512]{3,2,1,0:T(8,128)(2,1)}, u32[]{:S(2)}, u32[]{:S(2)}) %all-to-all-start.2) | async-done | bytes 4194336 | tf_op jit(solution)/shard_map/all_to_all | solution.py:376
  561.5 60.2 %all_to_all.60.refs_0_ = bf16[16,4,64,512]{3,2,1,0:T(8,128)(2,1)S(1)} all-to-all(bf16[16,4,64,512]{3,2,1,0:T(8,128)(2,1)} %bitcast.79), channel_id=1, replica_groups=mesh['core'=2,'half'=2,'inner'=8] {'core','inner'}, dimensions={0} | all-to-all | bytes 8388608 | tf_op jit(solution)/shard_map/all_to_all | solution.py:376
  621.7 52.1 %all_to_all.61.left_ref = bf16[16,4,64,512]{3,2,1,0:T(8,128)(2,1)S(1)} all-to-all(bf16[16,4,64,512]{3,2,1,0:T(8,128)(2,1)S(1)} %bitcast.69), channel_id=1, replica_groups=mesh['core'=2,'half'=2,'inner'=8] {'core','inner'}, dimensions={0} | all-to-all | bytes 8388608 | tf_op jit(solution)/shard_map/all_to_all | solution.py:376
  673.8 7.0 shard_map.68
  680.9 52.8 %all_to_all.62 = bf16[16,4,64,512]{3,2,1,0:T(8,128)(2,1)} all-to-all(bf16[16,4,64,512]{3,2,1,0:T(8,128)(2,1)S(1)} %shard_map.68), channel_id=1, replica_groups=mesh['core'=2,'half'=2,'inner'=8] {'core','inner'}, dimensions={0} | all-to-all | bytes 8388608 | tf_op jit(solution)/shard_map/all_to_all | solution.py:376
  733.7 4.5 all-to-all-start.6
  738.2 25.3 %shard_map.69 = (bf16[64,64,512]{2,1,0:T(8,128)(2,1)S(1)}, bf16[64,64,512]{2,1,0:T(8,128)(2,1)}, bf16[64,64,512]{2,1,0:T(8,128)(2,1)}, bf16[64,64,512]{2,1,0:T(8,128)(2,1)}) custom-call(s32[8]{0:T(128)S(1)} %broadcast_select_fusion.ids_ref, bf16[16,64,64,128]{3,2,1,0:T(8,128)(2,1)} %copy-done, bf16[16,64,64,128]{3,2,1,0:T(8,128)(2,1)} %copy-done, ...), custom_call_target="tpu_custom_call" | custom-call | flops 12884901888 | bytes 33554432 | tf_op jit(solution)/shard_map/pallas_call | solution.py:180
  765.4 22.4 %all-to-all-done.6.left_ref = bf16[16,4,64,512]{3,2,1,0:T(8,128)(2,1)} async-done(((bf16[16,4,64,512]{3,2,1,0:T(8,128)(2,1)}), bf16[16,4,64,512]{3,2,1,0:T(8,128)(2,1)}, u32[]{:S(2)}, u32[]{:S(2)}) %all-to-all-start.6) | async-done | bytes 4194336 | tf_op jit(solution)/shard_map/all_to_all | solution.py:376
  787.9 11.0 all-to-all-start.4
  801.1 7.2 shard_map.70
  810.4 38.5 %all-to-all-done.4.left_ref = bf16[16,4,64,512]{3,2,1,0:T(8,128)(2,1)} async-done(((bf16[16,4,64,512]{3,2,1,0:T(8,128)(2,1)}), bf16[16,4,64,512]{3,2,1,0:T(8,128)(2,1)}, u32[]{:S(2)}, u32[]{:S(2)}) %all-to-all-start.4) | async-done | bytes 4194336 | tf_op jit(solution)/shard_map/all_to_all | solution.py:376
  848.9 60.1 %all_to_all.63 = bf16[16,4,64,512]{3,2,1,0:T(8,128)(2,1)} all-to-all(bf16[16,4,64,512]{3,2,1,0:T(8,128)(2,1)} %copy-done.4), channel_id=1, replica_groups=mesh['core'=2,'half'=2,'inner'=8] {'core','inner'}, dimensions={0} | all-to-all | bytes 8388608 | tf_op jit(solution)/shard_map/all_to_all | solution.py:376
  909.0 4.5 all-to-all-start.5
  913.5 25.3 %shard_map.71 = (bf16[64,64,512]{2,1,0:T(8,128)(2,1)S(1)}, bf16[64,64,512]{2,1,0:T(8,128)(2,1)}, bf16[64,64,512]{2,1,0:T(8,128)(2,1)}, bf16[64,64,512]{2,1,0:T(8,128)(2,1)}) custom-call(s32[8]{0:T(128)S(1)} %broadcast_select_fusion.ids_ref, bf16[16,64,64,128]{3,2,1,0:T(8,128)(2,1)} %copy-done, bf16[16,64,64,128]{3,2,1,0:T(8,128)(2,1)} %copy-done, ...), custom_call_target="tpu_custom_call" | custom-call | flops 12884901888 | bytes 33554432 | tf_op jit(solution)/shard_map/pallas_call | solution.py:180
  940.8 22.4 %all-to-all-done.5.refs_0_ = bf16[16,4,64,512]{3,2,1,0:T(8,128)(2,1)} async-done(((bf16[16,4,64,512]{3,2,1,0:T(8,128)(2,1)}), bf16[16,4,64,512]{3,2,1,0:T(8,128)(2,1)}, u32[]{:S(2)}, u32[]{:S(2)}) %all-to-all-start.5) | async-done | bytes 4194336 | tf_op jit(solution)/shard_map/all_to_all | solution.py:376
  963.1 60.4 %all_to_all.64.refs_1_ = bf16[16,4,64,512]{3,2,1,0:T(8,128)(2,1)S(1)} all-to-all(bf16[16,4,64,512]{3,2,1,0:T(8,128)(2,1)} %bitcast.77), channel_id=1, replica_groups=mesh['core'=2,'half'=2,'inner'=8] {'core','inner'}, dimensions={0} | all-to-all | bytes 8388608 | tf_op jit(solution)/shard_map/all_to_all | solution.py:376
  1023.6 7.2 shard_map.72
  1030.8 53.1 %all_to_all.65 = bf16[16,4,64,512]{3,2,1,0:T(8,128)(2,1)} all-to-all(bf16[16,4,64,512]{3,2,1,0:T(8,128)(2,1)S(1)} %shard_map.72), channel_id=1, replica_groups=mesh['core'=2,'half'=2,'inner'=8] {'core','inner'}, dimensions={0} | all-to-all | bytes 8388608 | tf_op jit(solution)/shard_map/all_to_all | solution.py:376
  1083.9 52.1 %all_to_all.66.left_ref = bf16[16,4,64,512]{3,2,1,0:T(8,128)(2,1)S(1)} all-to-all(bf16[16,4,64,512]{3,2,1,0:T(8,128)(2,1)S(1)} %bitcast.76), channel_id=1, replica_groups=mesh['core'=2,'half'=2,'inner'=8] {'core','inner'}, dimensions={0} | all-to-all | bytes 8388608 | tf_op jit(solution)/shard_map/all_to_all | solution.py:376
  1136.0 7.0 shard_map.74
  1144.9 4.5 all-to-all-start.11
  1149.4 12.4 shard_map.73
  1163.3 70.1 %all-to-all-done.11 = bf16[16,4,64,512]{3,2,1,0:T(8,128)(2,1)} async-done(((bf16[16,4,64,512]{3,2,1,0:T(8,128)(2,1)}), bf16[16,4,64,512]{3,2,1,0:T(8,128)(2,1)}, u32[]{:S(2)}, u32[]{:S(2)}) %all-to-all-start.11) | async-done | bytes 4194336 | tf_op jit(solution)/shard_map/all_to_all | solution.py:376
  1233.5 11.1 shard_map.75
  1245.9 57.7 %collective-permute-done.1 = bf16[64,64,512]{2,1,0:T(8,128)(2,1)} collective-permute-done((bf16[64,64,512]{2,1,0:T(8,128)(2,1)}, bf16[64,64,512]{2,1,0:T(8,128)(2,1)}, u32[]{:S(2)}, u32[]{:S(2)}) %collective-permute-start.1) | collective-permute-done | bytes 4194336 | tf_op jit(solution)/shard_map/ppermute | solution.py:382
  1303.6 7.4 maximum_convert_fusion.1.refs_0_
  1310.9 3.3 collective-permute-start.3
  1314.2 34.2 %collective-permute-done.2 = bf16[64,64,512]{2,1,0:T(8,128)(2,1)S(1)} collective-permute-done((bf16[64,64,512]{2,1,0:T(8,128)(2,1)S(1)}, bf16[64,64,512]{2,1,0:T(8,128)(2,1)S(1)}, u32[]{:S(2)}, u32[]{:S(2)}) %collective-permute-start.2) | collective-permute-done | bytes 4194336 | tf_op jit(solution)/shard_map/ppermute | solution.py:382
  1348.4 3.7 maximum_convert_fusion.refs_1_
  1352.1 3.2 collective-permute-start.4
  1355.3 5.2 collective-permute-done.4.refs_3_
  1360.5 16.9 %shard_map.76 = bf16[128,64,1024]{2,1,0:T(8,128)(2,1)} custom-call(s32[1]{0:T(128)} %bitcast.home_ref, bf16[64,64,512]{2,1,0:T(8,128)(2,1)} %maximum_convert_fusion.1.refs_0_, bf16[64,64,512]{2,1,0:T(8,128)(2,1)} %maximum_convert_fusion.refs_1_, bf16[64,64,512]{2,1,0:T(8,128)(2,1)} %collective-permute-done.3.refs_2_, ...), custom_call_target="tpu_custom_call" | custom-call | flops 8589934592 | bytes 33554432 | tf_op jit(solution)/shard_map/pallas_call | solution.py:180
  (42 shorter events, 20.6 us)
Async XLA Ops:
  0.0 447.1 %collective-permute-start = (s32[8]{0:T(128)}, s32[8]{0:T(128)S(1)}, u32[]{:S(2)}, u32[]{:S(2)}) collective-permute-start(s32[8]{0:T(128)} %bitcast.80), channel_id=1, source_target_pairs={{0,16},{16,0},{1,17},{17,1},{2,18},{18,2},{3,19},{19,3},{4,20},{20... | collective-permute-start | bytes 104 | tf_op jit(solution)/shard_map/ppermute | solution.py:400
  55.5 385.9 %copy-start.10 = (bf16[2,64,320]{2,1,0:T(8,128)(2,1)S(1)}, bf16[2,64,320]{2,1,0:T(8,128)(2,1)}, u32[]{:S(2)}) copy-start(bf16[2,64,320]{2,1,0:T(8,128)(2,1)} %proj_ref.1) | copy-start | bytes 245764
  55.5 385.9 %copy-start.11 = (bf16[2,64,64]{2,1,0:T(8,128)(2,1)S(1)}, bf16[2,64,64]{2,1,0:T(8,128)(2,1)}, u32[]{:S(2)}) copy-start(bf16[2,64,64]{2,1,0:T(8,128)(2,1)} %out_ref.1) | copy-start | bytes 49156
  55.5 385.9 %copy-start.12 = (bf16[64,128]{1,0:T(8,128)(2,1)S(1)}, bf16[64,128]{1,0:T(8,128)(2,1)}, u32[]{:S(2)}) copy-start(bf16[64,128]{1,0:T(8,128)(2,1)} %final_ref.1) | copy-start | bytes 49156
  55.5 391.6 %copy-start.14 = (s32[1,8]{1,0:T(1,128)S(1)}, s32[1,8]{1,0:T(1,128)}, u32[]{:S(2)}) copy-start(s32[1,8]{1,0:T(1,128)} %param.7) | copy-start | bytes 100
  435.2 6.2 copy-start
  471.9 2.1 copy-start.7
  474.0 87.5 %all-to-all-start.2 = ((bf16[16,4,64,512]{3,2,1,0:T(8,128)(2,1)}), bf16[16,4,64,512]{3,2,1,0:T(8,128)(2,1)}, u32[]{:S(2)}, u32[]{:S(2)}) async-start(bf16[16,4,64,512]{3,2,1,0:T(8,128)(2,1)} %bitcast.78), calls=%async_computation.2 | async-start | bytes 8388608 | tf_op jit(solution)/shard_map/all_to_all | solution.py:376
  530.5 1.9 copy-start.8
  561.5 60.2 %copy-start.9 = (bf16[64,64,512]{2,1,0:T(8,128)(2,1)S(1)}, bf16[64,64,512]{2,1,0:T(8,128)(2,1)}, u32[]{:S(2)}) copy-start(bf16[64,64,512]{2,1,0:T(8,128)(2,1)} %copy-done.8) | copy-start | bytes 12582916
  621.7 52.1 %copy-start.1 = (bf16[16,4,64,512]{3,2,1,0:T(8,128)(2,1)}, bf16[16,4,64,512]{3,2,1,0:T(8,128)(2,1)S(1)}, u32[]{:S(2)}) copy-start(bf16[16,4,64,512]{3,2,1,0:T(8,128)(2,1)S(1)} %all_to_all.60.refs_0_) | copy-start | bytes 12582916
  733.7 54.2 %all-to-all-start.6 = ((bf16[16,4,64,512]{3,2,1,0:T(8,128)(2,1)}), bf16[16,4,64,512]{3,2,1,0:T(8,128)(2,1)}, u32[]{:S(2)}, u32[]{:S(2)}) async-start(bf16[16,4,64,512]{3,2,1,0:T(8,128)(2,1)} %bitcast.68), calls=%async_computation.6 | async-start | bytes 8388608 | tf_op jit(solution)/shard_map/all_to_all | solution.py:376
  763.5 2.0 copy-start.5
  787.9 61.0 %all-to-all-start.4 = ((bf16[16,4,64,512]{3,2,1,0:T(8,128)(2,1)}), bf16[16,4,64,512]{3,2,1,0:T(8,128)(2,1)}, u32[]{:S(2)}, u32[]{:S(2)}) async-start(bf16[16,4,64,512]{3,2,1,0:T(8,128)(2,1)} %bitcast.75), calls=%async_computation.4 | async-start | bytes 8388608 | tf_op jit(solution)/shard_map/all_to_all | solution.py:376
  798.9 2.2 copy-start.2
  808.3 2.0 copy-start.4
  909.0 54.2 %all-to-all-start.5 = ((bf16[16,4,64,512]{3,2,1,0:T(8,128)(2,1)}), bf16[16,4,64,512]{3,2,1,0:T(8,128)(2,1)}, u32[]{:S(2)}, u32[]{:S(2)}) async-start(bf16[16,4,64,512]{3,2,1,0:T(8,128)(2,1)} %bitcast.74), calls=%async_computation.5 | async-start | bytes 8388608 | tf_op jit(solution)/shard_map/all_to_all | solution.py:376
  938.8 2.0 copy-start.6
  1030.8 53.1 %copy-start.13 = (bf16[64,64,512]{2,1,0:T(8,128)(2,1)S(1)}, bf16[64,64,512]{2,1,0:T(8,128)(2,1)}, u32[]{:S(2)}) copy-start(bf16[64,64,512]{2,1,0:T(8,128)(2,1)} %get-tuple-element.39) | copy-start | bytes 12582916
  1143.0 1.9 copy-start.3
  1144.9 88.6 %all-to-all-start.11 = ((bf16[16,4,64,512]{3,2,1,0:T(8,128)(2,1)}), bf16[16,4,64,512]{3,2,1,0:T(8,128)(2,1)}, u32[]{:S(2)}, u32[]{:S(2)}) async-start(bf16[16,4,64,512]{3,2,1,0:T(8,128)(2,1)} %copy-done.3), calls=%async_computation.11 | async-start | bytes 8388608 | tf_op jit(solution)/shard_map/all_to_all | solution.py:376
  1161.8 141.8 %collective-permute-start.1 = (bf16[64,64,512]{2,1,0:T(8,128)(2,1)}, bf16[64,64,512]{2,1,0:T(8,128)(2,1)}, u32[]{:S(2)}, u32[]{:S(2)}) collective-permute-start(bf16[64,64,512]{2,1,0:T(8,128)(2,1)} %shard_map.73), channel_id=1, source_target_pairs={{8,0},{16,24},{9,1},{17,25},{10,2},{18,26},{11,3},{19,27},{12,4},{... | collective-permute-start | bytes 12582920 | tf_op jit(solution)/shard_map/ppermute | solution.py:382
  1244.6 103.8 %collective-permute-start.2 = (bf16[64,64,512]{2,1,0:T(8,128)(2,1)S(1)}, bf16[64,64,512]{2,1,0:T(8,128)(2,1)S(1)}, u32[]{:S(2)}, u32[]{:S(2)}) collective-permute-start(bf16[64,64,512]{2,1,0:T(8,128)(2,1)S(1)} %shard_map.75), channel_id=1, source_target_pairs={{8,0},{16,24},{9,1},{17,25},{10,2},{18,26},{11,3},{19,27},{12,4},{... | collective-permute-start | bytes 12582920 | tf_op jit(solution)/shard_map/ppermute | solution.py:382
  1310.9 44.4 %collective-permute-start.3 = (bf16[64,64,512]{2,1,0:T(8,128)(2,1)}, bf16[64,64,512]{2,1,0:T(8,128)(2,1)}, u32[]{:S(2)}, u32[]{:S(2)}) collective-permute-start(bf16[64,64,512]{2,1,0:T(8,128)(2,1)} %maximum_convert_fusion.1.refs_0_), channel_id=1, source_target_pairs={{0,16},{24,8},{1,17},{25,9},{2,18},{26,10},{3,19},{27,11},{4,20},{... | collective-permute-start | bytes 12582920 | tf_op jit(solution)/shard_map/ppermute | solution.py:382
  1352.1 8.4 collective-permute-start.4

commit v3 on v2

--- a/solution.py
+++ b/solution.py
@@ -32,6 +32,8 @@
 SPLIT = 2
 SUB = 8
 PARTS = 2
+COLUMN_PARTS = 2
+LEFT_PARTS = 1
 
 
 def widened(weight, source):
@@ -89,45 +91,69 @@
     ).reshape(weight.shape[0] // sub, sub, lanes)
 
 
-def project(values, wide_ref, mask_ref, left_ref, right_ref, gate_ref):
+def project(values, wide_ref, mask_ref, store):
     normed = channel_norm(values)
     mask = mask_ref[...][None]
     size = CH // PARTS
     for part in range(PARTS):
         projected = flat_dot(wide_ref[part], normed)
-        piece = slice(part * size, (part + 1) * size)
         left = sigmoid(projected[:size]) * projected[size : 2 * size] * mask
-        left_ref[piece] = left.astype(left_ref.dtype)
         right = sigmoid(projected[2 * size : 3 * size]) * projected[3 * size : 4 * size] * mask
-        right_ref[piece] = right.astype(right_ref.dtype)
-        gate_ref[piece] = sigmoid(projected[4 * size :]).astype(gate_ref.dtype)
-
-
-def updated(values, back_ref, gate_ref, out_ref):
+        gate = sigmoid(projected[4 * size :])
+        pieces = [item.astype(jnp.bfloat16) for item in (left, right, gate)]
+        store(slice(part * size, (part + 1) * size), *pieces)
+
+
+def updated(values, back_ref, gate, out_ref):
     normed = channel_norm(back_ref[...].astype(jnp.float32))
     update = flat_dot(out_ref[...], normed)
-    pair = values + gate_ref[...].astype(jnp.float32) * update
-    return pair.astype(jnp.bfloat16)
+    return (values + gate * update).astype(jnp.bfloat16)
 
 
 def tiles_of(refs):
     return jnp.concatenate([ref[...].astype(jnp.float32) for ref in refs], axis=-1)
 
 
-def first_kernel(tiles, ids_ref, *refs):
-    project(tiles_of(refs[:tiles]), *refs[tiles:])
-
-
-def middle_kernel(tiles, ids_ref, *refs):
-    back_ref, gate_ref, out_ref, wide_ref, mask_ref = refs[tiles : tiles + 5]
-    pair_ref, left_ref, right_ref, next_ref = refs[tiles + 5 :]
-    pair = updated(tiles_of(refs[:tiles]), back_ref, gate_ref, out_ref)
+def first_kernel(per, ids_ref, *refs):
+    wide_ref, mask_ref, both_ref, gate_ref = refs[per:]
+    _, _, group, sub, lanes = both_ref.shape
+
+    def store(piece, left, right, gate):
+        place = slice(piece.start // group, piece.stop // group)
+        both_ref[place, 0] = left.reshape(-1, group, sub, lanes)
+        both_ref[place, 1] = right.reshape(-1, group, sub, lanes)
+        gate_ref[piece] = gate
+
+    project(tiles_of(refs[:per]), wide_ref, mask_ref, store)
+
+
+def middle_kernel(parts, per, count, ids_ref, *refs):
+    tiles, refs = refs[: parts * per], refs[parts * per :]
+    gates, refs = refs[:parts], refs[parts:]
+    back_ref, out_ref, wide_ref, mask_ref, pair_ref, right_ref, next_ref = refs[:7]
+    left_refs = refs[7:]
+
+    def store(piece, left, right, gate):
+        right_ref[piece] = right
+        next_ref[piece] = gate
+        for number, left_ref in enumerate(left_refs):
+            lanes = left_ref.shape[-1]
+            left_ref[piece] = left[:, :, number * lanes : (number + 1) * lanes]
+
+    values = tiles_of(tiles[:per])
+    gate = gates[0][...].astype(jnp.float32)
+    for part in range(1, parts):
+        reached = pl.program_id(0) >= part * count
+        values = jnp.where(reached, tiles_of(tiles[part * per : (part + 1) * per]), values)
+        gate = jnp.where(reached, gates[part][...].astype(jnp.float32), gate)
+    pair = updated(values, back_ref, gate, out_ref)
     pair_ref[...] = pair
-    project(pair.astype(jnp.float32), wide_ref, mask_ref, left_ref, right_ref, next_ref)
+    project(pair.astype(jnp.float32), wide_ref, mask_ref, store)
 
 
 def last_kernel(pair_ref, back_ref, gate_ref, out_ref, final_ref):
-    pair = updated(pair_ref[...].astype(jnp.float32), back_ref, gate_ref, out_ref)
+    gate = gate_ref[...].astype(jnp.float32)
+    pair = updated(pair_ref[...].astype(jnp.float32), back_ref, gate, out_ref)
     final_ref[...] = channel_norm(pair.astype(jnp.float32)).astype(final_ref.dtype)
 
 
@@ -164,14 +190,19 @@
     return pl.BlockSpec((None, *shape[1:]), lambda w, *_: (layer,) + (0,) * (len(shape) - 1))
 
 
-def tile_specs(got, number, per):
+def tile_specs(got, per, place):
     def at(tile):
-        return pl.BlockSpec(
-            (None, got.shape[1], SUB, got.shape[3]),
-            lambda w, ids: (ids[number * per + tile], 0, w, 0),
-        )
+        def index(*position):
+            number, column = place(*position[:-1])
+            return position[-1][number * per + tile], 0, column, 0
+
+        return pl.BlockSpec((None, got.shape[1], SUB, got.shape[3]), index)
 
     return [at(tile) for tile in range(per)]
+
+
+def part_column(part, count):
+    return lambda w: jnp.clip(w - part * count, 0, count - 1)
 
 
 def stage(kernel, specs, out_shapes, ids, operands, flops):
@@ -191,48 +222,85 @@
     )(ids, *operands)
 
 
-def first_stage(number, per, ids, got, wide, mask):
-    _, channels, width, tile = got.shape
-    shape = jax.ShapeDtypeStruct((channels, width, per * tile), got.dtype)
-    specs = tile_specs(got, number, per) + [
-        layer_of(wide.shape, 0),
-        pl.BlockSpec((SUB, per * tile), lambda w, *_: (w, 0)),
+def first_stage(part, ids, got, wide, mask):
+    targets, channels, width, tile = got.shape
+    per = ids.shape[0] // SPLIT
+    lanes = per * tile
+    count = width // SUB
+    group = channels // targets
+    specs = tile_specs(got, per, lambda n, w: (n, w)) + [
+        pl.BlockSpec((None, *wide.shape[1:]), lambda n, w, _: (0, 0, 0, 0)),
+        pl.BlockSpec((SUB, lanes), lambda n, w, _: (part * count + w, n)),
     ]
-    kernel = functools.partial(first_kernel, per)
-    flops = 2 * wide.size // NLAYER * width // SUB * per * tile
-    return stage(kernel, specs, [shape] * 3, ids, [got] * per + [wide, mask], flops)
-
-
-def middle_stage(layer, number, per, ids, got, back, gate, out_wide, wide, mask):
-    _, channels, width, tile = got.shape
-    shape = jax.ShapeDtypeStruct((channels, width, per * tile), got.dtype)
-    specs = tile_specs(got, number, per) + [
+    return pl.pallas_call(
+        functools.partial(first_kernel, per),
+        grid_spec=pltpu.PrefetchScalarGridSpec(
+            num_scalar_prefetch=1,
+            grid=(SPLIT, count),
+            in_specs=specs,
+            out_specs=[
+                pl.BlockSpec((targets, 2, group, SUB, lanes), lambda n, w, _: (0, 0, 0, w, n)),
+                pl.BlockSpec((channels, SUB, lanes), lambda n, w, _: (0, w, n)),
+            ],
+        ),
+        out_shape=[
+            jax.ShapeDtypeStruct((targets, 2, group, width, SPLIT * lanes), got.dtype),
+            jax.ShapeDtypeStruct((channels, width, SPLIT * lanes), got.dtype),
+        ],
+        compiler_params=PARAMS,
+        cost_estimate=cost(
+            2 * wide.size // NLAYER * count * SPLIT * lanes, 8 * channels * width * SPLIT * lanes
+        ),
+    )(ids, *[got] * per, wide, mask)
+
+
+def middle_stage(layer, number, ids, gots, back, gates, out_wide, wide, mask):
+    _, channels, width, tile = gots[0].shape
+    per = ids.shape[0] // SPLIT
+    lanes = per * tile
+    count = width // SUB
+    shape = jax.ShapeDtypeStruct((channels, width * len(gots), lanes), back.dtype)
+    specs, operands = [], []
+    for part, got in enumerate(gots):
+        column = part_column(part, count)
+        specs += tile_specs(got, per, lambda w, column=column: (number, column(w)))
+        operands += [got] * per
+    for part, gate in enumerate(gates):
+        column = part_column(part, count)
+        specs.append(
+            pl.BlockSpec(
+                (channels, SUB, lanes), lambda w, _, column=column: (0, column(w), number)
+            )
+        )
+        operands.append(gate)
+    specs += [
         by_columns(back.shape),
-        by_columns(gate.shape),
         layer_of(out_wide.shape, layer),
         layer_of(wide.shape, layer + 1),
-        pl.BlockSpec((SUB, per * tile), lambda w, *_: (w, 0)),
+        pl.BlockSpec((SUB, lanes), lambda w, _: (w, number)),
     ]
-    kernel = functools.partial(middle_kernel, per)
-    flops = 2 * (wide.size + out_wide.size) // NLAYER * width // SUB * per * tile
-    operands = [got] * per + [back, gate, out_wide, wide, mask]
-    return stage(kernel, specs, [shape] * 4, ids, operands, flops)
-
-
-def last_stage(layer, pair, back, gate, out_wide):
+    operands += [back, out_wide, wide, mask]
+    kernel = functools.partial(middle_kernel, len(gots), per, count)
+    flops = 2 * (wide.size + out_wide.size) // NLAYER * count * len(gots) * lanes
+    left = jax.ShapeDtypeStruct((*shape.shape[:2], lanes // LEFT_PARTS), back.dtype)
+    return stage(kernel, specs, [shape] * 3 + [left] * LEFT_PARTS, ids, operands, flops)
+
+
+def last_stage(layer, piece, pair, back, gate, out_wide):
+    block = pl.BlockSpec((back.shape[0], SUB, back.shape[2]), lambda w: (0, w, piece))
     return pl.pallas_call(
         last_kernel,
-        grid=(pair.shape[1] // SUB,),
-        in_specs=[by_columns(pair.shape)] * 3 + [layer_of(out_wide.shape, layer)],
-        out_specs=by_columns(pair.shape),
-        out_shape=jax.ShapeDtypeStruct(pair.shape, pair.dtype),
+        grid=(back.shape[1] // SUB,),
+        in_specs=[block, by_columns(back.shape), block, layer_of(out_wide.shape, layer)],
+        out_specs=by_columns(back.shape),
+        out_shape=jax.ShapeDtypeStruct(back.shape, back.dtype),
         compiler_params=PARAMS,
-        cost_estimate=cost(out_wide.size * pair.size // CH // SUB, 8 * pair.size),
+        cost_estimate=cost(out_wide.size * back.size // CH // SUB, 8 * back.size),
     )(pair, back, gate, out_wide)
 
 
 def end_stage(home, hiddens, shareds, wide):
-    channels, width, lanes = hiddens[0].shape
+    _, width, lanes = hiddens[0].shape
     shape = (wide.shape[0] // SUB, width, lanes * len(hiddens))
     out = jax.ShapeDtypeStruct(shape, hiddens[0].dtype)
     specs = [by_columns(hiddens[0].shape)] * (2 * len(hiddens)) + [whole(wide.shape)]
@@ -240,41 +308,93 @@
     return stage(end_kernel, specs, [out], home, [*hiddens, *shareds, wide], flops)[0]
 
 
-def product_kernel(left_ref, *refs):
-    rights, out_ref = refs[:-1], refs[-1]
-    sources, _, width, chunk = left_ref.shape
-    left = left_ref[...].reshape(sources * width, chunk)
-    per = out_ref.shape[0] // len(rights)
-    for number, right_ref in enumerate(rights):
-        right = right_ref[...].reshape(sources * width, right_ref.shape[-1])
-        product = lax.dot_general(
+def product_kernel(axis, count, *refs):
+    lefts, rights, out_ref = refs[:count], refs[count:-1], refs[-1]
+    targets, _, width, chunk = out_ref.shape
+
+    def matrix(ref):
+        value = ref[...]
+        return value.reshape(value.shape[0] * value.shape[-2], value.shape[-1])
+
+    def times(left, right):
+        return lax.dot_general(
             right, left, (((0,), (0,)), ((), ())), preferred_element_type=jnp.float32
         )
-        out_ref[number * per : (number + 1) * per] = product.astype(out_ref.dtype).reshape(
+
+    if axis == "depth":
+        left = jnp.concatenate([matrix(ref) for ref in lefts], axis=0)
+        right = jnp.concatenate([matrix(ref) for ref in rights], axis=0)
+        pieces = [times(left, right)]
+    else:
+        pieces = [times(matrix(lefts[0]), matrix(right)) for right in rights]
+    per = targets // len(pieces)
+    for number, piece in enumerate(pieces):
+        out_ref[number * per : (number + 1) * per] = piece.astype(out_ref.dtype).reshape(
             per, 1, width, chunk
         )
 
 
-def channel_products(left, rights):
-    sources, channels, width, chunk = left.shape
-    spec = pl.BlockSpec((sources, 1, width, chunk), lambda c: (0, c, 0, 0))
-    depth = sources * width
+def product_call(axis, specs, operands, count, out):
+    targets, channels, width, chunk = out.shape
     return pl.pallas_call(
-        product_kernel,
+        functools.partial(product_kernel, axis, count),
         grid=(channels,),
-        in_specs=[spec] * (1 + len(rights)),
-        out_specs=spec,
-        out_shape=jax.ShapeDtypeStruct(left.shape, left.dtype),
-        compiler_params=pltpu.CompilerParams(vmem_limit_bytes=32 << 20),
-        cost_estimate=pl.CostEstimate(
-            flops=2 * channels * depth * depth * chunk,
-            bytes_accessed=2 * left.size * (2 + len(rights)),
-            transcendentals=0,
+        in_specs=specs,
+        out_specs=pl.BlockSpec((targets, 1, width, chunk), lambda c: (0, c, 0, 0)),
+        out_shape=out,
+        compiler_params=pltpu.CompilerParams(vmem_limit_bytes=40 << 20),
+        cost_estimate=cost(2 * out.size * targets * width, 8 * out.size),
+    )(*operands)
+
+
+def depth_products(number, boths, chunk):
+    targets, _, channels, width, lanes = boths[0].shape
+
+    def spec(side, size, place):
+        return pl.BlockSpec((targets, None, 1, width, size), lambda c: (0, side, c, 0, place))
+
+    out = jax.ShapeDtypeStruct((targets, channels, width * len(boths), chunk), boths[0].dtype)
+    specs = [spec(0, chunk, number)] * len(boths) + [spec(1, lanes, 0)] * len(boths)
+    return product_call("depth", specs, boths + boths, len(boths), out)
+
+
+def row_products(left, rights):
+    targets, _, width, _ = left.shape
+
+    def spec(array):
+        return pl.BlockSpec((targets, 1, width, array.shape[3]), lambda c: (0, c, 0, 0))
+
+    out = jax.ShapeDtypeStruct(left.shape, left.dtype)
+    specs = [spec(array) for array in (left, *rights)]
+    return product_call("rows", specs, [left, *rights], 1, out)
+
+
+def pack_kernel(ids_ref, rows_ref, packed_ref):
+    rows = rows_ref[...].astype(jnp.float32)
+    packed_ref[...] = jnp.swapaxes(jnp.swapaxes(rows, 0, 1), 1, 2).astype(packed_ref.dtype)
+
+
+def pack(ids, rows):
+    tile, channels, _ = rows.shape
+    slots = ids.shape[0]
+    group = 2 * SUB
+    out = jax.ShapeDtypeStruct((channels, slots * TILE, tile), rows.dtype)
+    return pl.pallas_call(
+        pack_kernel,
+        grid_spec=pltpu.PrefetchScalarGridSpec(
+            num_scalar_prefetch=1,
+            grid=(slots, channels // group),
+            in_specs=[pl.BlockSpec((tile, group, TILE), lambda s, c, ids: (0, c, ids[s]))],
+            out_specs=pl.BlockSpec((group, TILE, tile), lambda s, c, ids: (c, s, 0)),
         ),
-    )(left, *rights)
-
-
-def spread_kernel(send_ref, got_ref, hold, send_sem, recv_sem, hold_sem):
+        out_shape=out,
+        compiler_params=PARAMS,
+        cost_estimate=cost(0, 4 * out.size),
+    )(ids, rows)
+
+
+def spread_kernel(part, send_ref, got_ref, hold, send_sem, recv_sem, hold_sem):
+    columns = pl.ds(part * got_ref.shape[2], got_ref.shape[2])
     core, half, inner = (lax.axis_index(name) for name in ("core", "half", "inner"))
     cores, halves, width = (lax.axis_size(name) for name in ("core", "half", "inner"))
     blocks = cores * width
@@ -300,7 +420,7 @@
     def outgoing(step):
         block = lax.rem(mine + step, blocks)
         return pltpu.make_async_remote_copy(
-            src_ref=send_ref.at[:, block],
+            src_ref=send_ref.at[:, block, columns],
             dst_ref=got_ref.at[row],
             send_sem=send_sem.at[step],
             recv_sem=recv_sem.at[row],
@@ -314,7 +434,7 @@
 
     @pl.when(home)
     def _():
-        bring = pltpu.make_async_copy(send_ref.at[:, mine], hold, hold_sem.at[0])
+        bring = pltpu.make_async_copy(send_ref.at[:, mine, columns], hold, hold_sem.at[0])
         bring.start()
         bring.wait()
         put = pltpu.make_async_copy(hold, got_ref.at[row], hold_sem.at[1])
@@ -327,7 +447,7 @@
 
     def incoming(slot):
         return pltpu.make_async_remote_copy(
-            src_ref=send_ref.at[:, 0],
+            src_ref=send_ref.at[:, 0, columns],
             dst_ref=got_ref.at[slot],
             send_sem=send_sem.at[0],
             recv_sem=recv_sem.at[slot],
@@ -350,10 +470,11 @@
         incoming(row).wait_recv()
 
 
-def spread(send):
+def spread(send, part):
     channels, blocks, width, tile = send.shape
+    width = width // COLUMN_PARTS
     return pl.pallas_call(
-        spread_kernel,
+        functools.partial(spread_kernel, part),
         in_specs=[pl.BlockSpec(memory_space=pl.ANY)],
         out_specs=pl.BlockSpec(memory_space=pl.ANY),
         out_shape=jax.ShapeDtypeStruct((blocks, channels, width, tile), send.dtype),
@@ -364,8 +485,9 @@
             pltpu.SemaphoreType.DMA((2,)),
         ],
         compiler_params=pltpu.CompilerParams(
-            collective_id=0, has_side_effects=True, vmem_limit_bytes=32 << 20
+            collective_id=part, has_side_effects=True, vmem_limit_bytes=32 << 20
         ),
+        cost_estimate=cost(0, 64 * blocks * channels * width * tile),
     )(send)
 
 
@@ -393,9 +515,7 @@
     my_index = core * inner_count + inner
     col_width = CROP // row_count
     per_group = CH // row_count
-    tiles = CROP // TILE
     chunk = CROP // SPLIT
-    per = tiles // SPLIT
     held_ids = crop_tiles[0]
     other_ids = lax.ppermute(held_ids, "core", [(0, 1), (1, 0)])
     crop_ids = jnp.where(core == half, held_ids, other_ids)
@@ -404,46 +524,38 @@
     usable = (position < full_length[0]).astype(jnp.float32)
     col_usable = lax.dynamic_slice_in_dim(usable, my_index * col_width, col_width)
     pair_mask = col_usable[:, None] * usable[None, :]
-    masks = jnp.split(pair_mask, SPLIT, axis=1)
-    by_channel = jnp.transpose(pair_maps[0], (0, 2, 1))
-    columns = jnp.concatenate(
-        [
-            lax.dynamic_slice_in_dim(by_channel, held_ids[tile] * TILE, TILE, axis=2)
-            for tile in range(tiles)
-        ],
-        axis=2,
-    )
-    send = jnp.transpose(columns, (1, 2, 0)).reshape(CH, row_count, col_width, TILE)
-    got = spread(send)
+    send = pack(held_ids, jnp.transpose(pair_maps[0], (0, 2, 1)))
+    send = send.reshape(CH, row_count, col_width, TILE)
     wides, outs, final_wide = widen(proj_weight, out_weight, final_weight)
-    shape = (row_count, per_group, col_width, chunk)
-    ready = [
-        first_stage(number, per, crop_ids, got, wides, masks[number]) for number in range(SPLIT)
+    gots, gates, boths = [], [], []
+    for part in range(COLUMN_PARTS):
+        got = spread(send, part)
+        both, gate = first_stage(part, crop_ids, got, wides, pair_mask)
+        send = after(send, both)
+        gots.append(got)
+        gates.append(gate)
+        boths.append(exchange(both))
+    following = []
+    for number in range(SPLIT):
+        merged = exchange(depth_products(number, boths, chunk)).reshape(CH, col_width, chunk)
+        following.append(
+            middle_stage(0, number, crop_ids, gots, merged, gates, outs, wides, pair_mask)
+        )
+    rights = [
+        exchange(item[1].reshape(row_count, per_group, col_width, chunk)) for item in following
     ]
-    pairs = [None] * SPLIT
-    for layer in range(NLAYER):
-        lefts = [item[0].reshape(shape) for item in ready]
-        rights = [exchange(item[1].reshape(shape)) for item in ready]
-        gates = [item[2] for item in ready]
-        following = []
-        back = None
-        for number in range(SPLIT):
-            left = lefts[number] if back is None else after(lefts[number], back)
-            back = exchange(channel_products(exchange(left), rights))
-            merged = back.reshape(CH, col_width, chunk)
-            if layer + 1 < NLAYER:
-                pair, left, right, gate = middle_stage(
-                    layer, number, per, crop_ids, got, merged, gates[number], outs, wides,
-                    masks[number],
-                )
-                pairs[number] = pair
-                following.append((left, right, gate))
-            else:
-                following.append(last_stage(layer, pairs[number], merged, gates[number], outs))
-        ready = following
+    ready, arrived = [], []
+    back = None
+    for pair, _, gate, *lefts in following:
+        for piece, left in enumerate(lefts):
+            left = left.reshape(row_count, per_group, col_width, chunk // LEFT_PARTS)
+            left = exchange(left if back is None else after(left, back, ready[-1]))
+            back = exchange(row_products(left, rights))
+            merged = back.reshape(CH, col_width, chunk // LEFT_PARTS)
+            ready.append(last_stage(NLAYER - 1, piece, pair, merged, gate, outs))
+            arrived.append(moved(ready[-1], [((0, 1), (0, 0)), ((1, 0), (1, 1))]))
     hiddens, shareds = [], []
-    for normed_final in ready:
-        across = moved(normed_final, [((0, 1), (0, 0)), ((1, 0), (1, 1))])
+    for normed_final, across in zip(ready, arrived):
         summed = normed_final.astype(jnp.float32) + across.astype(jnp.float32)
         hiddens.append(jnp.maximum(summed / halves, 0.0).astype(jnp.bfloat16))
         shareds.append(moved(hiddens[-1], [((0, 0), (1, 0)), ((1, 1), (0, 1))]))

time: 1380 us -> 1330 us (0.964)
  Pallas kernels: 543 us -> 622 us
  local copies, waits for them, and re-layouts: 70.3 us -> 22.1 us
  blocking collectives: 391 us -> 344 us
  waiting for transfers between devices: 280 us -> 260 us
    pallas_call x7 -> x11, Pallas kernels: 432 us -> 545 us  [the longest x2 426 us: spread(): pl.pallas_call(functools.partial(spread_kernel, part), in_specs=[pl.Block...]
    all_to_all x7 -> x5, blocking collectives: 391 us -> 344 us  [exchange(): return lax.all_to_all(value, GROUP, split_axis=0, concat_axis=0, tiled=True)]
    pallas_call x5 -> x3, Pallas kernels: 105 us -> 71.1 us  [stage(): pl.pallas_call(kernel, grid_spec=pltpu.PrefetchScalarGridSpec(num_scalar_...]
    transpose x1 -> x0, local copies, waits for them, and re-layouts: 23 us -> none  [in_halves(): jnp.transpose(columns, (1, 2, 0)).reshape(CH, row_count, col_width, TILE)]
    unnamed x37 -> x36, local copies, waits for them, and re-layouts: 41.8 us -> 21.3 us
  transfers between devices with their start and end apart: 10 -> 10, of which waited for: 8 -> 6; matrix products, arithmetic and copies ran while one was open for 4% -> 1% of each run, Pallas kernels for 35% -> 42%
where the time goes in v3:
time: 1330 us; the launch traced here: 1320 us
  Pallas kernels  622 us (47%)
  blocking collectives  344 us (26%)
  waiting for transfers between devices  260 us (20%)
  starting transfers between devices  60.4 us (5%)
  local copies, waits for them, and re-layouts  22.1 us (2%)
  other arithmetic  15.1 us (1%)
    pallas_call x2, Pallas kernels, spread(): pl.pallas_call(functools.partial(spread_kernel, part), in_specs=[pl.Block...  426 us
    all_to_all x5, blocking collectives, exchange(): return lax.all_to_all(value, GROUP, split_axis=0, concat_axis=0, tiled=True)  344 us
    all_to_all x5, waiting for transfers between devices, exchange(): return lax.all_to_all(value, GROUP, split_axis=0, concat_axis=0, tiled=True)  172 us
    ppermute x4, waiting for transfers between devices, moved(): return lax.ppermute(value, ('core', 'half'), steps)  88 us
    pallas_call x3, Pallas kernels, stage(): pl.pallas_call(kernel, grid_spec=pltpu.PrefetchScalarGridSpec(num_scalar_...  71.1 us
    all_to_all x5, starting transfers between devices, exchange(): return lax.all_to_all(value, GROUP, split_axis=0, concat_axis=0, tiled=True)  49.1 us
    pallas_call x2, Pallas kernels, first_stage(): pl.pallas_call(functools.partial(first_kernel, per), grid_spec=pltpu.Pref...  38 us
    pallas_call x4, Pallas kernels, product_call(): pl.pallas_call(functools.partial(product_kernel, axis, count), grid=(chan...  30 us
  transfers between devices with their start and end apart: 10, of which 6 were waited for; matrix products, arithmetic and copies ran while one was open for 1% of the time, Pallas kernels for 42%

profile of v3, /device:TPU:0, one launch (start us, length us, event | category | flops | bytes accessed | tf_op | source)
XLA Modules:
  0.0 1324.5 jit_solution(3317540667234815814)
XLA Ops:
  1.8 28.8 %shard_map.64 = bf16[64,1024,128]{2,1,0:T(8,128)(2,1)} custom-call(s32[8]{0:T(128)S(1)} %bitcast.27, bf16[128,64,2048]{2,1,0:T(8,128)(2,1)} %bitcast.30), custom_call_target="tpu_custom_call" | custom-call | bytes 33554432 | tf_op jit(solution)/shard_map/pallas_call | solution.py:382
  30.7 190.1 %shard_map.65.refs_0_.refs_1_.refs_2_.refs_3_ = bf16[16,64,32,128]{3,2,1,0:T(8,128)(2,1)S(1)} custom-call(bf16[64,16,64,128]{3,2,1,0:T(8,128)(2,1)} %bitcast.28), custom_call_target="tpu_custom_call" | custom-call | bytes 268435456 | tf_op jit(solution)/shard_map/pallas_call | solution.py:476
  220.8 3.3 copy-done
  224.1 5.7 shard_map.66
  229.8 0.7 fusion.6
  230.5 4.3 compare_select_fusion.1
  235.6 19.0 %shard_map.67 = (bf16[16,2,4,32,1024]{4,3,2,1,0:T(8,128)(2,1)}, bf16[64,32,1024]{2,1,0:T(8,128)(2,1)S(1)}) custom-call(s32[8]{0:T(128)S(1)} %broadcast_select_fusion.ids_ref, bf16[16,64,32,128]{3,2,1,0:T(8,128)(2,1)} %copy-done, bf16[16,64,32,128]{3,2,1,0:T(8,128)(2,1)} %copy-done, bf16[16,64,32,128]{3,2,1,0:T(8,128)(2,1)} %copy-done, ...), custom_call_target="tpu_custom_call" | custom-call | flops 10737418240 | bytes 16777216 | tf_op jit(solution)/shard_map/pallas_call | solution.py:235
  254.5 2.0 copy-done.2
  256.5 18.2 %all-to-all-start = ((bf16[16,2,4,32,1024]{4,3,2,1,0:T(8,128)(2,1)}), bf16[16,2,4,32,1024]{4,3,2,1,0:T(8,128)(2,1)}, u32[]{:S(2)}, u32[]{:S(2)}) async-start(bf16[16,2,4,32,1024]{4,3,2,1,0:T(8,128)(2,1)} %get-tuple-element.23), calls=%async_computation | async-start | bytes 16777216 | tf_op jit(solution)/shard_map/all_to_all | solution.py:498
  274.7 236.0 %shard_map.68.refs_0_.refs_1_.refs_2_.refs_3_.refs_4_.refs_5_.refs_6_.refs_7_ = bf16[16,64,32,128]{3,2,1,0:T(8,128)(2,1)S(1)} custom-call(bf16[64,16,64,128]{3,2,1,0:T(8,128)(2,1)} %bitcast.29), custom_call_target="tpu_custom_call" | custom-call | bytes 268435456 | tf_op jit(solution)/shard_map/pallas_call | solution.py:476
  510.7 3.4 copy-done.1
  514.1 19.0 %shard_map.69 = (bf16[16,2,4,32,1024]{4,3,2,1,0:T(8,128)(2,1)}, bf16[64,32,1024]{2,1,0:T(8,128)(2,1)S(1)}) custom-call(s32[8]{0:T(128)S(1)} %broadcast_select_fusion.ids_ref, bf16[16,64,32,128]{3,2,1,0:T(8,128)(2,1)} %copy-done.1, bf16[16,64,32,128]{3,2,1,0:T(8,128)(2,1)} %copy-done.1, bf16[16,64,32,128]{3,2,1,0:T(8,128)(2,1)} %copy-done.1, ...), custom_call_target="tpu_custom_call" | custom-call | flops 10737418240 | bytes 16777216 | tf_op jit(solution)/shard_map/pallas_call | solution.py:235
  533.1 2.1 copy-done.3
  535.2 126.6 %all_to_all.50.refs_1_.refs_3_ = bf16[16,2,4,32,1024]{4,3,2,1,0:T(8,128)(2,1)} all-to-all(bf16[16,2,4,32,1024]{4,3,2,1,0:T(8,128)(2,1)} %get-tuple-element.27), channel_id=1, replica_groups=mesh['core'=2,'half'=2,'inner'=8] {'core','inner'}, dimensions={0} | all-to-all | bytes 16777216 | tf_op jit(solution)/shard_map/all_to_all | solution.py:498
  661.8 7.9 shard_map.72
  669.7 2.0 copy-done.7
  671.7 4.7 all-to-all-start.5
  676.5 8.0 shard_map.70
  684.5 2.0 copy-done.6
  686.5 39.6 %all-to-all-done.5 = bf16[16,4,64,512]{3,2,1,0:T(8,128)(2,1)} async-done(((bf16[16,4,64,512]{3,2,1,0:T(8,128)(2,1)}), bf16[16,4,64,512]{3,2,1,0:T(8,128)(2,1)}, u32[]{:S(2)}, u32[]{:S(2)}) %all-to-all-start.5) | async-done | bytes 4194336 | tf_op jit(solution)/shard_map/all_to_all | solution.py:498
  726.1 11.0 all-to-all-start.2
  737.1 27.1 %shard_map.73 = (bf16[64,64,512]{2,1,0:T(8,128)(2,1)S(1)}, bf16[64,64,512]{2,1,0:T(8,128)(2,1)}, bf16[64,64,512]{2,1,0:T(8,128)(2,1)}, bf16[64,64,512]{2,1,0:T(8,128)(2,1)}) custom-call(s32[8]{0:T(128)S(1)} %broadcast_select_fusion.ids_ref, bf16[16,64,32,128]{3,2,1,0:T(8,128)(2,1)} %copy-done, bf16[16,64,32,128]{3,2,1,0:T(8,128)(2,1)} %copy-done, ...), custom_call_target="tpu_custom_call" | custom-call | flops 12884901888 | bytes 33554432 | tf_op jit(solution)/shard_map/pallas_call | solution.py:211
  764.2 1.9 copy-done.9
  766.1 21.0 %all-to-all-done.2 = bf16[16,4,64,512]{3,2,1,0:T(8,128)(2,1)} async-done(((bf16[16,4,64,512]{3,2,1,0:T(8,128)(2,1)}), bf16[16,4,64,512]{3,2,1,0:T(8,128)(2,1)}, u32[]{:S(2)}, u32[]{:S(2)}) %all-to-all-start.2) | async-done | bytes 4194336 | tf_op jit(solution)/shard_map/all_to_all | solution.py:498
  787.1 10.6 all-to-all-start.6
  797.7 27.1 %shard_map.71 = (bf16[64,64,512]{2,1,0:T(8,128)(2,1)S(1)}, bf16[64,64,512]{2,1,0:T(8,128)(2,1)}, bf16[64,64,512]{2,1,0:T(8,128)(2,1)}, bf16[64,64,512]{2,1,0:T(8,128)(2,1)}) custom-call(s32[8]{0:T(128)S(1)} %broadcast_select_fusion.ids_ref, bf16[16,64,32,128]{3,2,1,0:T(8,128)(2,1)} %copy-done, bf16[16,64,32,128]{3,2,1,0:T(8,128)(2,1)} %copy-done, ...), custom_call_target="tpu_custom_call" | custom-call | flops 12884901888 | bytes 33554432 | tf_op jit(solution)/shard_map/pallas_call | solution.py:211
  824.8 2.0 copy-done.10
  826.8 20.9 %all-to-all-done.6.refs_2_ = bf16[16,4,64,512]{3,2,1,0:T(8,128)(2,1)} async-done(((bf16[16,4,64,512]{3,2,1,0:T(8,128)(2,1)}), bf16[16,4,64,512]{3,2,1,0:T(8,128)(2,1)}, u32[]{:S(2)}, u32[]{:S(2)}) %all-to-all-start.6) | async-done | bytes 4194336 | tf_op jit(solution)/shard_map/all_to_all | solution.py:498
  847.8 60.2 %all_to_all.51.refs_0_ = bf16[16,4,64,512]{3,2,1,0:T(8,128)(2,1)S(1)} all-to-all(bf16[16,4,64,512]{3,2,1,0:T(8,128)(2,1)} %bitcast.35), channel_id=1, replica_groups=mesh['core'=2,'half'=2,'inner'=8] {'core','inner'}, dimensions={0} | all-to-all | bytes 8388608 | tf_op jit(solution)/shard_map/all_to_all | solution.py:498
  907.9 52.1 %all_to_all.52.refs_1_ = bf16[16,4,64,512]{3,2,1,0:T(8,128)(2,1)S(1)} all-to-all(bf16[16,4,64,512]{3,2,1,0:T(8,128)(2,1)S(1)} %bitcast.34), channel_id=1, replica_groups=mesh['core'=2,'half'=2,'inner'=8] {'core','inner'}, dimensions={0} | all-to-all | bytes 8388608 | tf_op jit(solution)/shard_map/all_to_all | solution.py:498
  960.0 7.0 shard_map.74
  967.1 52.8 %all_to_all.53 = bf16[16,4,64,512]{3,2,1,0:T(8,128)(2,1)} all-to-all(bf16[16,4,64,512]{3,2,1,0:T(8,128)(2,1)S(1)} %shard_map.74), channel_id=1, replica_groups=mesh['core'=2,'half'=2,'inner'=8] {'core','inner'}, dimensions={0} | all-to-all | bytes 8388608 | tf_op jit(solution)/shard_map/all_to_all | solution.py:498
  1019.9 11.3 shard_map.75
  1031.2 52.1 %all_to_all.54.refs_0_ = bf16[16,4,64,512]{3,2,1,0:T(8,128)(2,1)S(1)} all-to-all(bf16[16,4,64,512]{3,2,1,0:T(8,128)(2,1)S(1)} %bitcast.32), channel_id=1, replica_groups=mesh['core'=2,'half'=2,'inner'=8] {'core','inner'}, dimensions={0} | all-to-all | bytes 8388608 | tf_op jit(solution)/shard_map/all_to_all | solution.py:498
  1083.3 7.1 shard_map.76
  1090.3 1.9 copy-done.8
  1092.3 4.6 all-to-all-start.9
  1096.8 1.5 collective-permute-start.1
  1098.4 90.6 %all-to-all-done.9 = bf16[16,4,64,512]{3,2,1,0:T(8,128)(2,1)} async-done(((bf16[16,4,64,512]{3,2,1,0:T(8,128)(2,1)}), bf16[16,4,64,512]{3,2,1,0:T(8,128)(2,1)}, u32[]{:S(2)}, u32[]{:S(2)}) %all-to-all-start.9) | async-done | bytes 4194336 | tf_op jit(solution)/shard_map/all_to_all | solution.py:498
  1188.9 11.3 shard_map.77
  1200.2 1.3 collective-permute-start.2
  1201.5 6.1 maximum_convert_fusion.1.refs_0_
  1207.7 4.8 collective-permute-start.3
  1212.5 82.8 %collective-permute-done.2 = bf16[64,64,512]{2,1,0:T(8,128)(2,1)S(1)} collective-permute-done((bf16[64,64,512]{2,1,0:T(8,128)(2,1)S(1)}, bf16[64,64,512]{2,1,0:T(8,128)(2,1)S(1)}, u32[]{:S(2)}, u32[]{:S(2)}) %collective-permute-start.2) | collective-permute-done | bytes 4194336 | tf_op jit(solution)/shard_map/ppermute | solution.py:504
  1295.3 3.9 maximum_convert_fusion.refs_1_
  1299.2 3.2 collective-permute-start.4
  1302.4 5.2 collective-permute-done.4.refs_3_
  1307.6 16.9 %shard_map.78 = bf16[128,64,1024]{2,1,0:T(8,128)(2,1)} custom-call(s32[1]{0:T(128)} %bitcast.home_ref, bf16[64,64,512]{2,1,0:T(8,128)(2,1)} %maximum_convert_fusion.1.refs_0_, bf16[64,64,512]{2,1,0:T(8,128)(2,1)} %maximum_convert_fusion.refs_1_, bf16[64,64,512]{2,1,0:T(8,128)(2,1)} %collective-permute-done.3.refs_2_, ...), custom_call_target="tpu_custom_call" | custom-call | flops 8589934592 | bytes 33554432 | tf_op jit(solution)/shard_map/pallas_call | solution.py:211
  (37 shorter events, 2.0 us)
Async XLA Ops:
  0.0 229.8 %collective-permute-start = (s32[8]{0:T(128)}, s32[8]{0:T(128)S(1)}, u32[]{:S(2)}, u32[]{:S(2)}) collective-permute-start(s32[8]{0:T(128)} %bitcast.26), channel_id=1, source_target_pairs={{0,16},{16,0},{1,17},{17,1},{2,18},{18,2},{3,19},{19,3},{4,20},{20... | collective-permute-start | bytes 104 | tf_op jit(solution)/shard_map/ppermute | solution.py:520
  1.2 0.7 copy-start.14
  30.7 193.4 %copy-start.11 = (bf16[2,64,320]{2,1,0:T(8,128)(2,1)S(1)}, bf16[2,64,320]{2,1,0:T(8,128)(2,1)}, u32[]{:S(2)}) copy-start(bf16[2,64,320]{2,1,0:T(8,128)(2,1)} %proj_ref.1) | copy-start | bytes 245764
  30.7 193.4 %copy-start.12 = (bf16[2,64,64]{2,1,0:T(8,128)(2,1)S(1)}, bf16[2,64,64]{2,1,0:T(8,128)(2,1)}, u32[]{:S(2)}) copy-start(bf16[2,64,64]{2,1,0:T(8,128)(2,1)} %out_ref.1) | copy-start | bytes 49156
  30.7 193.4 %copy-start.13 = (bf16[64,128]{1,0:T(8,128)(2,1)S(1)}, bf16[64,128]{1,0:T(8,128)(2,1)}, u32[]{:S(2)}) copy-start(bf16[64,128]{1,0:T(8,128)(2,1)} %final_ref.1) | copy-start | bytes 49156
  30.7 199.1 %copy-start.15 = (s32[1,8]{1,0:T(1,128)S(1)}, s32[1,8]{1,0:T(1,128)}, u32[]{:S(2)}) copy-start(s32[1,8]{1,0:T(1,128)} %param.7) | copy-start | bytes 100
  220.8 3.3 copy-start
  254.5 2.0 copy-start.2
  256.5 278.7 %all-to-all-start = ((bf16[16,2,4,32,1024]{4,3,2,1,0:T(8,128)(2,1)}), bf16[16,2,4,32,1024]{4,3,2,1,0:T(8,128)(2,1)}, u32[]{:S(2)}, u32[]{:S(2)}) async-start(bf16[16,2,4,32,1024]{4,3,2,1,0:T(8,128)(2,1)} %get-tuple-element.23), calls=%async_computation | async-start | bytes 16777216 | tf_op jit(solution)/shard_map/all_to_all | solution.py:498
  510.7 3.4 copy-start.1
  533.1 2.1 copy-start.3
  669.7 2.0 copy-start.7
  671.7 54.4 %all-to-all-start.5 = ((bf16[16,4,64,512]{3,2,1,0:T(8,128)(2,1)}), bf16[16,4,64,512]{3,2,1,0:T(8,128)(2,1)}, u32[]{:S(2)}, u32[]{:S(2)}) async-start(bf16[16,4,64,512]{3,2,1,0:T(8,128)(2,1)} %copy-done.7), calls=%async_computation.5 | async-start | bytes 8388608 | tf_op jit(solution)/shard_map/all_to_all | solution.py:498
  684.4 2.0 copy-start.6
  726.1 61.0 %all-to-all-start.2 = ((bf16[16,4,64,512]{3,2,1,0:T(8,128)(2,1)}), bf16[16,4,64,512]{3,2,1,0:T(8,128)(2,1)}, u32[]{:S(2)}, u32[]{:S(2)}) async-start(bf16[16,4,64,512]{3,2,1,0:T(8,128)(2,1)} %copy-done.6), calls=%async_computation.2 | async-start | bytes 8388608 | tf_op jit(solution)/shard_map/all_to_all | solution.py:498
  764.2 1.9 copy-start.9
  787.1 60.6 %all-to-all-start.6 = ((bf16[16,4,64,512]{3,2,1,0:T(8,128)(2,1)}), bf16[16,4,64,512]{3,2,1,0:T(8,128)(2,1)}, u32[]{:S(2)}, u32[]{:S(2)}) async-start(bf16[16,4,64,512]{3,2,1,0:T(8,128)(2,1)} %bitcast.33), calls=%async_computation.6 | async-start | bytes 8388608 | tf_op jit(solution)/shard_map/all_to_all | solution.py:498
  824.8 2.0 copy-start.10
  847.8 60.2 %copy-start.17 = (bf16[64,64,512]{2,1,0:T(8,128)(2,1)S(1)}, bf16[64,64,512]{2,1,0:T(8,128)(2,1)}, u32[]{:S(2)}) copy-start(bf16[64,64,512]{2,1,0:T(8,128)(2,1)} %get-tuple-element.31) | copy-start | bytes 12582916
  1019.9 11.3 copy-start.16
  1031.1 52.1 %copy-start.4 = (bf16[64,64,512]{2,1,0:T(8,128)(2,1)}, bf16[64,64,512]{2,1,0:T(8,128)(2,1)S(1)}, u32[]{:S(2)}) copy-start(bf16[64,64,512]{2,1,0:T(8,128)(2,1)S(1)} %shard_map.75) | copy-start | bytes 12582916
  1090.3 2.0 copy-start.8
  1092.3 96.7 %all-to-all-start.9 = ((bf16[16,4,64,512]{3,2,1,0:T(8,128)(2,1)}), bf16[16,4,64,512]{3,2,1,0:T(8,128)(2,1)}, u32[]{:S(2)}, u32[]{:S(2)}) async-start(bf16[16,4,64,512]{3,2,1,0:T(8,128)(2,1)} %copy-done.8), calls=%async_computation.9 | async-start | bytes 8388608 | tf_op jit(solution)/shard_map/all_to_all | solution.py:498
  1096.8 104.7 %collective-permute-start.1 = (bf16[64,64,512]{2,1,0:T(8,128)(2,1)}, bf16[64,64,512]{2,1,0:T(8,128)(2,1)}, u32[]{:S(2)}, u32[]{:S(2)}) collective-permute-start(bf16[64,64,512]{2,1,0:T(8,128)(2,1)} %copy-done.4), channel_id=1, source_target_pairs={{8,0},{16,24},{9,1},{17,25},{10,2},{18,26},{11,3},{19,27},{12,4},{... | collective-permute-start | bytes 12582920 | tf_op jit(solution)/shard_map/ppermute | solution.py:504
  1188.9 12.6 copy-start.5
  1200.2 95.1 %collective-permute-start.2 = (bf16[64,64,512]{2,1,0:T(8,128)(2,1)S(1)}, bf16[64,64,512]{2,1,0:T(8,128)(2,1)S(1)}, u32[]{:S(2)}, u32[]{:S(2)}) collective-permute-start(bf16[64,64,512]{2,1,0:T(8,128)(2,1)S(1)} %shard_map.77), channel_id=1, source_target_pairs={{8,0},{16,24},{9,1},{17,25},{10,2},{18,26},{11,3},{19,27},{12,4},{... | collective-permute-start | bytes 12582920 | tf_op jit(solution)/shard_map/ppermute | solution.py:504
  1207.7 94.7 %collective-permute-start.3 = (bf16[64,64,512]{2,1,0:T(8,128)(2,1)}, bf16[64,64,512]{2,1,0:T(8,128)(2,1)}, u32[]{:S(2)}, u32[]{:S(2)}) collective-permute-start(bf16[64,64,512]{2,1,0:T(8,128)(2,1)} %maximum_convert_fusion.1.refs_0_), channel_id=1, source_target_pairs={{0,16},{24,8},{1,17},{25,9},{2,18},{26,10},{3,19},{27,11},{4,20},{... | collective-permute-start | bytes 12582920 | tf_op jit(solution)/shard_map/ppermute | solution.py:504
  1299.2 8.4 collective-permute-start.4

commit v4 on v3

--- a/solution.py
+++ b/solution.py
@@ -115,13 +115,17 @@
 
 
 def first_kernel(per, ids_ref, *refs):
-    wide_ref, mask_ref, both_ref, gate_ref = refs[per:]
-    _, _, group, sub, lanes = both_ref.shape
+    wide_ref, mask_ref, gate_ref, *send_refs = refs[per:]
+    group, sub, lanes = send_refs[0].shape[-3:]
 
     def store(piece, left, right, gate):
         place = slice(piece.start // group, piece.stop // group)
-        both_ref[place, 0] = left.reshape(-1, group, sub, lanes)
-        both_ref[place, 1] = right.reshape(-1, group, sub, lanes)
+        for side, value in enumerate((left, right)):
+            value = value.reshape(-1, group, sub, lanes)
+            if len(send_refs) == 1:
+                send_refs[0][place, side] = value
+            else:
+                send_refs[side][place] = value
         gate_ref[piece] = gate
 
     project(tiles_of(refs[:per]), wide_ref, mask_ref, store)
@@ -157,18 +161,11 @@
     final_ref[...] = channel_norm(pair.astype(jnp.float32)).astype(final_ref.dtype)
 
 
-def end_kernel(home_ref, *refs):
-    hiddens, shareds = refs[: len(refs) // 2 - 1], refs[len(refs) // 2 - 1 : -2]
-    wide_ref, out_ref = refs[-2:]
-    home = home_ref[0] == 1
-    lanes = hiddens[0].shape[-1]
-    for number, (hidden_ref, shared_ref) in enumerate(zip(hiddens, shareds)):
-        hidden = jnp.where(
-            home, hidden_ref[...].astype(jnp.float32), shared_ref[...].astype(jnp.float32)
-        )
-        out_ref[:, :, number * lanes : (number + 1) * lanes] = flat_dot(
-            wide_ref[...], hidden
-        ).astype(out_ref.dtype)
+def end_kernel(home_ref, hidden_ref, shared_ref, wide_ref, *refs):
+    hidden = jnp.where(
+        home_ref[0] == 1, hidden_ref[...].astype(jnp.float32), shared_ref[...].astype(jnp.float32)
+    )
+    refs[-1][...] = flat_dot(wide_ref[...], hidden).astype(refs[-1].dtype)
 
 
 PARAMS = pltpu.CompilerParams(vmem_limit_bytes=48 << 20)
@@ -222,12 +219,14 @@
     )(ids, *operands)
 
 
-def first_stage(part, ids, got, wide, mask):
+def first_stage(part, joint, ids, got, wide, mask):
     targets, channels, width, tile = got.shape
     per = ids.shape[0] // SPLIT
     lanes = per * tile
     count = width // SUB
     group = channels // targets
+    lead, copies = ((targets, 2), 1) if joint else ((targets,), 2)
+    zeros = (0,) * (len(lead) + 1)
     specs = tile_specs(got, per, lambda n, w: (n, w)) + [
         pl.BlockSpec((None, *wide.shape[1:]), lambda n, w, _: (0, 0, 0, 0)),
         pl.BlockSpec((SUB, lanes), lambda n, w, _: (part * count + w, n)),
@@ -238,15 +237,11 @@
             num_scalar_prefetch=1,
             grid=(SPLIT, count),
             in_specs=specs,
-            out_specs=[
-                pl.BlockSpec((targets, 2, group, SUB, lanes), lambda n, w, _: (0, 0, 0, w, n)),
-                pl.BlockSpec((channels, SUB, lanes), lambda n, w, _: (0, w, n)),
-            ],
+            out_specs=[pl.BlockSpec((channels, SUB, lanes), lambda n, w, _: (0, w, n))]
+            + [pl.BlockSpec((*lead, group, SUB, lanes), lambda n, w, _: (*zeros, w, n))] * copies,
         ),
-        out_shape=[
-            jax.ShapeDtypeStruct((targets, 2, group, width, SPLIT * lanes), got.dtype),
-            jax.ShapeDtypeStruct((channels, width, SPLIT * lanes), got.dtype),
-        ],
+        out_shape=[jax.ShapeDtypeStruct((channels, width, SPLIT * lanes), got.dtype)]
+        + [jax.ShapeDtypeStruct((*lead, group, width, SPLIT * lanes), got.dtype)] * copies,
         compiler_params=PARAMS,
         cost_estimate=cost(
             2 * wide.size // NLAYER * count * SPLIT * lanes, 8 * channels * width * SPLIT * lanes
@@ -299,13 +294,28 @@
     )(pair, back, gate, out_wide)
 
 
-def end_stage(home, hiddens, shareds, wide):
-    _, width, lanes = hiddens[0].shape
-    shape = (wide.shape[0] // SUB, width, lanes * len(hiddens))
-    out = jax.ShapeDtypeStruct(shape, hiddens[0].dtype)
-    specs = [by_columns(hiddens[0].shape)] * (2 * len(hiddens)) + [whole(wide.shape)]
-    flops = 2 * wide.size * width // SUB * shape[2]
-    return stage(end_kernel, specs, [out], home, [*hiddens, *shareds, wide], flops)[0]
+def end_stage(home, number, count, hidden, shared, wide, earlier):
+    width, lanes = hidden.shape[1:]
+    columns = wide.shape[0] // SUB
+    out = jax.ShapeDtypeStruct((columns, width, lanes * count), hidden.dtype)
+    specs = [by_columns(hidden.shape)] * 2 + [whole(wide.shape)]
+    operands = [hidden, shared, wide]
+    if earlier is not None:
+        specs.append(pl.BlockSpec(memory_space=pl.ANY))
+        operands.append(earlier)
+    return pl.pallas_call(
+        end_kernel,
+        grid_spec=pltpu.PrefetchScalarGridSpec(
+            num_scalar_prefetch=1,
+            grid=(width // SUB,),
+            in_specs=specs,
+            out_specs=pl.BlockSpec((columns, SUB, lanes), lambda w, _: (0, w, number)),
+        ),
+        out_shape=out,
+        input_output_aliases={} if earlier is None else {4: 0},
+        compiler_params=PARAMS,
+        cost_estimate=cost(2 * wide.size * width // SUB * lanes, 8 * hidden.size),
+    )(home, *operands)
 
 
 def product_kernel(axis, count, *refs):
@@ -348,14 +358,26 @@
 
 
 def depth_products(number, boths, chunk):
-    targets, _, channels, width, lanes = boths[0].shape
-
-    def spec(side, size, place):
-        return pl.BlockSpec((targets, None, 1, width, size), lambda c: (0, side, c, 0, place))
-
-    out = jax.ShapeDtypeStruct((targets, channels, width * len(boths), chunk), boths[0].dtype)
-    specs = [spec(0, chunk, number)] * len(boths) + [spec(1, lanes, 0)] * len(boths)
-    return product_call("depth", specs, boths + boths, len(boths), out)
+    targets, channels = boths[0][0].shape[0], boths[0][0].shape[-3]
+    specs, operands, depth = [], [], 0
+    for side in range(2):
+        for arrays in boths:
+            width, lanes = arrays[0].shape[-2:]
+            size, place = (lanes, 0) if side else (chunk, number)
+            if len(arrays) == 1:
+                spec = pl.BlockSpec(
+                    (targets, None, 1, width, size),
+                    lambda c, side=side, place=place: (0, side, c, 0, place),
+                )
+            else:
+                spec = pl.BlockSpec(
+                    (targets, 1, width, size), lambda c, place=place: (0, c, 0, place)
+                )
+            specs.append(spec)
+            operands.append(arrays[0] if len(arrays) == 1 else arrays[side])
+            depth += (1 - side) * width
+    out = jax.ShapeDtypeStruct((targets, channels, depth, chunk), operands[0].dtype)
+    return product_call("depth", specs, operands, len(boths), out)
 
 
 def row_products(left, rights):
@@ -519,9 +541,8 @@
     held_ids = crop_tiles[0]
     other_ids = lax.ppermute(held_ids, "core", [(0, 1), (1, 0)])
     crop_ids = jnp.where(core == half, held_ids, other_ids)
-    steps_crop = jnp.arange(CROP, dtype=jnp.int32)
-    position = crop_ids[steps_crop // TILE] * TILE + steps_crop % TILE
-    usable = (position < full_length[0]).astype(jnp.float32)
+    position = crop_ids[:, None] * TILE + jnp.arange(TILE, dtype=jnp.int32)
+    usable = (position < full_length[0]).astype(jnp.float32).reshape(CROP)
     col_usable = lax.dynamic_slice_in_dim(usable, my_index * col_width, col_width)
     pair_mask = col_usable[:, None] * usable[None, :]
     send = pack(held_ids, jnp.transpose(pair_maps[0], (0, 2, 1)))
@@ -530,20 +551,24 @@
     gots, gates, boths = [], [], []
     for part in range(COLUMN_PARTS):
         got = spread(send, part)
-        both, gate = first_stage(part, crop_ids, got, wides, pair_mask)
-        send = after(send, both)
+        joint = part + 1 < COLUMN_PARTS
+        gate, *sends = first_stage(part, joint, crop_ids, got, wides, pair_mask)
+        send = after(send, sends[0])
         gots.append(got)
         gates.append(gate)
-        boths.append(exchange(both))
+        arrays = []
+        for value in sends:
+            arrays.append(exchange(value))
+        boths.append(arrays)
     following = []
     for number in range(SPLIT):
         merged = exchange(depth_products(number, boths, chunk)).reshape(CH, col_width, chunk)
         following.append(
             middle_stage(0, number, crop_ids, gots, merged, gates, outs, wides, pair_mask)
         )
-    rights = [
-        exchange(item[1].reshape(row_count, per_group, col_width, chunk)) for item in following
-    ]
+    rights = []
+    for item in following:
+        rights.append(exchange(item[1].reshape(row_count, per_group, col_width, chunk)))
     ready, arrived = [], []
     back = None
     for pair, _, gate, *lefts in following:
@@ -560,7 +585,10 @@
         hiddens.append(jnp.maximum(summed / halves, 0.0).astype(jnp.bfloat16))
         shareds.append(moved(hiddens[-1], [((0, 0), (1, 0)), ((1, 1), (0, 1))]))
     home = (core == half).astype(jnp.int32)[None]
-    return end_stage(home, hiddens, shareds, final_wide)
+    result = None
+    for number, (hidden, shared) in enumerate(zip(hiddens, shareds)):
+        result = end_stage(home, number, len(hiddens), hidden, shared, final_wide, result)
+    return result
 
 
 def on_device(pair_maps, crop_tiles, full_length, proj_weight, out_weight, final_weight):

time: 1330 us -> 1360 us (1.023)
  blocking collectives: 344 us -> 444 us
  Pallas kernels: 622 us -> 591 us
  starting transfers between devices: 60.4 us -> 35.8 us
    all_to_all x5 -> x7, blocking collectives: 344 us -> 444 us  [exchange(): return lax.all_to_all(value, GROUP, split_axis=0, concat_axis=0, tiled=True)]
    pallas_call x2, Pallas kernels: 426 us -> 392 us  [spread(): pl.pallas_call(functools.partial(spread_kernel, part), in_specs=[pl.Block...]
    all_to_all x5 -> x4, starting transfers between devices: 49.1 us -> 24.7 us  [exchange(): return lax.all_to_all(value, GROUP, split_axis=0, concat_axis=0, tiled=True)]
    pallas_call x0 -> x2, Pallas kernels: none -> 21.8 us  [end_stage(): pl.pallas_call(end_kernel, grid_spec=pltpu.PrefetchScalarGridSpec(num_sca...]
    pallas_call x3 -> x2, Pallas kernels: 71.1 us -> 54.2 us  [stage(): pl.pallas_call(kernel, grid_spec=pltpu.PrefetchScalarGridSpec(num_scalar_...]
    all_to_all x5 -> x4, waiting for transfers between devices: 172 us -> 168 us  [exchange(): return lax.all_to_all(value, GROUP, split_axis=0, concat_axis=0, tiled=True)]
  transfers between devices with their start and end apart: 10 -> 9, of which waited for: 6 -> 5; matrix products, arithmetic and copies ran while one was open for 1% -> 1% of each run, Pallas kernels for 42% -> 23%
where the time goes in v4:
time: 1360 us
  Pallas kernels  591 us (43%)
  blocking collectives  444 us (33%)
  waiting for transfers between devices  251 us (18%)
  starting transfers between devices  35.8 us (3%)
  local copies, waits for them, and re-layouts  23.7 us (2%)
    all_to_all x7, blocking collectives, exchange(): return lax.all_to_all(value, GROUP, split_axis=0, concat_axis=0, tiled=True)  444 us
    pallas_call x2, Pallas kernels, spread(): pl.pallas_call(functools.partial(spread_kernel, part), in_specs=[pl.Block...  392 us
    all_to_all x4, waiting for transfers between devices, exchange(): return lax.all_to_all(value, GROUP, split_axis=0, concat_axis=0, tiled=True)  168 us
    ppermute x4, waiting for transfers between devices, moved(): return lax.ppermute(value, ('core', 'half'), steps)  83 us
    pallas_call x2, Pallas kernels, stage(): pl.pallas_call(kernel, grid_spec=pltpu.PrefetchScalarGridSpec(num_scalar_...  54.2 us
    pallas_call x2, Pallas kernels, first_stage(): pl.pallas_call(functools.partial(first_kernel, per), grid_spec=pltpu.Pref...  38.2 us
    pallas_call x1, Pallas kernels, pack(): pl.pallas_call(pack_kernel, grid_spec=pltpu.PrefetchScalarGridSpec(num_sc...  28.8 us
    pallas_call x4, Pallas kernels, product_call(): pl.pallas_call(functools.partial(product_kernel, axis, count), grid=(chan...  28.4 us
  transfers between devices with their start and end apart: 9, of which 5 were waited for; matrix products, arithmetic and copies ran while one was open for 1% of the time, Pallas kernels for 23%

profile of v4, /device:TPU:0, one launch (start us, length us, event | category | flops | bytes accessed | tf_op | source)
XLA Modules:
  0.0 1358.0 jit_solution(1322132078228532966)
XLA Ops:
  1.8 28.8 %shard_map.64 = bf16[64,1024,128]{2,1,0:T(8,128)(2,1)} custom-call(s32[8]{0:T(128)S(1)} %bitcast.21, bf16[128,64,2048]{2,1,0:T(8,128)(2,1)} %bitcast.24), custom_call_target="tpu_custom_call" | custom-call | bytes 33554432 | tf_op jit(solution)/shard_map/pallas_call | solution.py:404
  30.7 190.1 %shard_map.65.refs_0_.refs_1_.refs_2_.refs_3_ = bf16[16,64,32,128]{3,2,1,0:T(8,128)(2,1)S(1)} custom-call(bf16[64,16,64,128]{3,2,1,0:T(8,128)(2,1)} %bitcast.22), custom_call_target="tpu_custom_call" | custom-call | bytes 268435456 | tf_op jit(solution)/shard_map/pallas_call | solution.py:498
  220.8 3.3 copy-done
  224.0 5.7 shard_map.66
  230.0 19.1 %shard_map.67 = (bf16[64,32,1024]{2,1,0:T(8,128)(2,1)S(1)}, bf16[16,2,4,32,1024]{4,3,2,1,0:T(8,128)(2,1)}) custom-call(s32[8]{0:T(128)S(1)} %get-tuple-element.42.ids_ref, bf16[16,64,32,128]{3,2,1,0:T(8,128)(2,1)} %copy-done, bf16[16,64,32,128]{3,2,1,0:T(8,128)(2,1)} %copy-done, bf16[16,64,32,128]{3,2,1,0:T(8,128)(2,1)} %copy-done, ...), custom_call_target="tpu_custom_call" | custom-call | flops 10737418240 | bytes 16777216 | tf_op jit(solution)/shard_map/pallas_call | solution.py:234
  249.1 2.0 copy-done.7
  251.1 201.7 %shard_map.68.refs_0_.refs_1_.refs_2_.refs_3_.refs_4_.refs_5_.refs_6_.refs_7_ = bf16[16,64,32,128]{3,2,1,0:T(8,128)(2,1)S(1)} custom-call(bf16[64,16,64,128]{3,2,1,0:T(8,128)(2,1)} %bitcast.23), custom_call_target="tpu_custom_call" | custom-call | bytes 268435456 | tf_op jit(solution)/shard_map/pallas_call | solution.py:498
  452.8 3.4 copy-done.1
  456.2 19.1 %shard_map.69 = (bf16[64,32,1024]{2,1,0:T(8,128)(2,1)S(1)}, bf16[16,4,32,1024]{3,2,1,0:T(8,128)(2,1)}, bf16[16,4,32,1024]{3,2,1,0:T(8,128)(2,1)}) custom-call(s32[8]{0:T(128)S(1)} %get-tuple-element.42.ids_ref, bf16[16,64,32,128]{3,2,1,0:T(8,128)(2,1)} %copy-done.1, bf16[16,64,32,128]{3,2,1,0:T(8,128)(2,1)} %copy-done.1, ...), custom_call_target="tpu_custom_call" | custom-call | flops 10737418240 | bytes 16777216 | tf_op jit(solution)/shard_map/pallas_call | solution.py:234
  475.4 67.9 %all_to_all.55.refs_1_ = bf16[16,4,32,1024]{3,2,1,0:T(8,128)(2,1)S(1)} all-to-all(bf16[16,4,32,1024]{3,2,1,0:T(8,128)(2,1)} %get-tuple-element.28), channel_id=1, replica_groups=mesh['core'=2,'half'=2,'inner'=8] {'core','inner'}, dimensions={0} | all-to-all | bytes 8388608 | tf_op jit(solution)/shard_map/all_to_all | solution.py:520
  543.2 52.6 %all_to_all.56.refs_3_ = bf16[16,4,32,1024]{3,2,1,0:T(8,128)(2,1)S(1)} all-to-all(bf16[16,4,32,1024]{3,2,1,0:T(8,128)(2,1)S(1)} %copy-done.22), channel_id=1, replica_groups=mesh['core'=2,'half'=2,'inner'=8] {'core','inner'}, dimensions={0} | all-to-all | bytes 8388608 | tf_op jit(solution)/shard_map/all_to_all | solution.py:520
  595.9 98.2 %all_to_all.57.refs_0_.refs_2_ = bf16[16,2,4,32,1024]{4,3,2,1,0:T(8,128)(2,1)} all-to-all(bf16[16,2,4,32,1024]{4,3,2,1,0:T(8,128)(2,1)S(1)} %bitcast.27), channel_id=1, replica_groups=mesh['core'=2,'half'=2,'inner'=8] {'core','inner'}, dimensions={0} | all-to-all | bytes 16777216 | tf_op jit(solution)/shard_map/all_to_all | solution.py:520
  694.1 7.1 shard_map.72
  701.2 2.0 copy-done.12
  703.1 4.6 all-to-all-start.4
  707.7 2.2 copy-done.3
  709.9 2.2 copy-done.5
  712.1 7.0 shard_map.70
  719.1 2.0 copy-done.11
  721.1 36.2 %all-to-all-done.4 = bf16[16,4,64,512]{3,2,1,0:T(8,128)(2,1)} async-done(((bf16[16,4,64,512]{3,2,1,0:T(8,128)(2,1)}), bf16[16,4,64,512]{3,2,1,0:T(8,128)(2,1)}, u32[]{:S(2)}, u32[]{:S(2)}) %all-to-all-start.4) | async-done | bytes 4194336 | tf_op jit(solution)/shard_map/all_to_all | solution.py:520
  757.3 11.0 all-to-all-start.3
  768.3 27.1 %shard_map.73 = (bf16[64,64,512]{2,1,0:T(8,128)(2,1)S(1)}, bf16[64,64,512]{2,1,0:T(8,128)(2,1)}, bf16[64,64,512]{2,1,0:T(8,128)(2,1)}, bf16[64,64,512]{2,1,0:T(8,128)(2,1)}) custom-call(s32[8]{0:T(128)S(1)} %get-tuple-element.42.ids_ref, bf16[16,64,32,128]{3,2,1,0:T(8,128)(2,1)} %copy-done, bf16[16,64,32,128]{3,2,1,0:T(8,128)(2,1)} %copy-done, ...), custom_call_target="tpu_custom_call" | custom-call | flops 12884901888 | bytes 33554432 | tf_op jit(solution)/shard_map/pallas_call | solution.py:208
  795.4 1.9 copy-done.15
  797.4 21.0 %all-to-all-done.3 = bf16[16,4,64,512]{3,2,1,0:T(8,128)(2,1)} async-done(((bf16[16,4,64,512]{3,2,1,0:T(8,128)(2,1)}), bf16[16,4,64,512]{3,2,1,0:T(8,128)(2,1)}, u32[]{:S(2)}, u32[]{:S(2)}) %all-to-all-start.3) | async-done | bytes 4194336 | tf_op jit(solution)/shard_map/all_to_all | solution.py:520
  818.3 60.1 %all_to_all.58.refs_1_ = bf16[16,4,64,512]{3,2,1,0:T(8,128)(2,1)} all-to-all(bf16[16,4,64,512]{3,2,1,0:T(8,128)(2,1)} %bitcast.31), channel_id=1, replica_groups=mesh['core'=2,'half'=2,'inner'=8] {'core','inner'}, dimensions={0} | all-to-all | bytes 8388608 | tf_op jit(solution)/shard_map/all_to_all | solution.py:520
  878.4 4.5 all-to-all-start.5
  883.0 27.1 %shard_map.71 = (bf16[64,64,512]{2,1,0:T(8,128)(2,1)S(1)}, bf16[64,64,512]{2,1,0:T(8,128)(2,1)}, bf16[64,64,512]{2,1,0:T(8,128)(2,1)}, bf16[64,64,512]{2,1,0:T(8,128)(2,1)}) custom-call(s32[8]{0:T(128)S(1)} %get-tuple-element.42.ids_ref, bf16[16,64,32,128]{3,2,1,0:T(8,128)(2,1)} %copy-done, bf16[16,64,32,128]{3,2,1,0:T(8,128)(2,1)} %copy-done, ...), custom_call_target="tpu_custom_call" | custom-call | flops 12884901888 | bytes 33554432 | tf_op jit(solution)/shard_map/pallas_call | solution.py:208
  910.1 2.0 copy-done.14
  912.1 20.5 %all-to-all-done.5.refs_0_ = bf16[16,4,64,512]{3,2,1,0:T(8,128)(2,1)} async-done(((bf16[16,4,64,512]{3,2,1,0:T(8,128)(2,1)}), bf16[16,4,64,512]{3,2,1,0:T(8,128)(2,1)}, u32[]{:S(2)}, u32[]{:S(2)}) %all-to-all-start.5) | async-done | bytes 4194336 | tf_op jit(solution)/shard_map/all_to_all | solution.py:520
  932.6 60.8 %all_to_all.59.refs_2_ = bf16[16,4,64,512]{3,2,1,0:T(8,128)(2,1)} all-to-all(bf16[16,4,64,512]{3,2,1,0:T(8,128)(2,1)} %bitcast.30), channel_id=1, replica_groups=mesh['core'=2,'half'=2,'inner'=8] {'core','inner'}, dimensions={0} | all-to-all | bytes 8388608 | tf_op jit(solution)/shard_map/all_to_all | solution.py:520
  993.4 7.3 shard_map.74
  1000.6 52.8 %all_to_all.60 = bf16[16,4,64,512]{3,2,1,0:T(8,128)(2,1)} all-to-all(bf16[16,4,64,512]{3,2,1,0:T(8,128)(2,1)S(1)} %shard_map.74), channel_id=1, replica_groups=mesh['core'=2,'half'=2,'inner'=8] {'core','inner'}, dimensions={0} | all-to-all | bytes 8388608 | tf_op jit(solution)/shard_map/all_to_all | solution.py:520
  1053.5 11.3 shard_map.75
  1064.8 52.1 %all_to_all.61.refs_0_ = bf16[16,4,64,512]{3,2,1,0:T(8,128)(2,1)S(1)} all-to-all(bf16[16,4,64,512]{3,2,1,0:T(8,128)(2,1)S(1)} %bitcast.29), channel_id=1, replica_groups=mesh['core'=2,'half'=2,'inner'=8] {'core','inner'}, dimensions={0} | all-to-all | bytes 8388608 | tf_op jit(solution)/shard_map/all_to_all | solution.py:520
  1116.8 7.0 shard_map.76
  1123.9 2.0 copy-done.13
  1125.9 4.5 all-to-all-start.10
  1130.4 1.3 collective-permute-start.3
  1131.7 90.8 %all-to-all-done.10 = bf16[16,4,64,512]{3,2,1,0:T(8,128)(2,1)} async-done(((bf16[16,4,64,512]{3,2,1,0:T(8,128)(2,1)}), bf16[16,4,64,512]{3,2,1,0:T(8,128)(2,1)}, u32[]{:S(2)}, u32[]{:S(2)}) %all-to-all-start.10) | async-done | bytes 4194336 | tf_op jit(solution)/shard_map/all_to_all | solution.py:520
  1222.5 11.3 shard_map.77
  1233.8 1.3 collective-permute-start.1
  1235.1 6.1 maximum_convert_fusion.hidden_ref
  1241.2 4.7 collective-permute-start.4
  1246.0 82.9 %collective-permute-done.1 = bf16[64,64,512]{2,1,0:T(8,128)(2,1)S(1)} collective-permute-done((bf16[64,64,512]{2,1,0:T(8,128)(2,1)S(1)}, bf16[64,64,512]{2,1,0:T(8,128)(2,1)S(1)}, u32[]{:S(2)}, u32[]{:S(2)}) %collective-permute-start.1) | collective-permute-done | bytes 4194336 | tf_op jit(solution)/shard_map/ppermute | solution.py:526
  1328.9 4.0 maximum_convert_fusion.1.hidden_ref
  1332.9 3.3 collective-permute-start.2
  1336.2 10.9 shard_map.78.refs_0_
  1347.1 10.9 shard_map.79
  (50 shorter events, 1.5 us)
Async XLA Ops:
  0.0 229.7 %collective-permute-start = (s32[8]{0:T(128)}, s32[8]{0:T(128)S(1)}, u32[]{:S(2)}, u32[]{:S(2)}) collective-permute-start(s32[8]{0:T(128)} %bitcast.20), channel_id=1, source_target_pairs={{0,16},{16,0},{1,17},{17,1},{2,18},{18,2},{3,19},{19,3},{4,20},{20... | collective-permute-start | bytes 104 | tf_op jit(solution)/shard_map/ppermute | solution.py:542
  1.1 0.7 copy-start.19
  30.6 193.4 %copy-start.16 = (bf16[2,64,320]{2,1,0:T(8,128)(2,1)S(1)}, bf16[2,64,320]{2,1,0:T(8,128)(2,1)}, u32[]{:S(2)}) copy-start(bf16[2,64,320]{2,1,0:T(8,128)(2,1)} %proj_ref.1) | copy-start | bytes 245764
  30.6 193.4 %copy-start.17 = (bf16[2,64,64]{2,1,0:T(8,128)(2,1)S(1)}, bf16[2,64,64]{2,1,0:T(8,128)(2,1)}, u32[]{:S(2)}) copy-start(bf16[2,64,64]{2,1,0:T(8,128)(2,1)} %out_ref.1) | copy-start | bytes 49156
  30.7 193.4 %copy-start.18 = (bf16[64,128]{1,0:T(8,128)(2,1)S(1)}, bf16[64,128]{1,0:T(8,128)(2,1)}, u32[]{:S(2)}) copy-start(bf16[64,128]{1,0:T(8,128)(2,1)} %final_ref.1) | copy-start | bytes 49156
  30.7 199.1 %copy-start.20 = (s32[1,8]{1,0:T(1,128)S(1)}, s32[1,8]{1,0:T(1,128)}, u32[]{:S(2)}) copy-start(s32[1,8]{1,0:T(1,128)} %param.7) | copy-start | bytes 100
  220.8 3.3 copy-start
  249.1 2.0 copy-start.7
  452.8 3.4 copy-start.1
  475.3 67.9 %copy-start.8 = (bf16[64,32,1024]{2,1,0:T(8,128)(2,1)}, bf16[64,32,1024]{2,1,0:T(8,128)(2,1)S(1)}, u32[]{:S(2)}) copy-start(bf16[64,32,1024]{2,1,0:T(8,128)(2,1)S(1)} %get-tuple-element.27.refs_9_) | copy-start | bytes 12582916
  475.3 67.9 %copy-start.22 = (bf16[16,4,32,1024]{3,2,1,0:T(8,128)(2,1)S(1)}, bf16[16,4,32,1024]{3,2,1,0:T(8,128)(2,1)}, u32[]{:S(2)}) copy-start(bf16[16,4,32,1024]{3,2,1,0:T(8,128)(2,1)} %get-tuple-element.29) | copy-start | bytes 12582916
  475.3 120.5 %slice-start = ((s8[8388608]{0:T(1024)(128)(4,1)}), s8[4194304]{0:T(1024)(128)(4,1)S(1)}, s32[]{:S(2)}) async-start(s8[8388608]{0:T(1024)(128)(4,1)} %bitcast.26), calls=%async_computation.11 | async-start | bytes 8388608
  543.2 150.9 %copy-start.2 = (bf16[16,4,32,1024]{3,2,1,0:T(8,128)(2,1)}, bf16[16,4,32,1024]{3,2,1,0:T(8,128)(2,1)S(1)}, u32[]{:S(2)}) copy-start(bf16[16,4,32,1024]{3,2,1,0:T(8,128)(2,1)S(1)} %all_to_all.55.refs_1_) | copy-start | bytes 12582916
  543.2 52.6 %slice-start.1 = ((s8[8388608]{0:T(1024)(128)(4,1)}), s8[4194304]{0:T(1024)(128)(4,1)S(1)}, s32[]{:S(2)}) async-start(s8[8388608]{0:T(1024)(128)(4,1)} %bitcast.26), calls=%async_computation.12 | async-start | bytes 8388608
  595.9 98.2 %copy-start.4 = (bf16[16,4,32,1024]{3,2,1,0:T(8,128)(2,1)}, bf16[16,4,32,1024]{3,2,1,0:T(8,128)(2,1)S(1)}, u32[]{:S(2)}) copy-start(bf16[16,4,32,1024]{3,2,1,0:T(8,128)(2,1)S(1)} %all_to_all.56.refs_3_) | copy-start | bytes 12582916
  701.2 2.0 copy-start.12
  703.1 54.2 %all-to-all-start.4 = ((bf16[16,4,64,512]{3,2,1,0:T(8,128)(2,1)}), bf16[16,4,64,512]{3,2,1,0:T(8,128)(2,1)}, u32[]{:S(2)}, u32[]{:S(2)}) async-start(bf16[16,4,64,512]{3,2,1,0:T(8,128)(2,1)} %copy-done.12), calls=%async_computation.4 | async-start | bytes 8388608 | tf_op jit(solution)/shard_map/all_to_all | solution.py:520
  707.7 2.2 copy-start.3
  709.9 2.2 copy-start.5
  719.1 2.0 copy-start.11
  757.3 61.0 %all-to-all-start.3 = ((bf16[16,4,64,512]{3,2,1,0:T(8,128)(2,1)}), bf16[16,4,64,512]{3,2,1,0:T(8,128)(2,1)}, u32[]{:S(2)}, u32[]{:S(2)}) async-start(bf16[16,4,64,512]{3,2,1,0:T(8,128)(2,1)} %copy-done.11), calls=%async_computation.3 | async-start | bytes 8388608 | tf_op jit(solution)/shard_map/all_to_all | solution.py:520
  795.4 2.0 copy-start.15
  878.4 54.2 %all-to-all-start.5 = ((bf16[16,4,64,512]{3,2,1,0:T(8,128)(2,1)}), bf16[16,4,64,512]{3,2,1,0:T(8,128)(2,1)}, u32[]{:S(2)}, u32[]{:S(2)}) async-start(bf16[16,4,64,512]{3,2,1,0:T(8,128)(2,1)} %bitcast.28), calls=%async_computation.5 | async-start | bytes 8388608 | tf_op jit(solution)/shard_map/all_to_all | solution.py:520
  910.1 2.0 copy-start.14
  932.6 60.8 %copy-start.6 = (bf16[16,4,64,512]{3,2,1,0:T(8,128)(2,1)S(1)}, bf16[16,4,64,512]{3,2,1,0:T(8,128)(2,1)}, u32[]{:S(2)}) copy-start(bf16[16,4,64,512]{3,2,1,0:T(8,128)(2,1)} %all_to_all.58.refs_1_) | copy-start | bytes 12582916
  1053.5 11.3 copy-start.21
  1064.7 52.1 %copy-start.9 = (bf16[64,64,512]{2,1,0:T(8,128)(2,1)}, bf16[64,64,512]{2,1,0:T(8,128)(2,1)S(1)}, u32[]{:S(2)}) copy-start(bf16[64,64,512]{2,1,0:T(8,128)(2,1)S(1)} %shard_map.75) | copy-start | bytes 12582916
  1123.9 2.0 copy-start.13
  1125.9 96.7 %all-to-all-start.10 = ((bf16[16,4,64,512]{3,2,1,0:T(8,128)(2,1)}), bf16[16,4,64,512]{3,2,1,0:T(8,128)(2,1)}, u32[]{:S(2)}, u32[]{:S(2)}) async-start(bf16[16,4,64,512]{3,2,1,0:T(8,128)(2,1)} %copy-done.13), calls=%async_computation.10 | async-start | bytes 8388608 | tf_op jit(solution)/shard_map/all_to_all | solution.py:520
  1130.4 104.7 %collective-permute-start.3 = (bf16[64,64,512]{2,1,0:T(8,128)(2,1)}, bf16[64,64,512]{2,1,0:T(8,128)(2,1)}, u32[]{:S(2)}, u32[]{:S(2)}) collective-permute-start(bf16[64,64,512]{2,1,0:T(8,128)(2,1)} %copy-done.9), channel_id=1, source_target_pairs={{8,0},{16,24},{9,1},{17,25},{10,2},{18,26},{11,3},{19,27},{12,4},{... | collective-permute-start | bytes 12582920 | tf_op jit(solution)/shard_map/ppermute | solution.py:526
  1222.5 12.6 copy-start.10
  1233.8 95.1 %collective-permute-start.1 = (bf16[64,64,512]{2,1,0:T(8,128)(2,1)S(1)}, bf16[64,64,512]{2,1,0:T(8,128)(2,1)S(1)}, u32[]{:S(2)}, u32[]{:S(2)}) collective-permute-start(bf16[64,64,512]{2,1,0:T(8,128)(2,1)S(1)} %shard_map.77), channel_id=1, source_target_pairs={{8,0},{16,24},{9,1},{17,25},{10,2},{18,26},{11,3},{19,27},{12,4},{... | collective-permute-start | bytes 12582920 | tf_op jit(solution)/shard_map/ppermute | solution.py:526
  1241.2 95.0 %collective-permute-start.4 = (bf16[64,64,512]{2,1,0:T(8,128)(2,1)}, bf16[64,64,512]{2,1,0:T(8,128)(2,1)}, u32[]{:S(2)}, u32[]{:S(2)}) collective-permute-start(bf16[64,64,512]{2,1,0:T(8,128)(2,1)} %maximum_convert_fusion.hidden_ref), channel_id=1, source_target_pairs={{0,16},{24,8},{1,17},{25,9},{2,18},{26,10},{3,19},{27,11},{4,20},{... | collective-permute-start | bytes 12582920 | tf_op jit(solution)/shard_map/ppermute | solution.py:526
  1332.9 14.2 %collective-permute-start.2 = (bf16[64,64,512]{2,1,0:T(8,128)(2,1)}, bf16[64,64,512]{2,1,0:T(8,128)(2,1)}, u32[]{:S(2)}, u32[]{:S(2)}) collective-permute-start(bf16[64,64,512]{2,1,0:T(8,128)(2,1)} %maximum_convert_fusion.1.hidden_ref), channel_id=1, source_target_pairs={{0,16},{24,8},{1,17},{25,9},{2,18},{26,10},{3,19},{27,11},{4,20},{... | collective-permute-start | bytes 12582920 | tf_op jit(solution)/shard_map/ppermute | solution.py:526

commit v5 on v4

--- a/solution.py
+++ b/solution.py
@@ -551,8 +551,7 @@
     gots, gates, boths = [], [], []
     for part in range(COLUMN_PARTS):
         got = spread(send, part)
-        joint = part + 1 < COLUMN_PARTS
-        gate, *sends = first_stage(part, joint, crop_ids, got, wides, pair_mask)
+        gate, *sends = first_stage(part, True, crop_ids, got, wides, pair_mask)
         send = after(send, sends[0])
         gots.append(got)
         gates.append(gate)
@@ -574,8 +573,9 @@
     for pair, _, gate, *lefts in following:
         for piece, left in enumerate(lefts):
             left = left.reshape(row_count, per_group, col_width, chunk // LEFT_PARTS)
-            left = exchange(left if back is None else after(left, back, ready[-1]))
-            back = exchange(row_products(left, rights))
+            left = exchange(left if back is None else after(left, back))
+            products = row_products(left, rights)
+            back = exchange(products)
             merged = back.reshape(CH, col_width, chunk // LEFT_PARTS)
             ready.append(last_stage(NLAYER - 1, piece, pair, merged, gate, outs))
             arrived.append(moved(ready[-1], [((0, 1), (0, 0)), ((1, 0), (1, 1))]))

time: 1360 us -> 1310 us (0.963)
  blocking collectives: 444 us -> 353 us
  Pallas kernels: 591 us -> 629 us
  starting transfers between devices: 35.8 us -> 52.9 us
    all_to_all x7 -> x5, blocking collectives: 444 us -> 353 us  [exchange(): return lax.all_to_all(value, GROUP, split_axis=0, concat_axis=0, tiled=True)]
    pallas_call x2, Pallas kernels: 392 us -> 426 us  [spread(): pl.pallas_call(functools.partial(spread_kernel, part), in_specs=[pl.Block...]
    all_to_all x4 -> x5, starting transfers between devices: 24.7 us -> 43 us  [exchange(): return lax.all_to_all(value, GROUP, split_axis=0, concat_axis=0, tiled=True)]
    all_to_all x4 -> x5, waiting for transfers between devices: 168 us -> 155 us  [exchange(): return lax.all_to_all(value, GROUP, split_axis=0, concat_axis=0, tiled=True)]
  transfers between devices with their start and end apart: 9 -> 10, of which waited for: 5 -> 6; matrix products, arithmetic and copies ran while one was open for 1% -> 1% of each run, Pallas kernels for 23% -> 44%
where the time goes in v5:
time: 1310 us
  Pallas kernels  629 us (48%)
  blocking collectives  353 us (27%)
  waiting for transfers between devices  243 us (19%)
  starting transfers between devices  52.9 us (4%)
  local copies, waits for them, and re-layouts  21.3 us (2%)
    pallas_call x2, Pallas kernels, spread(): pl.pallas_call(functools.partial(spread_kernel, part), in_specs=[pl.Block...  426 us
    all_to_all x5, blocking collectives, exchange(): return lax.all_to_all(value, GROUP, split_axis=0, concat_axis=0, tiled=True)  353 us
    all_to_all x5, waiting for transfers between devices, exchange(): return lax.all_to_all(value, GROUP, split_axis=0, concat_axis=0, tiled=True)  155 us
    ppermute x4, waiting for transfers between devices, moved(): return lax.ppermute(value, ('core', 'half'), steps)  88.4 us
    pallas_call x2, Pallas kernels, stage(): pl.pallas_call(kernel, grid_spec=pltpu.PrefetchScalarGridSpec(num_scalar_...  54.2 us
    all_to_all x5, starting transfers between devices, exchange(): return lax.all_to_all(value, GROUP, split_axis=0, concat_axis=0, tiled=True)  43 us
    pallas_call x2, Pallas kernels, first_stage(): pl.pallas_call(functools.partial(first_kernel, per), grid_spec=pltpu.Pref...  38.3 us
    pallas_call x4, Pallas kernels, product_call(): pl.pallas_call(functools.partial(product_kernel, axis, count), grid=(chan...  30.2 us
  transfers between devices with their start and end apart: 10, of which 6 were waited for; matrix products, arithmetic and copies ran while one was open for 1% of the time, Pallas kernels for 44%

profile of v5, /device:TPU:0, one launch (start us, length us, event | category | flops | bytes accessed | tf_op | source)
XLA Modules:
  0.0 1310.7 jit_solution(5972843384393757280)
XLA Ops:
  1.2 0.6 copy-done.13
  1.8 28.8 %shard_map.64 = bf16[64,1024,128]{2,1,0:T(8,128)(2,1)} custom-call(s32[8]{0:T(128)S(1)} %bitcast.21, bf16[128,64,2048]{2,1,0:T(8,128)(2,1)} %bitcast.24), custom_call_target="tpu_custom_call" | custom-call | bytes 33554432 | tf_op jit(solution)/shard_map/pallas_call | solution.py:404
  30.7 190.1 %shard_map.65.refs_0_.refs_1_.refs_2_.refs_3_ = bf16[16,64,32,128]{3,2,1,0:T(8,128)(2,1)S(1)} custom-call(bf16[64,16,64,128]{3,2,1,0:T(8,128)(2,1)} %bitcast.22), custom_call_target="tpu_custom_call" | custom-call | bytes 268435456 | tf_op jit(solution)/shard_map/pallas_call | solution.py:498
  220.8 3.3 copy-done
  224.0 5.7 shard_map.66
  230.0 19.1 %shard_map.67 = (bf16[64,32,1024]{2,1,0:T(8,128)(2,1)S(1)}, bf16[16,2,4,32,1024]{4,3,2,1,0:T(8,128)(2,1)}) custom-call(s32[8]{0:T(128)S(1)} %get-tuple-element.40.ids_ref, bf16[16,64,32,128]{3,2,1,0:T(8,128)(2,1)} %copy-done, bf16[16,64,32,128]{3,2,1,0:T(8,128)(2,1)} %copy-done, bf16[16,64,32,128]{3,2,1,0:T(8,128)(2,1)} %copy-done, ...), custom_call_target="tpu_custom_call" | custom-call | flops 10737418240 | bytes 16777216 | tf_op jit(solution)/shard_map/pallas_call | solution.py:234
  249.1 2.0 copy-done.3
  251.1 18.2 %all-to-all-start = ((bf16[16,2,4,32,1024]{4,3,2,1,0:T(8,128)(2,1)}), bf16[16,2,4,32,1024]{4,3,2,1,0:T(8,128)(2,1)}, u32[]{:S(2)}, u32[]{:S(2)}) async-start(bf16[16,2,4,32,1024]{4,3,2,1,0:T(8,128)(2,1)} %get-tuple-element.23), calls=%async_computation | async-start | bytes 16777216 | tf_op jit(solution)/shard_map/all_to_all | solution.py:520
  269.3 236.0 %shard_map.68.refs_0_.refs_1_.refs_2_.refs_3_.refs_4_.refs_5_.refs_6_.refs_7_ = bf16[16,64,32,128]{3,2,1,0:T(8,128)(2,1)S(1)} custom-call(bf16[64,16,64,128]{3,2,1,0:T(8,128)(2,1)} %bitcast.23), custom_call_target="tpu_custom_call" | custom-call | bytes 268435456 | tf_op jit(solution)/shard_map/pallas_call | solution.py:498
  505.3 3.4 copy-done.1
  508.7 19.2 %shard_map.69 = (bf16[64,32,1024]{2,1,0:T(8,128)(2,1)S(1)}, bf16[16,2,4,32,1024]{4,3,2,1,0:T(8,128)(2,1)}) custom-call(s32[8]{0:T(128)S(1)} %get-tuple-element.40.ids_ref, bf16[16,64,32,128]{3,2,1,0:T(8,128)(2,1)} %copy-done.1, bf16[16,64,32,128]{3,2,1,0:T(8,128)(2,1)} %copy-done.1, bf16[16,64,32,128]{3,2,1,0:T(8,128)(2,1)} %copy-done.1, ...), custom_call_target="tpu_custom_call" | custom-call | flops 10737418240 | bytes 16777216 | tf_op jit(solution)/shard_map/pallas_call | solution.py:234
  527.9 2.1 copy-done.4
  529.9 126.6 %all_to_all.50.refs_1_.refs_3_ = bf16[16,2,4,32,1024]{4,3,2,1,0:T(8,128)(2,1)} all-to-all(bf16[16,2,4,32,1024]{4,3,2,1,0:T(8,128)(2,1)} %get-tuple-element.27), channel_id=1, replica_groups=mesh['core'=2,'half'=2,'inner'=8] {'core','inner'}, dimensions={0} | all-to-all | bytes 16777216 | tf_op jit(solution)/shard_map/all_to_all | solution.py:520
  656.6 7.9 shard_map.72
  664.5 2.0 copy-done.6
  666.5 4.7 all-to-all-start.3
  671.3 8.0 shard_map.70
  679.2 1.9 copy-done.5
  681.2 39.7 %all-to-all-done.3 = bf16[16,4,64,512]{3,2,1,0:T(8,128)(2,1)} async-done(((bf16[16,4,64,512]{3,2,1,0:T(8,128)(2,1)}), bf16[16,4,64,512]{3,2,1,0:T(8,128)(2,1)}, u32[]{:S(2)}, u32[]{:S(2)}) %all-to-all-start.3) | async-done | bytes 4194336 | tf_op jit(solution)/shard_map/all_to_all | solution.py:520
  720.9 11.0 all-to-all-start.2
  731.9 27.1 %shard_map.73 = (bf16[64,64,512]{2,1,0:T(8,128)(2,1)S(1)}, bf16[64,64,512]{2,1,0:T(8,128)(2,1)}, bf16[64,64,512]{2,1,0:T(8,128)(2,1)}, bf16[64,64,512]{2,1,0:T(8,128)(2,1)}) custom-call(s32[8]{0:T(128)S(1)} %get-tuple-element.40.ids_ref, bf16[16,64,32,128]{3,2,1,0:T(8,128)(2,1)} %copy-done, bf16[16,64,32,128]{3,2,1,0:T(8,128)(2,1)} %copy-done, ...), custom_call_target="tpu_custom_call" | custom-call | flops 12884901888 | bytes 33554432 | tf_op jit(solution)/shard_map/pallas_call | solution.py:208
  759.0 1.9 copy-done.8
  760.9 21.0 %all-to-all-done.2 = bf16[16,4,64,512]{3,2,1,0:T(8,128)(2,1)} async-done(((bf16[16,4,64,512]{3,2,1,0:T(8,128)(2,1)}), bf16[16,4,64,512]{3,2,1,0:T(8,128)(2,1)}, u32[]{:S(2)}, u32[]{:S(2)}) %all-to-all-start.2) | async-done | bytes 4194336 | tf_op jit(solution)/shard_map/all_to_all | solution.py:520
  781.9 60.0 %all_to_all.51.refs_1_ = bf16[16,4,64,512]{3,2,1,0:T(8,128)(2,1)} all-to-all(bf16[16,4,64,512]{3,2,1,0:T(8,128)(2,1)} %bitcast.29), channel_id=1, replica_groups=mesh['core'=2,'half'=2,'inner'=8] {'core','inner'}, dimensions={0} | all-to-all | bytes 8388608 | tf_op jit(solution)/shard_map/all_to_all | solution.py:520
  842.0 4.5 all-to-all-start.4
  846.5 27.1 %shard_map.71 = (bf16[64,64,512]{2,1,0:T(8,128)(2,1)S(1)}, bf16[64,64,512]{2,1,0:T(8,128)(2,1)}, bf16[64,64,512]{2,1,0:T(8,128)(2,1)}, bf16[64,64,512]{2,1,0:T(8,128)(2,1)}) custom-call(s32[8]{0:T(128)S(1)} %get-tuple-element.40.ids_ref, bf16[16,64,32,128]{3,2,1,0:T(8,128)(2,1)} %copy-done, bf16[16,64,32,128]{3,2,1,0:T(8,128)(2,1)} %copy-done, ...), custom_call_target="tpu_custom_call" | custom-call | flops 12884901888 | bytes 33554432 | tf_op jit(solution)/shard_map/pallas_call | solution.py:208
  873.7 2.0 copy-done.9
  875.7 20.5 %all-to-all-done.4.refs_0_ = bf16[16,4,64,512]{3,2,1,0:T(8,128)(2,1)} async-done(((bf16[16,4,64,512]{3,2,1,0:T(8,128)(2,1)}), bf16[16,4,64,512]{3,2,1,0:T(8,128)(2,1)}, u32[]{:S(2)}, u32[]{:S(2)}) %all-to-all-start.4) | async-done | bytes 4194336 | tf_op jit(solution)/shard_map/all_to_all | solution.py:520
  896.2 60.8 %all_to_all.52.refs_2_ = bf16[16,4,64,512]{3,2,1,0:T(8,128)(2,1)} all-to-all(bf16[16,4,64,512]{3,2,1,0:T(8,128)(2,1)} %bitcast.28), channel_id=1, replica_groups=mesh['core'=2,'half'=2,'inner'=8] {'core','inner'}, dimensions={0} | all-to-all | bytes 8388608 | tf_op jit(solution)/shard_map/all_to_all | solution.py:520
  957.0 7.3 shard_map.74
  964.2 53.1 %all_to_all.53 = bf16[16,4,64,512]{3,2,1,0:T(8,128)(2,1)} all-to-all(bf16[16,4,64,512]{3,2,1,0:T(8,128)(2,1)S(1)} %shard_map.74), channel_id=1, replica_groups=mesh['core'=2,'half'=2,'inner'=8] {'core','inner'}, dimensions={0} | all-to-all | bytes 8388608 | tf_op jit(solution)/shard_map/all_to_all | solution.py:520
  1017.3 52.1 %all_to_all.54.refs_0_ = bf16[16,4,64,512]{3,2,1,0:T(8,128)(2,1)S(1)} all-to-all(bf16[16,4,64,512]{3,2,1,0:T(8,128)(2,1)S(1)} %bitcast.27), channel_id=1, replica_groups=mesh['core'=2,'half'=2,'inner'=8] {'core','inner'}, dimensions={0} | all-to-all | bytes 8388608 | tf_op jit(solution)/shard_map/all_to_all | solution.py:520
  1069.4 7.0 shard_map.75
  1076.5 2.0 copy-done.7
  1078.5 4.5 all-to-all-start.9
  1083.0 12.5 shard_map.77
  1095.5 1.5 collective-permute-start.3
  1097.0 73.4 %all-to-all-done.9 = bf16[16,4,64,512]{3,2,1,0:T(8,128)(2,1)} async-done(((bf16[16,4,64,512]{3,2,1,0:T(8,128)(2,1)}), bf16[16,4,64,512]{3,2,1,0:T(8,128)(2,1)}, u32[]{:S(2)}, u32[]{:S(2)}) %all-to-all-start.9) | async-done | bytes 4194336 | tf_op jit(solution)/shard_map/all_to_all | solution.py:520
  1170.4 11.1 shard_map.76
  1181.5 1.3 collective-permute-start.1
  1182.8 54.2 %collective-permute-done.3 = bf16[64,64,512]{2,1,0:T(8,128)(2,1)} collective-permute-done((bf16[64,64,512]{2,1,0:T(8,128)(2,1)}, bf16[64,64,512]{2,1,0:T(8,128)(2,1)}, u32[]{:S(2)}, u32[]{:S(2)}) %collective-permute-start.3) | collective-permute-done | bytes 4194336 | tf_op jit(solution)/shard_map/ppermute | solution.py:526
  1237.1 7.4 maximum_convert_fusion.hidden_ref
  1244.5 3.3 collective-permute-start.4
  1247.8 34.1 %collective-permute-done.1 = bf16[64,64,512]{2,1,0:T(8,128)(2,1)S(1)} collective-permute-done((bf16[64,64,512]{2,1,0:T(8,128)(2,1)S(1)}, bf16[64,64,512]{2,1,0:T(8,128)(2,1)S(1)}, u32[]{:S(2)}, u32[]{:S(2)}) %collective-permute-start.1) | collective-permute-done | bytes 4194336 | tf_op jit(solution)/shard_map/ppermute | solution.py:526
  1281.9 3.6 maximum_convert_fusion.1.hidden_ref
  1285.5 3.3 collective-permute-start.2
  1288.9 10.9 shard_map.78.refs_0_
  1299.8 10.9 shard_map.79
  (31 shorter events, 0.8 us)
Async XLA Ops:
  0.0 229.7 %collective-permute-start = (s32[8]{0:T(128)}, s32[8]{0:T(128)S(1)}, u32[]{:S(2)}, u32[]{:S(2)}) collective-permute-start(s32[8]{0:T(128)} %bitcast.20), channel_id=1, source_target_pairs={{0,16},{16,0},{1,17},{17,1},{2,18},{18,2},{3,19},{19,3},{4,20},{20... | collective-permute-start | bytes 104 | tf_op jit(solution)/shard_map/ppermute | solution.py:542
  1.1 0.7 copy-start.13
  30.6 193.4 %copy-start.10 = (bf16[2,64,320]{2,1,0:T(8,128)(2,1)S(1)}, bf16[2,64,320]{2,1,0:T(8,128)(2,1)}, u32[]{:S(2)}) copy-start(bf16[2,64,320]{2,1,0:T(8,128)(2,1)} %proj_ref.1) | copy-start | bytes 245764
  30.6 193.4 %copy-start.11 = (bf16[2,64,64]{2,1,0:T(8,128)(2,1)S(1)}, bf16[2,64,64]{2,1,0:T(8,128)(2,1)}, u32[]{:S(2)}) copy-start(bf16[2,64,64]{2,1,0:T(8,128)(2,1)} %out_ref.1) | copy-start | bytes 49156
  30.7 193.4 %copy-start.12 = (bf16[64,128]{1,0:T(8,128)(2,1)S(1)}, bf16[64,128]{1,0:T(8,128)(2,1)}, u32[]{:S(2)}) copy-start(bf16[64,128]{1,0:T(8,128)(2,1)} %final_ref.1) | copy-start | bytes 49156
  30.7 199.1 %copy-start.14 = (s32[1,8]{1,0:T(1,128)S(1)}, s32[1,8]{1,0:T(1,128)}, u32[]{:S(2)}) copy-start(s32[1,8]{1,0:T(1,128)} %param.7) | copy-start | bytes 100
  220.8 3.3 copy-start
  249.1 2.0 copy-start.3
  251.1 278.8 %all-to-all-start = ((bf16[16,2,4,32,1024]{4,3,2,1,0:T(8,128)(2,1)}), bf16[16,2,4,32,1024]{4,3,2,1,0:T(8,128)(2,1)}, u32[]{:S(2)}, u32[]{:S(2)}) async-start(bf16[16,2,4,32,1024]{4,3,2,1,0:T(8,128)(2,1)} %get-tuple-element.23), calls=%async_computation | async-start | bytes 16777216 | tf_op jit(solution)/shard_map/all_to_all | solution.py:520
  505.3 3.4 copy-start.1
  527.9 2.1 copy-start.4
  664.5 2.0 copy-start.6
  666.5 54.4 %all-to-all-start.3 = ((bf16[16,4,64,512]{3,2,1,0:T(8,128)(2,1)}), bf16[16,4,64,512]{3,2,1,0:T(8,128)(2,1)}, u32[]{:S(2)}, u32[]{:S(2)}) async-start(bf16[16,4,64,512]{3,2,1,0:T(8,128)(2,1)} %copy-done.6), calls=%async_computation.3 | async-start | bytes 8388608 | tf_op jit(solution)/shard_map/all_to_all | solution.py:520
  679.2 2.0 copy-start.5
  720.9 61.0 %all-to-all-start.2 = ((bf16[16,4,64,512]{3,2,1,0:T(8,128)(2,1)}), bf16[16,4,64,512]{3,2,1,0:T(8,128)(2,1)}, u32[]{:S(2)}, u32[]{:S(2)}) async-start(bf16[16,4,64,512]{3,2,1,0:T(8,128)(2,1)} %copy-done.5), calls=%async_computation.2 | async-start | bytes 8388608 | tf_op jit(solution)/shard_map/all_to_all | solution.py:520
  759.0 1.9 copy-start.8
  842.0 54.2 %all-to-all-start.4 = ((bf16[16,4,64,512]{3,2,1,0:T(8,128)(2,1)}), bf16[16,4,64,512]{3,2,1,0:T(8,128)(2,1)}, u32[]{:S(2)}, u32[]{:S(2)}) async-start(bf16[16,4,64,512]{3,2,1,0:T(8,128)(2,1)} %bitcast.26), calls=%async_computation.4 | async-start | bytes 8388608 | tf_op jit(solution)/shard_map/all_to_all | solution.py:520
  873.7 2.0 copy-start.9
  896.2 60.8 %copy-start.2 = (bf16[16,4,64,512]{3,2,1,0:T(8,128)(2,1)S(1)}, bf16[16,4,64,512]{3,2,1,0:T(8,128)(2,1)}, u32[]{:S(2)}) copy-start(bf16[16,4,64,512]{3,2,1,0:T(8,128)(2,1)} %all_to_all.51.refs_1_) | copy-start | bytes 12582916
  964.2 53.1 %copy-start.15 = (bf16[64,64,512]{2,1,0:T(8,128)(2,1)S(1)}, bf16[64,64,512]{2,1,0:T(8,128)(2,1)}, u32[]{:S(2)}) copy-start(bf16[64,64,512]{2,1,0:T(8,128)(2,1)} %get-tuple-element.30) | copy-start | bytes 12582916
  1076.5 2.0 copy-start.7
  1078.5 91.9 %all-to-all-start.9 = ((bf16[16,4,64,512]{3,2,1,0:T(8,128)(2,1)}), bf16[16,4,64,512]{3,2,1,0:T(8,128)(2,1)}, u32[]{:S(2)}, u32[]{:S(2)}) async-start(bf16[16,4,64,512]{3,2,1,0:T(8,128)(2,1)} %copy-done.7), calls=%async_computation.9 | async-start | bytes 8388608 | tf_op jit(solution)/shard_map/all_to_all | solution.py:520
  1095.5 141.5 %collective-permute-start.3 = (bf16[64,64,512]{2,1,0:T(8,128)(2,1)}, bf16[64,64,512]{2,1,0:T(8,128)(2,1)}, u32[]{:S(2)}, u32[]{:S(2)}) collective-permute-start(bf16[64,64,512]{2,1,0:T(8,128)(2,1)} %shard_map.77), channel_id=1, source_target_pairs={{8,0},{16,24},{9,1},{17,25},{10,2},{18,26},{11,3},{19,27},{12,4},{... | collective-permute-start | bytes 12582920 | tf_op jit(solution)/shard_map/ppermute | solution.py:526
  1181.5 100.4 %collective-permute-start.1 = (bf16[64,64,512]{2,1,0:T(8,128)(2,1)S(1)}, bf16[64,64,512]{2,1,0:T(8,128)(2,1)S(1)}, u32[]{:S(2)}, u32[]{:S(2)}) collective-permute-start(bf16[64,64,512]{2,1,0:T(8,128)(2,1)S(1)} %shard_map.76), channel_id=1, source_target_pairs={{8,0},{16,24},{9,1},{17,25},{10,2},{18,26},{11,3},{19,27},{12,4},{... | collective-permute-start | bytes 12582920 | tf_op jit(solution)/shard_map/ppermute | solution.py:526
  1244.5 44.4 %collective-permute-start.4 = (bf16[64,64,512]{2,1,0:T(8,128)(2,1)}, bf16[64,64,512]{2,1,0:T(8,128)(2,1)}, u32[]{:S(2)}, u32[]{:S(2)}) collective-permute-start(bf16[64,64,512]{2,1,0:T(8,128)(2,1)} %maximum_convert_fusion.hidden_ref), channel_id=1, source_target_pairs={{0,16},{24,8},{1,17},{25,9},{2,18},{26,10},{3,19},{27,11},{4,20},{... | collective-permute-start | bytes 12582920 | tf_op jit(solution)/shard_map/ppermute | solution.py:526
  1285.5 14.2 %collective-permute-start.2 = (bf16[64,64,512]{2,1,0:T(8,128)(2,1)}, bf16[64,64,512]{2,1,0:T(8,128)(2,1)}, u32[]{:S(2)}, u32[]{:S(2)}) collective-permute-start(bf16[64,64,512]{2,1,0:T(8,128)(2,1)} %maximum_convert_fusion.1.hidden_ref), channel_id=1, source_target_pairs={{0,16},{24,8},{1,17},{25,9},{2,18},{26,10},{3,19},{27,11},{4,20},{... | collective-permute-start | bytes 12582920 | tf_op jit(solution)/shard_map/ppermute | solution.py:526

commit v6 on v5

--- a/solution.py
+++ b/solution.py
@@ -33,7 +33,7 @@
 SUB = 8
 PARTS = 2
 COLUMN_PARTS = 2
-LEFT_PARTS = 1
+LEFT_PARTS = (1, 2)
 
 
 def widened(weight, source):
@@ -53,13 +53,16 @@
 
 def widen_kernel(proj_ref, out_ref, final_ref, wide_ref, out_wide_ref, final_wide_ref):
     size = CH // PARTS
-    for layer in range(NLAYER):
+
+    @pl.loop(0, NLAYER)
+    def _(layer):
         for part in range(PARTS):
             rows = lax.broadcasted_iota(jnp.int32, (5 * size * SUB, 5 * CH), 0) // SUB
             source = rows // size * CH + part * size + rows % size
             wide_ref[layer, part] = widened(proj_ref[layer], source)
         rows = lax.broadcasted_iota(jnp.int32, (CH * SUB, CH), 0) // SUB
         out_wide_ref[layer] = widened(out_ref[layer], rows)
+
     columns = final_ref.shape[1]
     rows = lax.broadcasted_iota(jnp.int32, (columns * SUB, columns), 0) // SUB
     final_wide_ref[...] = widened(final_ref[...], rows)
@@ -277,8 +280,9 @@
     operands += [back, out_wide, wide, mask]
     kernel = functools.partial(middle_kernel, len(gots), per, count)
     flops = 2 * (wide.size + out_wide.size) // NLAYER * count * len(gots) * lanes
-    left = jax.ShapeDtypeStruct((*shape.shape[:2], lanes // LEFT_PARTS), back.dtype)
-    return stage(kernel, specs, [shape] * 3 + [left] * LEFT_PARTS, ids, operands, flops)
+    pieces = LEFT_PARTS[number]
+    left = jax.ShapeDtypeStruct((*shape.shape[:2], lanes // pieces), back.dtype)
+    return stage(kernel, specs, [shape] * 3 + [left] * pieces, ids, operands, flops)
 
 
 def last_stage(layer, piece, pair, back, gate, out_wide):
@@ -294,10 +298,10 @@
     )(pair, back, gate, out_wide)
 
 
-def end_stage(home, number, count, hidden, shared, wide, earlier):
+def end_stage(home, start, total, hidden, shared, wide, earlier):
     width, lanes = hidden.shape[1:]
     columns = wide.shape[0] // SUB
-    out = jax.ShapeDtypeStruct((columns, width, lanes * count), hidden.dtype)
+    out = jax.ShapeDtypeStruct((columns, width, total), hidden.dtype)
     specs = [by_columns(hidden.shape)] * 2 + [whole(wide.shape)]
     operands = [hidden, shared, wide]
     if earlier is not None:
@@ -309,7 +313,7 @@
             num_scalar_prefetch=1,
             grid=(width // SUB,),
             in_specs=specs,
-            out_specs=pl.BlockSpec((columns, SUB, lanes), lambda w, _: (0, w, number)),
+            out_specs=pl.BlockSpec((columns, SUB, lanes), lambda w, _: (0, w, start // lanes)),
         ),
         out_shape=out,
         input_output_aliases={} if earlier is None else {4: 0},
@@ -572,11 +576,11 @@
     back = None
     for pair, _, gate, *lefts in following:
         for piece, left in enumerate(lefts):
-            left = left.reshape(row_count, per_group, col_width, chunk // LEFT_PARTS)
+            left = left.reshape(row_count, per_group, col_width, left.shape[2])
             left = exchange(left if back is None else after(left, back))
             products = row_products(left, rights)
             back = exchange(products)
-            merged = back.reshape(CH, col_width, chunk // LEFT_PARTS)
+            merged = back.reshape(CH, col_width, back.shape[3])
             ready.append(last_stage(NLAYER - 1, piece, pair, merged, gate, outs))
             arrived.append(moved(ready[-1], [((0, 1), (0, 0)), ((1, 0), (1, 1))]))
     hiddens, shareds = [], []
@@ -585,9 +589,10 @@
         hiddens.append(jnp.maximum(summed / halves, 0.0).astype(jnp.bfloat16))
         shareds.append(moved(hiddens[-1], [((0, 0), (1, 0)), ((1, 1), (0, 1))]))
     home = (core == half).astype(jnp.int32)[None]
-    result = None
-    for number, (hidden, shared) in enumerate(zip(hiddens, shareds)):
-        result = end_stage(home, number, len(hiddens), hidden, shared, final_wide, result)
+    result, start = None, 0
+    for hidden, shared in zip(hiddens, shareds):
+        result = end_stage(home, start, CROP, hidden, shared, final_wide, result)
+        start += hidden.shape[2]
     return result
 
 

time: 1310 us -> 1320 us (level)
  waiting for transfers between devices: 243 us -> 217 us
    all_to_all x5 -> x6, waiting for transfers between devices: 155 us -> 105 us  [exchange(): return lax.all_to_all(value, GROUP, split_axis=0, concat_axis=0, tiled=True)]
    ppermute x4 -> x6, waiting for transfers between devices: 88.4 us -> 112 us  [moved(): return lax.ppermute(value, ('core', 'half'), steps)]
    all_to_all x5 -> x6, starting transfers between devices: 43 us -> 53.7 us  [exchange(): return lax.all_to_all(value, GROUP, split_axis=0, concat_axis=0, tiled=True)]
    pallas_call x2 -> x3, Pallas kernels: 23.6 us -> 29 us  [last_stage(): pl.pallas_call(last_kernel, grid=(back.shape[1] // SUB,), in_specs=[block...]
    pallas_call x2 -> x3, Pallas kernels: 21.8 us -> 26.7 us  [end_stage(): pl.pallas_call(end_kernel, grid_spec=pltpu.PrefetchScalarGridSpec(num_sca...]
    pallas_call x4 -> x5, Pallas kernels: 30.2 us -> 33.5 us  [product_call(): pl.pallas_call(functools.partial(product_kernel, axis, count), grid=(chan...]
    all_to_all x5 -> x6, blocking collectives: 353 us -> 351 us  [exchange(): return lax.all_to_all(value, GROUP, split_axis=0, concat_axis=0, tiled=True)]
  transfers between devices with their start and end apart: 10 -> 13, of which waited for: 6 -> 7; matrix products, arithmetic and copies ran while one was open for 1% -> 1% of each run, Pallas kernels for 44% -> 45%
where the time goes in v6:
time: 1320 us
  Pallas kernels  642 us (49%)
  blocking collectives  351 us (27%)
  waiting for transfers between devices  217 us (16%)
  starting transfers between devices  65.6 us (5%)
  local copies, waits for them, and re-layouts  25.1 us (2%)
  other arithmetic  14.4 us (1%)
    pallas_call x2, Pallas kernels, spread(): pl.pallas_call(functools.partial(spread_kernel, part), in_specs=[pl.Block...  426 us
    all_to_all x6, blocking collectives, exchange(): return lax.all_to_all(value, GROUP, split_axis=0, concat_axis=0, tiled=True)  351 us
    ppermute x6, waiting for transfers between devices, moved(): return lax.ppermute(value, ('core', 'half'), steps)  112 us
    all_to_all x6, waiting for transfers between devices, exchange(): return lax.all_to_all(value, GROUP, split_axis=0, concat_axis=0, tiled=True)  105 us
    pallas_call x2, Pallas kernels, stage(): pl.pallas_call(kernel, grid_spec=pltpu.PrefetchScalarGridSpec(num_scalar_...  54.1 us
    all_to_all x6, starting transfers between devices, exchange(): return lax.all_to_all(value, GROUP, split_axis=0, concat_axis=0, tiled=True)  53.7 us
    pallas_call x2, Pallas kernels, first_stage(): pl.pallas_call(functools.partial(first_kernel, per), grid_spec=pltpu.Pref...  38.3 us
    pallas_call x5, Pallas kernels, product_call(): pl.pallas_call(functools.partial(product_kernel, axis, count), grid=(chan...  33.5 us
  transfers between devices with their start and end apart: 13, of which 7 were waited for; matrix products, arithmetic and copies ran while one was open for 1% of the time, Pallas kernels for 45%

profile of v6, /device:TPU:0, one launch (start us, length us, event | category | flops | bytes accessed | tf_op | source)
XLA Modules:
  0.0 1317.0 jit_solution(1561918629053571566)
XLA Ops:
  1.8 28.8 %shard_map.64 = bf16[64,1024,128]{2,1,0:T(8,128)(2,1)} custom-call(s32[8]{0:T(128)S(1)} %bitcast.26, bf16[128,64,2048]{2,1,0:T(8,128)(2,1)} %bitcast.29), custom_call_target="tpu_custom_call" | custom-call | bytes 33554432 | tf_op jit(solution)/shard_map/pallas_call | solution.py:408
  30.7 190.1 %shard_map.65.refs_0_.refs_1_.refs_2_.refs_3_ = bf16[16,64,32,128]{3,2,1,0:T(8,128)(2,1)S(1)} custom-call(bf16[64,16,64,128]{3,2,1,0:T(8,128)(2,1)} %bitcast.27), custom_call_target="tpu_custom_call" | custom-call | bytes 268435456 | tf_op jit(solution)/shard_map/pallas_call | solution.py:502
  220.8 3.3 copy-done
  224.0 5.6 shard_map.66
  229.9 19.1 %shard_map.67 = (bf16[64,32,1024]{2,1,0:T(8,128)(2,1)S(1)}, bf16[16,2,4,32,1024]{4,3,2,1,0:T(8,128)(2,1)}) custom-call(s32[8]{0:T(128)S(1)} %get-tuple-element.44.ids_ref, bf16[16,64,32,128]{3,2,1,0:T(8,128)(2,1)} %copy-done, bf16[16,64,32,128]{3,2,1,0:T(8,128)(2,1)} %copy-done, bf16[16,64,32,128]{3,2,1,0:T(8,128)(2,1)} %copy-done, ...), custom_call_target="tpu_custom_call" | custom-call | flops 10737418240 | bytes 16777216 | tf_op jit(solution)/shard_map/pallas_call | solution.py:237
  250.9 18.2 %all-to-all-start = ((bf16[16,2,4,32,1024]{4,3,2,1,0:T(8,128)(2,1)}), bf16[16,2,4,32,1024]{4,3,2,1,0:T(8,128)(2,1)}, u32[]{:S(2)}, u32[]{:S(2)}) async-start(bf16[16,2,4,32,1024]{4,3,2,1,0:T(8,128)(2,1)} %get-tuple-element.25), calls=%async_computation | async-start | bytes 16777216 | tf_op jit(solution)/shard_map/all_to_all | solution.py:524
  269.2 236.0 %shard_map.68.refs_0_.refs_1_.refs_2_.refs_3_.refs_4_.refs_5_.refs_6_.refs_7_ = bf16[16,64,32,128]{3,2,1,0:T(8,128)(2,1)S(1)} custom-call(bf16[64,16,64,128]{3,2,1,0:T(8,128)(2,1)} %bitcast.28), custom_call_target="tpu_custom_call" | custom-call | bytes 268435456 | tf_op jit(solution)/shard_map/pallas_call | solution.py:502
  505.1 3.4 copy-done.1
  508.5 19.2 %shard_map.69 = (bf16[64,32,1024]{2,1,0:T(8,128)(2,1)S(1)}, bf16[16,2,4,32,1024]{4,3,2,1,0:T(8,128)(2,1)}) custom-call(s32[8]{0:T(128)S(1)} %get-tuple-element.44.ids_ref, bf16[16,64,32,128]{3,2,1,0:T(8,128)(2,1)} %copy-done.1, bf16[16,64,32,128]{3,2,1,0:T(8,128)(2,1)} %copy-done.1, bf16[16,64,32,128]{3,2,1,0:T(8,128)(2,1)} %copy-done.1, ...), custom_call_target="tpu_custom_call" | custom-call | flops 10737418240 | bytes 16777216 | tf_op jit(solution)/shard_map/pallas_call | solution.py:237
  527.7 2.1 copy-done.5
  529.8 126.6 %all_to_all.60.refs_1_.refs_3_ = bf16[16,2,4,32,1024]{4,3,2,1,0:T(8,128)(2,1)} all-to-all(bf16[16,2,4,32,1024]{4,3,2,1,0:T(8,128)(2,1)} %get-tuple-element.29), channel_id=1, replica_groups=mesh['core'=2,'half'=2,'inner'=8] {'core','inner'}, dimensions={0} | all-to-all | bytes 16777216 | tf_op jit(solution)/shard_map/all_to_all | solution.py:524
  656.4 7.9 shard_map.70
  666.4 4.6 all-to-all-start.2
  671.0 8.0 shard_map.72
  680.9 39.7 %all-to-all-done.2 = bf16[16,4,64,512]{3,2,1,0:T(8,128)(2,1)} async-done(((bf16[16,4,64,512]{3,2,1,0:T(8,128)(2,1)}), bf16[16,4,64,512]{3,2,1,0:T(8,128)(2,1)}, u32[]{:S(2)}, u32[]{:S(2)}) %all-to-all-start.2) | async-done | bytes 4194336 | tf_op jit(solution)/shard_map/all_to_all | solution.py:524
  720.6 11.0 all-to-all-start.3
  731.6 27.0 %shard_map.71 = (bf16[64,64,512]{2,1,0:T(8,128)(2,1)}, bf16[64,64,512]{2,1,0:T(8,128)(2,1)}, bf16[64,64,512]{2,1,0:T(8,128)(2,1)}, bf16[64,64,256]{2,1,0:T(8,128)(2,1)S(1)}, bf16[64,64,256]{2,1,0:T(8,128)(2,1)S(1)}) custom-call(s32[8]{0:T(128)S(1)} %get-tuple-element.44.ids_ref, bf16[16,64,32,128]{3,2,1,0:T(8,128)(2,1)} %copy-done, ...), custom_call_target="tpu_custom_call" | custom-call | flops 12884901888 | bytes 33554432 | tf_op jit(solution)/shard_map/pallas_call | solution.py:211
  761.3 20.7 %all-to-all-done.3 = bf16[16,4,64,512]{3,2,1,0:T(8,128)(2,1)} async-done(((bf16[16,4,64,512]{3,2,1,0:T(8,128)(2,1)}), bf16[16,4,64,512]{3,2,1,0:T(8,128)(2,1)}, u32[]{:S(2)}, u32[]{:S(2)}) %all-to-all-start.3) | async-done | bytes 4194336 | tf_op jit(solution)/shard_map/all_to_all | solution.py:524
  781.9 10.3 all-to-all-start.6
  792.2 27.1 %shard_map.73 = (bf16[64,64,512]{2,1,0:T(8,128)(2,1)S(1)}, bf16[64,64,512]{2,1,0:T(8,128)(2,1)}, bf16[64,64,512]{2,1,0:T(8,128)(2,1)}, bf16[64,64,512]{2,1,0:T(8,128)(2,1)}) custom-call(s32[8]{0:T(128)S(1)} %get-tuple-element.44.ids_ref, bf16[16,64,32,128]{3,2,1,0:T(8,128)(2,1)} %copy-done, bf16[16,64,32,128]{3,2,1,0:T(8,128)(2,1)} %copy-done, ...), custom_call_target="tpu_custom_call" | custom-call | flops 12884901888 | bytes 33554432 | tf_op jit(solution)/shard_map/pallas_call | solution.py:211
  819.3 2.0 copy-done.10
  821.3 21.0 %all-to-all-done.6.refs_2_ = bf16[16,4,64,512]{3,2,1,0:T(8,128)(2,1)} async-done(((bf16[16,4,64,512]{3,2,1,0:T(8,128)(2,1)}), bf16[16,4,64,512]{3,2,1,0:T(8,128)(2,1)}, u32[]{:S(2)}, u32[]{:S(2)}) %all-to-all-start.6) | async-done | bytes 4194336 | tf_op jit(solution)/shard_map/all_to_all | solution.py:524
  842.3 60.1 %all_to_all.61.refs_1_ = bf16[16,4,64,512]{3,2,1,0:T(8,128)(2,1)S(1)} all-to-all(bf16[16,4,64,512]{3,2,1,0:T(8,128)(2,1)} %bitcast.33), channel_id=1, replica_groups=mesh['core'=2,'half'=2,'inner'=8] {'core','inner'}, dimensions={0} | all-to-all | bytes 8388608 | tf_op jit(solution)/shard_map/all_to_all | solution.py:524
  902.4 52.1 %all_to_all.62.refs_0_ = bf16[16,4,64,512]{3,2,1,0:T(8,128)(2,1)S(1)} all-to-all(bf16[16,4,64,512]{3,2,1,0:T(8,128)(2,1)S(1)} %bitcast.32), channel_id=1, replica_groups=mesh['core'=2,'half'=2,'inner'=8] {'core','inner'}, dimensions={0} | all-to-all | bytes 8388608 | tf_op jit(solution)/shard_map/all_to_all | solution.py:524
  954.5 7.0 shard_map.74
  961.6 53.0 %all_to_all.63 = bf16[16,4,64,512]{3,2,1,0:T(8,128)(2,1)} all-to-all(bf16[16,4,64,512]{3,2,1,0:T(8,128)(2,1)S(1)} %shard_map.74), channel_id=1, replica_groups=mesh['core'=2,'half'=2,'inner'=8] {'core','inner'}, dimensions={0} | all-to-all | bytes 8388608 | tf_op jit(solution)/shard_map/all_to_all | solution.py:524
  1014.5 29.4 %all_to_all.64.refs_0_ = bf16[16,4,64,256]{3,2,1,0:T(8,128)(2,1)S(1)} all-to-all(bf16[16,4,64,256]{3,2,1,0:T(8,128)(2,1)S(1)} %bitcast.24), channel_id=1, replica_groups=mesh['core'=2,'half'=2,'inner'=8] {'core','inner'}, dimensions={0} | all-to-all | bytes 4194304 | tf_op jit(solution)/shard_map/all_to_all | solution.py:524
  1044.0 5.2 shard_map.75
  1049.2 30.1 %all_to_all.65 = bf16[16,4,64,256]{3,2,1,0:T(8,128)(2,1)} all-to-all(bf16[16,4,64,256]{3,2,1,0:T(8,128)(2,1)S(1)} %shard_map.75), channel_id=1, replica_groups=mesh['core'=2,'half'=2,'inner'=8] {'core','inner'}, dimensions={0} | all-to-all | bytes 4194304 | tf_op jit(solution)/shard_map/all_to_all | solution.py:524
  1079.3 4.4 all-to-all-start.10
  1083.7 12.4 shard_map.79
  1097.5 23.9 %all-to-all-done.10.refs_0_ = bf16[16,4,64,256]{3,2,1,0:T(8,128)(2,1)} async-done(((bf16[16,4,64,256]{3,2,1,0:T(8,128)(2,1)}), bf16[16,4,64,256]{3,2,1,0:T(8,128)(2,1)}, u32[]{:S(2)}, u32[]{:S(2)}) %all-to-all-start.10) | async-done | bytes 2097184 | tf_op jit(solution)/shard_map/all_to_all | solution.py:524
  1121.3 2.2 copy-done.3
  1123.5 5.4 shard_map.76
  1130.2 5.2 all-to-all-start.11
  1137.0 8.6 shard_map.78
  1147.1 68.2 %collective-permute-done.5 = bf16[64,64,512]{2,1,0:T(8,128)(2,1)} collective-permute-done((bf16[64,64,512]{2,1,0:T(8,128)(2,1)}, bf16[64,64,512]{2,1,0:T(8,128)(2,1)}, u32[]{:S(2)}, u32[]{:S(2)}) %collective-permute-start.5) | collective-permute-done | bytes 4194336 | tf_op jit(solution)/shard_map/ppermute | solution.py:530
  1215.3 7.4 maximum_convert_fusion.hidden_ref
  1222.7 3.3 collective-permute-start.6
  1226.0 8.0 shard_map.77
  1235.3 2.5 collective-permute-done.3
  1237.8 4.6 maximum_convert_fusion.1.hidden_ref
  1243.8 41.5 %collective-permute-done.1 = bf16[64,64,256]{2,1,0:T(8,128)(2,1)S(1)} collective-permute-done((bf16[64,64,256]{2,1,0:T(8,128)(2,1)S(1)}, bf16[64,64,256]{2,1,0:T(8,128)(2,1)S(1)}, u32[]{:S(2)}, u32[]{:S(2)}) %collective-permute-start.1) | collective-permute-done | bytes 2097184 | tf_op jit(solution)/shard_map/ppermute | solution.py:530
  1285.3 2.3 maximum_convert_fusion.2.hidden_ref
  1287.6 2.7 collective-permute-start.2
  1290.3 10.9 shard_map.80.refs_0_
  1301.2 7.7 shard_map.81.refs_0_
  1308.9 8.1 shard_map.82
  (50 shorter events, 18.4 us)
Async XLA Ops:
  0.0 229.6 %collective-permute-start = (s32[8]{0:T(128)}, s32[8]{0:T(128)S(1)}, u32[]{:S(2)}, u32[]{:S(2)}) collective-permute-start(s32[8]{0:T(128)} %bitcast.25), channel_id=1, source_target_pairs={{0,16},{16,0},{1,17},{17,1},{2,18},{18,2},{3,19},{19,3},{4,20},{20... | collective-permute-start | bytes 104 | tf_op jit(solution)/shard_map/ppermute | solution.py:546
  1.1 0.7 copy-start.17
  30.6 193.4 %copy-start.14 = (bf16[2,64,320]{2,1,0:T(8,128)(2,1)S(1)}, bf16[2,64,320]{2,1,0:T(8,128)(2,1)}, u32[]{:S(2)}) copy-start(bf16[2,64,320]{2,1,0:T(8,128)(2,1)} %proj_ref.1) | copy-start | bytes 245764
  30.6 193.4 %copy-start.15 = (bf16[2,64,64]{2,1,0:T(8,128)(2,1)S(1)}, bf16[2,64,64]{2,1,0:T(8,128)(2,1)}, u32[]{:S(2)}) copy-start(bf16[2,64,64]{2,1,0:T(8,128)(2,1)} %out_ref.1) | copy-start | bytes 49156
  30.7 193.4 %copy-start.16 = (bf16[64,128]{1,0:T(8,128)(2,1)S(1)}, bf16[64,128]{1,0:T(8,128)(2,1)}, u32[]{:S(2)}) copy-start(bf16[64,128]{1,0:T(8,128)(2,1)} %final_ref.1) | copy-start | bytes 49156
  30.7 199.0 %copy-start.18 = (s32[1,8]{1,0:T(1,128)S(1)}, s32[1,8]{1,0:T(1,128)}, u32[]{:S(2)}) copy-start(s32[1,8]{1,0:T(1,128)} %param.7) | copy-start | bytes 100
  220.8 3.3 copy-start
  249.0 2.0 copy-start.4
  250.9 278.9 %all-to-all-start = ((bf16[16,2,4,32,1024]{4,3,2,1,0:T(8,128)(2,1)}), bf16[16,2,4,32,1024]{4,3,2,1,0:T(8,128)(2,1)}, u32[]{:S(2)}, u32[]{:S(2)}) async-start(bf16[16,2,4,32,1024]{4,3,2,1,0:T(8,128)(2,1)} %get-tuple-element.25), calls=%async_computation | async-start | bytes 16777216 | tf_op jit(solution)/shard_map/all_to_all | solution.py:524
  505.1 3.4 copy-start.1
  527.7 2.1 copy-start.5
  664.4 2.0 copy-start.7
  666.4 54.2 %all-to-all-start.2 = ((bf16[16,4,64,512]{3,2,1,0:T(8,128)(2,1)}), bf16[16,4,64,512]{3,2,1,0:T(8,128)(2,1)}, u32[]{:S(2)}, u32[]{:S(2)}) async-start(bf16[16,4,64,512]{3,2,1,0:T(8,128)(2,1)} %copy-done.7), calls=%async_computation.2 | async-start | bytes 8388608 | tf_op jit(solution)/shard_map/all_to_all | solution.py:524
  678.9 2.0 copy-start.6
  720.6 61.3 %all-to-all-start.3 = ((bf16[16,4,64,512]{3,2,1,0:T(8,128)(2,1)}), bf16[16,4,64,512]{3,2,1,0:T(8,128)(2,1)}, u32[]{:S(2)}, u32[]{:S(2)}) async-start(bf16[16,4,64,512]{3,2,1,0:T(8,128)(2,1)} %copy-done.6), calls=%async_computation.3 | async-start | bytes 8388608 | tf_op jit(solution)/shard_map/all_to_all | solution.py:524
  758.6 1.3 copy-start.11
  759.9 1.3 copy-start.12
  781.9 60.3 %all-to-all-start.6 = ((bf16[16,4,64,512]{3,2,1,0:T(8,128)(2,1)}), bf16[16,4,64,512]{3,2,1,0:T(8,128)(2,1)}, u32[]{:S(2)}, u32[]{:S(2)}) async-start(bf16[16,4,64,512]{3,2,1,0:T(8,128)(2,1)} %bitcast.31), calls=%async_computation.6 | async-start | bytes 8388608 | tf_op jit(solution)/shard_map/all_to_all | solution.py:524
  819.3 2.0 copy-start.10
  842.3 60.2 %copy-start.19 = (bf16[64,64,512]{2,1,0:T(8,128)(2,1)S(1)}, bf16[64,64,512]{2,1,0:T(8,128)(2,1)}, u32[]{:S(2)}) copy-start(bf16[64,64,512]{2,1,0:T(8,128)(2,1)} %get-tuple-element.34) | copy-start | bytes 12582916
  902.4 141.5 %copy-start.2 = (bf16[16,4,64,512]{3,2,1,0:T(8,128)(2,1)}, bf16[16,4,64,512]{3,2,1,0:T(8,128)(2,1)S(1)}, u32[]{:S(2)}) copy-start(bf16[16,4,64,512]{3,2,1,0:T(8,128)(2,1)S(1)} %all_to_all.61.refs_1_) | copy-start | bytes 12582916
  961.6 53.0 %copy-start.13 = (bf16[64,64,256]{2,1,0:T(8,128)(2,1)S(1)}, bf16[64,64,256]{2,1,0:T(8,128)(2,1)}, u32[]{:S(2)}) copy-start(bf16[64,64,256]{2,1,0:T(8,128)(2,1)} %copy-done.12) | copy-start | bytes 6291460
  1079.3 42.0 %all-to-all-start.10 = ((bf16[16,4,64,256]{3,2,1,0:T(8,128)(2,1)}), bf16[16,4,64,256]{3,2,1,0:T(8,128)(2,1)}, u32[]{:S(2)}, u32[]{:S(2)}) async-start(bf16[16,4,64,256]{3,2,1,0:T(8,128)(2,1)} %bitcast.23), calls=%async_computation.10 | async-start | bytes 4194304 | tf_op jit(solution)/shard_map/all_to_all | solution.py:524
  1096.2 119.1 %collective-permute-start.5 = (bf16[64,64,512]{2,1,0:T(8,128)(2,1)}, bf16[64,64,512]{2,1,0:T(8,128)(2,1)}, u32[]{:S(2)}, u32[]{:S(2)}) collective-permute-start(bf16[64,64,512]{2,1,0:T(8,128)(2,1)} %shard_map.79), channel_id=1, source_target_pairs={{8,0},{16,24},{9,1},{17,25},{10,2},{18,26},{11,3},{19,27},{12,4},{... | collective-permute-start | bytes 12582920 | tf_op jit(solution)/shard_map/ppermute | solution.py:530
  1121.3 2.2 copy-start.3
  1128.9 1.3 copy-start.9
  1130.2 95.8 %all-to-all-start.11 = ((bf16[16,4,64,256]{3,2,1,0:T(8,128)(2,1)}), bf16[16,4,64,256]{3,2,1,0:T(8,128)(2,1)}, u32[]{:S(2)}, u32[]{:S(2)}) async-start(bf16[16,4,64,256]{3,2,1,0:T(8,128)(2,1)} %copy-done.9), calls=%async_computation.11 | async-start | bytes 4194304 | tf_op jit(solution)/shard_map/all_to_all | solution.py:524
  1135.4 1.6 copy-start.8
  1145.5 92.2 %collective-permute-start.3 = (bf16[64,64,256]{2,1,0:T(8,128)(2,1)}, bf16[64,64,256]{2,1,0:T(8,128)(2,1)}, u32[]{:S(2)}, u32[]{:S(2)}) collective-permute-start(bf16[64,64,256]{2,1,0:T(8,128)(2,1)} %shard_map.78), channel_id=1, source_target_pairs={{8,0},{16,24},{9,1},{17,25},{10,2},{18,26},{11,3},{19,27},{12,4},{... | collective-permute-start | bytes 6291464 | tf_op jit(solution)/shard_map/ppermute | solution.py:530
  1222.7 67.6 %collective-permute-start.6 = (bf16[64,64,512]{2,1,0:T(8,128)(2,1)}, bf16[64,64,512]{2,1,0:T(8,128)(2,1)}, u32[]{:S(2)}, u32[]{:S(2)}) collective-permute-start(bf16[64,64,512]{2,1,0:T(8,128)(2,1)} %maximum_convert_fusion.hidden_ref), channel_id=1, source_target_pairs={{0,16},{24,8},{1,17},{25,9},{2,18},{26,10},{3,19},{27,11},{4,20},{... | collective-permute-start | bytes 12582920 | tf_op jit(solution)/shard_map/ppermute | solution.py:530
  1234.0 51.3 %collective-permute-start.1 = (bf16[64,64,256]{2,1,0:T(8,128)(2,1)S(1)}, bf16[64,64,256]{2,1,0:T(8,128)(2,1)S(1)}, u32[]{:S(2)}, u32[]{:S(2)}) collective-permute-start(bf16[64,64,256]{2,1,0:T(8,128)(2,1)S(1)} %shard_map.77), channel_id=1, source_target_pairs={{8,0},{16,24},{9,1},{17,25},{10,2},{18,26},{11,3},{19,27},{12,4},{... | collective-permute-start | bytes 6291464 | tf_op jit(solution)/shard_map/ppermute | solution.py:530
  1242.3 58.8 %collective-permute-start.4 = (bf16[64,64,256]{2,1,0:T(8,128)(2,1)}, bf16[64,64,256]{2,1,0:T(8,128)(2,1)S(1)}, u32[]{:S(2)}, u32[]{:S(2)}) collective-permute-start(bf16[64,64,256]{2,1,0:T(8,128)(2,1)} %maximum_convert_fusion.1.hidden_ref), channel_id=1, source_target_pairs={{0,16},{24,8},{1,17},{25,9},{2,18},{26,10},{3,19},{27,11},{4,20},{... | collective-permute-start | bytes 6291464 | tf_op jit(solution)/shard_map/ppermute | solution.py:530
  1287.6 21.3 %collective-permute-start.2 = (bf16[64,64,256]{2,1,0:T(8,128)(2,1)}, bf16[64,64,256]{2,1,0:T(8,128)(2,1)}, u32[]{:S(2)}, u32[]{:S(2)}) collective-permute-start(bf16[64,64,256]{2,1,0:T(8,128)(2,1)} %maximum_convert_fusion.2.hidden_ref), channel_id=1, source_target_pairs={{0,16},{24,8},{1,17},{25,9},{2,18},{26,10},{3,19},{27,11},{4,20},{... | collective-permute-start | bytes 6291464 | tf_op jit(solution)/shard_map/ppermute | solution.py:530
